TPU v7x, 32 devices: a whole 2x2x4 slice. The times are simulated.
32 devices in a mesh: groups: 2 (over y), img: 4 (over z), pair: 2 (over x), sub: 2 (over core).
Axes of the slice: x: 2, y: 2, z: 4, core: 2. Of those that a mesh axis runs over, the one named last changes fastest.
Arguments:
- descriptors: bfloat16 [16, 1024, 256], P(('groups', 'img', 'pair')), parts along dimension 0
- links: int32 [16, 3], P('groups'), parts along dimension 0, may hold values 0 or 1
- qk_weight: bfloat16 [256, 256], P(None, 'sub'), may hold values from -0.375 to 0.375
- value_weight: bfloat16 [256, 256], P(None, 'sub'), may hold values from -0.375 to 0.375
- out_weight: bfloat16 [256, 256], replicated, may hold values from -0.375 to 0.375
- mlp_in: bfloat16 [512, 512], replicated, may hold values from -0.25 to 0.25
- mlp_in_bias: float32 [512], replicated, may hold values from -4 to 4
- norm_gain: float32 [512], replicated, may hold values from 0.1 to 1.9
- norm_bias: float32 [512], replicated, may hold values from -3 to 3
- mlp_out: bfloat16 [512, 256], replicated, may hold values from -0.25 to 0.25
- mlp_out_bias: float32 [256], replicated, may hold values from -3 to 3
Outputs:
- updated: bfloat16 [16, 1024, 256], P(('groups', 'img', 'pair'), 'sub'), parts along dimension 0
There are 2 independent parts, one for each index of `groups`. A program takes and returns all parts, laid end to end along the dimension named above; an argument that names none is the same for every part. Nothing has to cross between parts.
All inputs are finite; a program needn't handle non-finite values.
Results may differ from a plain program's by a relative error of at most 0.0045.
Values may be sent and summed in bfloat16 or wider, within the bound.
No kernel may reach another device: no remote copies, remote signals or barrier semaphores. Data moves between devices by JAX's collectives and lax.ppermute only.
A program may use at most 64 MiB of HBM per device.

v0:
```python
import math

import jax
import jax.numpy as jnp
from jax import lax
from jax.sharding import PartitionSpec as P

D = 256
HEADS = 4
SPAN = 3


def passed_along(value, axis, by):
    length = lax.axis_size(axis)
    pairs = [(i, i + by) for i in range(length) if 0 <= i + by < length]
    return lax.ppermute(value, axis, pairs)


def link_value(links, lower_image, step_size, image_count):
    inside = jnp.logical_and(lower_image >= 0, lower_image + step_size < image_count)
    clipped = jnp.clip(lower_image, 0, image_count - 1)
    entry = lax.dynamic_slice(links, (clipped, jnp.int32(step_size - 1)), (1, 1))[0, 0]
    return jnp.where(inside, entry, 0).astype(jnp.float32)


def fetch_partner(offset, packed, local_width):
    partner = passed_along(packed, ("img", "pair"), -offset)
    return (partner[:, :local_width], partner[:, local_width:])


def tile_messages(own_keys, partner_keys, partner_values):
    head_width = D // HEADS
    score_scale = 1.0 / math.sqrt(head_width)
    heads_local = own_keys.shape[1] // head_width
    to_own = []
    for head_id in range(heads_local):
        lo_col = head_id * head_width
        query_part = own_keys[:, lo_col : lo_col + head_width]
        key_part = partner_keys[:, lo_col : lo_col + head_width]
        scores = (
            jnp.einsum("qd,kd->qk", query_part, key_part, preferred_element_type=jnp.float32)
            * score_scale
        )
        row_weights = jax.nn.softmax(scores, axis=1).astype(jnp.bfloat16)
        to_own.append(
            jnp.dot(
                row_weights,
                partner_values[:, lo_col : lo_col + head_width],
                preferred_element_type=jnp.float32,
            ).astype(jnp.bfloat16)
        )
    own_result = jnp.concatenate(to_own, axis=1)
    return (own_result, own_result)


def on_device(
    descriptors,
    links,
    qk_weight,
    value_weight,
    out_weight,
    mlp_in,
    mlp_in_bias,
    norm_gain,
    norm_bias,
    mlp_out,
    mlp_out_bias,
):
    own_rows = descriptors[0]
    key_rows = jnp.dot(own_rows, qk_weight, preferred_element_type=jnp.float32).astype(jnp.bfloat16)
    value_rows = jnp.dot(own_rows, value_weight, preferred_element_type=jnp.float32).astype(
        jnp.bfloat16
    )
    local_width = key_rows.shape[1]
    packed = jnp.concatenate([key_rows, value_rows], axis=1)
    half_rows = own_rows.shape[0] // lax.axis_size("sub")
    row_start = lax.axis_index("sub") * half_rows
    own_half = lax.dynamic_slice_in_dim(own_rows, row_start, half_rows, 0)
    position = lax.axis_index(("img", "pair"))
    image_count = lax.axis_size(("img", "pair"))
    summed = jnp.zeros(key_rows.shape, jnp.float32)
    offsets = list(range(1, SPAN + 1)) + list(range(-SPAN, 0))
    for offset in offsets:
        partner_keys, partner_values = fetch_partner(offset, packed, local_width)
        step_size = abs(offset)
        lower_image = position + min(offset, 0)
        linked = link_value(links, lower_image, step_size, image_count)
        message, unused = tile_messages(key_rows, partner_keys, partner_values)
        summed = summed + linked * message.astype(jnp.float32)
    summed_b = summed.astype(jnp.bfloat16)
    gathered = lax.all_to_all(summed_b, "sub", split_axis=0, concat_axis=1, tiled=True)
    projected = jnp.dot(gathered, out_weight, preferred_element_type=jnp.float32).astype(
        jnp.bfloat16
    )
    hidden = jnp.dot(own_half, mlp_in[:D], preferred_element_type=jnp.float32)
    hidden = (
        hidden + jnp.dot(projected, mlp_in[D:], preferred_element_type=jnp.float32) + mlp_in_bias
    )
    mean_value = jnp.mean(hidden, axis=1, keepdims=True)
    centered = hidden - mean_value
    variance = jnp.mean(centered * centered, axis=1, keepdims=True)
    normed = centered * lax.rsqrt(variance + 1e-05) * norm_gain + norm_bias
    activated = jax.nn.gelu(normed, approximate=False).astype(jnp.bfloat16)
    output_rows = jnp.dot(activated, mlp_out, preferred_element_type=jnp.float32) + mlp_out_bias
    output_rows = output_rows + own_half.astype(jnp.float32)
    return output_rows.astype(jnp.bfloat16)[None]


def solution(mesh):
    placed = (
        P(("groups", "img", "pair"), None, None),
        P("groups", None),
        P(None, "sub"),
        P(None, "sub"),
        P(),
        P(),
        P(),
        P(),
        P(),
        P(),
        P(),
    )
    return jax.shard_map(
        on_device,
        mesh=mesh,
        in_specs=placed,
        out_specs=P(("groups", "img", "pair"), "sub", None),
        check_vma=False,
    )
```

profile of v0, /device:TPU:17, one launch (start us, length us, event | category | flops | bytes accessed | tf_op | source)
XLA Modules:
  0.0 95.1 jit_solution(5887512537064446653)
XLA Ops:
  0.0 0.0 copy-start
  0.0 1.4 %convolution_convert_fusion.2 = bf16[1024,128]{0,1:T(8,128)(2,1)S(1)} fusion(bf16[256,128]{1,0:T(8,128)(2,1)} %param.13, bf16[1,1024,256]{2,1,0:T(8,128)(2,1)} %param.11), kind=kOutput, calls=%fused_computation.68 | convolution fusion | flops 67239936 | bytes 851968 | tf_op jit(solution)/shard_map/dot_general | solution.py:70
  1.4 1.4 %convolution_convert_fusion.1 = bf16[1024,128]{0,1:T(8,128)(2,1)S(1)} fusion(bf16[256,128]{1,0:T(8,128)(2,1)} %param.14, bf16[1,1024,256]{2,1,0:T(8,128)(2,1)} %param.11), kind=kOutput, calls=%fused_computation.67 | convolution fusion | flops 67239936 | bytes 851968 | tf_op jit(solution)/shard_map/dot_general | solution.py:71
  2.8 3.1 %collective-permute-start.5 = (bf16[1024,256]{0,1:T(8,128)(2,1)S(1)}, bf16[1024,256]{0,1:T(8,128)(2,1)}, u32[]{:S(2)}, u32[]{:S(2)}) collective-permute-start(bf16[1024,256]{0,1:T(8,128)(2,1)S(1)} %pad_maximum_fusion), channel_id=1, source_target_pairs={{0,2},{2,4},{4,6},{6,8},{8,10},{10,12},{12,14},{1,3},{3,5},{5,7},{... | collective-permute-start | bytes 1572872 | tf_op jit(solution)/shard_map/ppermute | solution.py:16
  5.9 3.2 %collective-permute-start.4 = (bf16[1024,256]{0,1:T(8,128)(2,1)S(1)}, bf16[1024,256]{0,1:T(8,128)(2,1)}, u32[]{:S(2)}, u32[]{:S(2)}) collective-permute-start(bf16[1024,256]{0,1:T(8,128)(2,1)S(1)} %pad_maximum_fusion), channel_id=1, source_target_pairs={{0,4},{2,6},{4,8},{6,10},{8,12},{10,14},{1,5},{3,7},{5,9},{7,11},{... | collective-permute-start | bytes 1572872 | tf_op jit(solution)/shard_map/ppermute | solution.py:16
  9.1 1.9 %collective-permute-start.3 = (bf16[1024,256]{0,1:T(8,128)(2,1)S(1)}, bf16[1024,256]{0,1:T(8,128)(2,1)}, u32[]{:S(2)}, u32[]{:S(2)}) collective-permute-start(bf16[1024,256]{0,1:T(8,128)(2,1)S(1)} %pad_maximum_fusion), channel_id=1, source_target_pairs={{0,6},{2,8},{4,10},{6,12},{8,14},{1,7},{3,9},{5,11},{7,13},{9,15},... | collective-permute-start | bytes 1572872 | tf_op jit(solution)/shard_map/ppermute | solution.py:16
  11.1 5.9 %collective-permute-start.2 = (bf16[1024,256]{0,1:T(8,128)(2,1)S(1)}, bf16[1024,256]{0,1:T(8,128)(2,1)S(1)}, u32[]{:S(2)}, u32[]{:S(2)}) collective-permute-start(bf16[1024,256]{0,1:T(8,128)(2,1)S(1)} %pad_maximum_fusion), channel_id=1, source_target_pairs={{6,0},{8,2},{10,4},{12,6},{14,8},{7,1},{9,3},{11,5},{13,7},{15,9},... | collective-permute-start | bytes 1572872 | tf_op jit(solution)/shard_map/ppermute | solution.py:16
  17.0 1.9 %collective-permute-start.1 = (bf16[1024,256]{0,1:T(8,128)(2,1)S(1)}, bf16[1024,256]{0,1:T(8,128)(2,1)S(1)}, u32[]{:S(2)}, u32[]{:S(2)}) collective-permute-start(bf16[1024,256]{0,1:T(8,128)(2,1)S(1)} %pad_maximum_fusion), channel_id=1, source_target_pairs={{4,0},{6,2},{8,4},{10,6},{12,8},{14,10},{5,1},{7,3},{9,5},{11,7},{... | collective-permute-start | bytes 1572872 | tf_op jit(solution)/shard_map/ppermute | solution.py:16
  19.0 1.6 %constant_dynamic-slice_fusion.1 = (s32[1,1]{0,1:T(1,128)}, s32[1,1]{0,1:T(1,128)}, s32[1,1]{0,1:T(1,128)}, s32[1,1]{0,1:T(1,128)}, s32[1,1]{0,1:T(1,128)}, /*index=5*/s32[1,1]{0,1:T(1,128)}) fusion(s32[8,3]{0,1:T(4,128)} %param.12, s32[]{:T(128)S(6)} %min.15, s32[]{:T(128)S(6)} %min.16, s32[]{:T(128)S(6)} %min.18, s32[]{:T(128)S(6)} %min.17), kind=kLoop, calls=%fused_computation.208 | loop fusion | bytes 64 | tf_op jit(solution)/shard_map/dynamic_slice | solution.py:22
  24.3 1.4 %fusion.87 = f32[512,512]{0,1:T(8,128)S(1)} fusion(bf16[512,512]{1,0:T(8,128)(2,1)} %param.16, bf16[1,1024,256]{2,1,0:T(8,128)(2,1)} %param.11, s32[]{:T(128)S(6)} %select_n.28), kind=kOutput, calls=%fused_computation.140 | convolution fusion | flops 134217728 | bytes 1572868 | tf_op jit(solution)/shard_map/dot_general | solution.py:95
  25.7 0.0 collective-permute-done.5
  25.7 2.2 %collective-permute-start = (bf16[1024,256]{0,1:T(8,128)(2,1)S(1)}, bf16[1024,256]{0,1:T(8,128)(2,1)S(1)}, u32[]{:S(2)}, u32[]{:S(2)}) collective-permute-start(bf16[1024,256]{0,1:T(8,128)(2,1)S(1)} %pad_maximum_fusion), channel_id=1, source_target_pairs={{2,0},{4,2},{6,4},{8,6},{10,8},{12,10},{14,12},{3,1},{5,3},{7,5},{... | collective-permute-start | bytes 1572872 | tf_op jit(solution)/shard_map/ppermute | solution.py:16
  27.8 1.7 %multiply_reduce_fusion.1 = (f32[1024]{0:T(1024)S(1)}, f32[1024,1024]{0,1:T(8,128)S(1)}) fusion(bf16[1024,256]{0,1:T(8,128)(2,1)} %collective-permute-done.5, bf16[1024,128]{0,1:T(8,128)(2,1)S(1)} %convolution_convert_fusion.2), kind=kOutput, calls=%fused_computation.25 | convolution fusion | flops 136313856 | bytes 4460544 | tf_op jit(solution)/shard_map/qd,kd->qk/dot_general | solution.py:41
  29.5 1.7 %multiply_reduce_fusion = (f32[1024]{0:T(1024)S(1)}, f32[1024,1024]{0,1:T(8,128)S(1)}) fusion(bf16[1024,256]{0,1:T(8,128)(2,1)} %collective-permute-done.5, bf16[1024,128]{0,1:T(8,128)(2,1)S(1)} %convolution_convert_fusion.2), kind=kOutput, calls=%fused_computation.24 | convolution fusion | flops 136313856 | bytes 4460544 | tf_op jit(solution)/shard_map/qd,kd->qk/dot_general | solution.py:41
  31.2 0.7 fusion.10
  31.9 0.7 fusion.11
  32.6 0.0 collective-permute-done.4
  32.7 1.7 %multiply_reduce_fusion.3 = (f32[1024]{0:T(1024)S(1)}, f32[1024,1024]{0,1:T(8,128)S(1)}) fusion(bf16[1024,256]{0,1:T(8,128)(2,1)} %collective-permute-done.4, bf16[1024,128]{0,1:T(8,128)(2,1)S(1)} %convolution_convert_fusion.2), kind=kOutput, calls=%fused_computation.27 | convolution fusion | flops 136313856 | bytes 4460544 | tf_op jit(solution)/shard_map/qd,kd->qk/dot_general | solution.py:41
  34.3 1.7 %multiply_reduce_fusion.2 = (f32[1024]{0:T(1024)S(1)}, f32[1024,1024]{0,1:T(8,128)S(1)}) fusion(bf16[1024,256]{0,1:T(8,128)(2,1)} %collective-permute-done.4, bf16[1024,128]{0,1:T(8,128)(2,1)S(1)} %convolution_convert_fusion.2), kind=kOutput, calls=%fused_computation.26 | convolution fusion | flops 136313856 | bytes 4460544 | tf_op jit(solution)/shard_map/qd,kd->qk/dot_general | solution.py:41
  36.0 0.7 fusion.8
  36.7 0.7 fusion.9
  37.5 3.5 %collective-permute-done.3 = bf16[1024,256]{0,1:T(8,128)(2,1)} collective-permute-done((bf16[1024,256]{0,1:T(8,128)(2,1)S(1)}, bf16[1024,256]{0,1:T(8,128)(2,1)}, u32[]{:S(2)}, u32[]{:S(2)}) %collective-permute-start.3) | collective-permute-done | bytes 524320 | tf_op jit(solution)/shard_map/ppermute | solution.py:16
  41.0 1.7 %multiply_reduce_fusion.5 = (f32[1024]{0:T(1024)S(1)}, f32[1024,1024]{0,1:T(8,128)S(1)}) fusion(bf16[1024,256]{0,1:T(8,128)(2,1)} %collective-permute-done.3, bf16[1024,128]{0,1:T(8,128)(2,1)S(1)} %convolution_convert_fusion.2), kind=kOutput, calls=%fused_computation.29 | convolution fusion | flops 136313856 | bytes 4460544 | tf_op jit(solution)/shard_map/qd,kd->qk/dot_general | solution.py:41
  42.7 0.7 fusion.6
  43.4 1.7 %multiply_reduce_fusion.4 = (f32[1024]{0:T(1024)S(1)}, f32[1024,1024]{0,1:T(8,128)S(1)}) fusion(bf16[1024,256]{0,1:T(8,128)(2,1)} %collective-permute-done.3, bf16[1024,128]{0,1:T(8,128)(2,1)S(1)} %convolution_convert_fusion.2), kind=kOutput, calls=%fused_computation.28 | convolution fusion | flops 136313856 | bytes 4460544 | tf_op jit(solution)/shard_map/qd,kd->qk/dot_general | solution.py:41
  45.1 1.9 %fusion.29 = bf16[1024,64]{0,1:T(8,128)(2,1)S(1)} fusion(f32[1024,1024]{0,1:T(8,128)S(1)} %get-tuple-element.34, f32[1024]{0:T(1024)S(1)} %fusion.10, f32[1024]{0:T(1024)S(1)} %get-tuple-element.33, bf16[1024,256]{0,1:T(8,128)(2,1)} %collective-permute-done.5), kind=kOutput, calls=%fused_computation.71 | convolution fusion | flops 138477568 | bytes 4464640 | tf_op jit(solution)/shard_map/dot_general | solution.py:46
  46.9 1.9 %fusion.28 = bf16[1024,64]{0,1:T(8,128)(2,1)S(1)} fusion(f32[1024,1024]{0,1:T(8,128)S(1)} %get-tuple-element.32, f32[1024]{0:T(1024)S(1)} %fusion.11, f32[1024]{0:T(1024)S(1)} %get-tuple-element.31, bf16[1024,256]{0,1:T(8,128)(2,1)} %collective-permute-done.5), kind=kOutput, calls=%fused_computation.70 | convolution fusion | flops 138477568 | bytes 4464640 | tf_op jit(solution)/shard_map/dot_general | solution.py:46
  48.8 0.7 fusion.7
  49.5 0.0 collective-permute-done.2
  49.5 0.8 multiply_reduce_fusion.7
  50.3 0.7 fusion.4
  51.0 1.0 %multiply_reduce_fusion.6 = (f32[1024]{0:T(1024)S(1)}, f32[1024,1024]{0,1:T(8,128)S(1)}) fusion(bf16[1024,256]{0,1:T(8,128)(2,1)S(1)} %collective-permute-done.2, bf16[1024,128]{0,1:T(8,128)(2,1)S(1)} %convolution_convert_fusion.2), kind=kOutput, calls=%fused_computation.30 | convolution fusion | flops 136313856 | bytes 4460544 | tf_op jit(solution)/shard_map/qd,kd->qk/dot_general | solution.py:41
  52.0 1.9 %fusion.31 = bf16[1024,64]{0,1:T(8,128)(2,1)S(1)} fusion(f32[1024,1024]{0,1:T(8,128)S(1)} %get-tuple-element.30, f32[1024]{0:T(1024)S(1)} %fusion.8, f32[1024]{0:T(1024)S(1)} %get-tuple-element.29, bf16[1024,256]{0,1:T(8,128)(2,1)} %collective-permute-done.4), kind=kOutput, calls=%fused_computation.73 | convolution fusion | flops 138477568 | bytes 4464640 | tf_op jit(solution)/shard_map/dot_general | solution.py:46
  53.9 1.9 %fusion.30 = bf16[1024,64]{0,1:T(8,128)(2,1)S(1)} fusion(f32[1024,1024]{0,1:T(8,128)S(1)} %get-tuple-element.28, f32[1024]{0:T(1024)S(1)} %fusion.9, f32[1024]{0:T(1024)S(1)} %get-tuple-element.27, bf16[1024,256]{0,1:T(8,128)(2,1)} %collective-permute-done.4), kind=kOutput, calls=%fused_computation.72 | convolution fusion | flops 138477568 | bytes 4464640 | tf_op jit(solution)/shard_map/dot_general | solution.py:46
  55.8 0.7 fusion.5
  56.5 0.0 collective-permute-done.1
  56.5 0.8 multiply_reduce_fusion.9
  57.3 0.7 fusion.2
  58.0 0.8 multiply_reduce_fusion.8
  58.8 0.7 fusion.3
  59.5 1.9 %fusion.33 = bf16[1024,64]{0,1:T(8,128)(2,1)S(1)} fusion(f32[1024,1024]{0,1:T(8,128)S(1)} %get-tuple-element.26, f32[1024]{0:T(1024)S(1)} %fusion.6, f32[1024]{0:T(1024)S(1)} %get-tuple-element.25, bf16[1024,256]{0,1:T(8,128)(2,1)} %collective-permute-done.3), kind=kOutput, calls=%fused_computation.75 | convolution fusion | flops 138477568 | bytes 4464640 | tf_op jit(solution)/shard_map/dot_general | solution.py:46
  61.4 1.9 %fusion.32 = bf16[1024,64]{0,1:T(8,128)(2,1)S(1)} fusion(f32[1024,1024]{0,1:T(8,128)S(1)} %get-tuple-element.24, f32[1024]{0:T(1024)S(1)} %fusion.7, f32[1024]{0:T(1024)S(1)} %get-tuple-element.23, bf16[1024,256]{0,1:T(8,128)(2,1)} %collective-permute-done.3), kind=kOutput, calls=%fused_computation.74 | convolution fusion | flops 138477568 | bytes 4464640 | tf_op jit(solution)/shard_map/dot_general | solution.py:46
  63.2 1.0 %fusion.35 = bf16[1024,64]{0,1:T(8,128)(2,1)S(1)} fusion(f32[1024,1024]{0,1:T(8,128)S(1)} %get-tuple-element.22, f32[1024]{0:T(1024)S(1)} %fusion.4, f32[1024]{0:T(1024)S(1)} %get-tuple-element.21, bf16[1024,256]{0,1:T(8,128)(2,1)S(1)} %collective-permute-done.2), kind=kOutput, calls=%fused_computation.77 | convolution fusion | flops 138477568 | bytes 4464640 | tf_op jit(solution)/shard_map/dot_general | solution.py:46
  64.2 1.0 %fusion.34 = bf16[1024,64]{0,1:T(8,128)(2,1)S(1)} fusion(f32[1024,1024]{0,1:T(8,128)S(1)} %get-tuple-element.20, f32[1024]{0:T(1024)S(1)} %fusion.5, f32[1024]{0:T(1024)S(1)} %get-tuple-element.19, bf16[1024,256]{0,1:T(8,128)(2,1)S(1)} %collective-permute-done.2), kind=kOutput, calls=%fused_computation.76 | convolution fusion | flops 138477568 | bytes 4464640 | tf_op jit(solution)/shard_map/dot_general | solution.py:46
  65.2 1.0 %fusion.37 = bf16[1024,64]{0,1:T(8,128)(2,1)S(1)} fusion(f32[1024,1024]{0,1:T(8,128)S(1)} %get-tuple-element.18, f32[1024]{0:T(1024)S(1)} %fusion.2, f32[1024]{0:T(1024)S(1)} %get-tuple-element.17, bf16[1024,256]{0,1:T(8,128)(2,1)S(1)} %collective-permute-done.1), kind=kOutput, calls=%fused_computation.79 | convolution fusion | flops 138477568 | bytes 4464640 | tf_op jit(solution)/shard_map/dot_general | solution.py:46
  66.1 1.0 %fusion.36 = bf16[1024,64]{0,1:T(8,128)(2,1)S(1)} fusion(f32[1024,1024]{0,1:T(8,128)S(1)} %get-tuple-element.16, f32[1024]{0:T(1024)S(1)} %fusion.3, f32[1024]{0:T(1024)S(1)} %get-tuple-element.15, bf16[1024,256]{0,1:T(8,128)(2,1)S(1)} %collective-permute-done.1), kind=kOutput, calls=%fused_computation.78 | convolution fusion | flops 138477568 | bytes 4464640 | tf_op jit(solution)/shard_map/dot_general | solution.py:46
  67.2 0.0 collective-permute-done
  67.2 0.8 multiply_reduce_fusion.11
  67.9 1.0 fusion
  68.9 0.8 multiply_reduce_fusion.10
  69.7 0.7 fusion.1
  70.4 1.0 fusion.39
  71.4 0.0 copy-start.2
  71.4 0.0 copy-start.3
  71.4 1.0 %fusion.38 = bf16[1024,64]{0,1:T(8,128)(2,1)S(1)} fusion(f32[1024,1024]{0,1:T(8,128)S(1)} %get-tuple-element.12, f32[1024]{0:T(1024)S(1)} %fusion.1, f32[1024]{0:T(1024)S(1)} %get-tuple-element.11, bf16[1024,256]{0,1:T(8,128)(2,1)S(1)} %collective-permute-done), kind=kOutput, calls=%fused_computation.80 | convolution fusion | flops 138477568 | bytes 4464640 | tf_op jit(solution)/shard_map/dot_general | solution.py:46
  72.3 0.0 copy-start.4
  72.4 0.0 copy-start.5
  72.4 0.0 copy-start.6
  72.4 0.3 add_convert_fusion
  72.7 17.1 %all_to_all.16 = bf16[2,512,128]{1,2,0:T(8,128)(2,1)S(1)} all-to-all(bf16[2,512,128]{1,2,0:T(8,128)(2,1)S(1)} %add_convert_fusion), channel_id=1, replica_groups=mesh['groups'=2,'img'=4,'pair'=2,'sub'=2] {'sub'}, dimensions={0} | all-to-all | bytes 524288 | tf_op jit(solution)/shard_map/all_to_all | solution.py:91
  89.8 1.5 %fusion.183 = (f32[512]{0:T(512)S(1)}, f32[512,512]{0,1:T(8,128)S(1)}) fusion(f32[512]{0:T(512)S(1)} %copy-done.3, f32[512,512]{0,1:T(8,128)S(1)} %fusion.87, bf16[512,512]{1,0:T(8,128)(2,1)} %param.16, bf16[512,256]{0,1:T(8,128)(2,1)S(1)} %bitcast.61, bf16[256,256]{1,0:T(8,128)(2,1)S(1)} %copy-done.2), kind=kOutput, calls=%fused_computation.256 | convolution fusion | flops 202243584 | bytes 2756608 | tf_op jit(solution)/shard_map/dot_general | solution.py:97
  91.4 0.2 multiply_reduce_fusion.12
  91.6 0.0 copy-done
  91.6 3.5 %fusion.27 = bf16[1,512,256]{2,1,0:T(8,128)(2,1)} fusion(bf16[512,256]{1,0:T(8,128)(2,1)S(1)} %copy-done, f32[512,512]{0,1:T(8,128)S(1)} %get-tuple-element.36, f32[512]{0:T(512)S(1)} %copy-done.4, f32[512]{0:T(512)S(1)} %copy-done.5, f32[512]{0:T(512)S(1)} %add_rsqrt_fusion, f32[512]{0:T(512)S(1)} %broadcast_multiply_fusion, f32[256]{0:T(256)S(1)} %copy-done.6, ...), kind=kOutput, calls=%fused_computation.69 | convolution fusion | flops 152829952 | bytes 1844228 | tf_op jit(solution)/shard_map/dot_general | solution.py:104
  (16 shorter events, 0.2 us)
Async XLA Ops:
  0.0 91.6 %copy-start = (bf16[512,256]{1,0:T(8,128)(2,1)S(1)}, bf16[512,256]{1,0:T(8,128)(2,1)}, u32[]{:S(2)}) copy-start(bf16[512,256]{1,0:T(8,128)(2,1)} %param.20) | copy-start | bytes 786436
  2.8 22.9 %collective-permute-start.5 = (bf16[1024,256]{0,1:T(8,128)(2,1)S(1)}, bf16[1024,256]{0,1:T(8,128)(2,1)}, u32[]{:S(2)}, u32[]{:S(2)}) collective-permute-start(bf16[1024,256]{0,1:T(8,128)(2,1)S(1)} %pad_maximum_fusion), channel_id=1, source_target_pairs={{0,2},{2,4},{4,6},{6,8},{8,10},{10,12},{12,14},{1,3},{3,5},{5,7},{... | collective-permute-start | bytes 1572872 | tf_op jit(solution)/shard_map/ppermute | solution.py:16
  5.9 26.7 %collective-permute-start.4 = (bf16[1024,256]{0,1:T(8,128)(2,1)S(1)}, bf16[1024,256]{0,1:T(8,128)(2,1)}, u32[]{:S(2)}, u32[]{:S(2)}) collective-permute-start(bf16[1024,256]{0,1:T(8,128)(2,1)S(1)} %pad_maximum_fusion), channel_id=1, source_target_pairs={{0,4},{2,6},{4,8},{6,10},{8,12},{10,14},{1,5},{3,7},{5,9},{7,11},{... | collective-permute-start | bytes 1572872 | tf_op jit(solution)/shard_map/ppermute | solution.py:16
  9.1 31.8 %collective-permute-start.3 = (bf16[1024,256]{0,1:T(8,128)(2,1)S(1)}, bf16[1024,256]{0,1:T(8,128)(2,1)}, u32[]{:S(2)}, u32[]{:S(2)}) collective-permute-start(bf16[1024,256]{0,1:T(8,128)(2,1)S(1)} %pad_maximum_fusion), channel_id=1, source_target_pairs={{0,6},{2,8},{4,10},{6,12},{8,14},{1,7},{3,9},{5,11},{7,13},{9,15},... | collective-permute-start | bytes 1572872 | tf_op jit(solution)/shard_map/ppermute | solution.py:16
  11.1 38.5 %collective-permute-start.2 = (bf16[1024,256]{0,1:T(8,128)(2,1)S(1)}, bf16[1024,256]{0,1:T(8,128)(2,1)S(1)}, u32[]{:S(2)}, u32[]{:S(2)}) collective-permute-start(bf16[1024,256]{0,1:T(8,128)(2,1)S(1)} %pad_maximum_fusion), channel_id=1, source_target_pairs={{6,0},{8,2},{10,4},{12,6},{14,8},{7,1},{9,3},{11,5},{13,7},{15,9},... | collective-permute-start | bytes 1572872 | tf_op jit(solution)/shard_map/ppermute | solution.py:16
  17.0 39.5 %collective-permute-start.1 = (bf16[1024,256]{0,1:T(8,128)(2,1)S(1)}, bf16[1024,256]{0,1:T(8,128)(2,1)S(1)}, u32[]{:S(2)}, u32[]{:S(2)}) collective-permute-start(bf16[1024,256]{0,1:T(8,128)(2,1)S(1)} %pad_maximum_fusion), channel_id=1, source_target_pairs={{4,0},{6,2},{8,4},{10,6},{12,8},{14,10},{5,1},{7,3},{9,5},{11,7},{... | collective-permute-start | bytes 1572872 | tf_op jit(solution)/shard_map/ppermute | solution.py:16
  25.7 41.5 %collective-permute-start = (bf16[1024,256]{0,1:T(8,128)(2,1)S(1)}, bf16[1024,256]{0,1:T(8,128)(2,1)S(1)}, u32[]{:S(2)}, u32[]{:S(2)}) collective-permute-start(bf16[1024,256]{0,1:T(8,128)(2,1)S(1)} %pad_maximum_fusion), channel_id=1, source_target_pairs={{2,0},{4,2},{6,4},{8,6},{10,8},{12,10},{14,12},{3,1},{5,3},{7,5},{... | collective-permute-start | bytes 1572872 | tf_op jit(solution)/shard_map/ppermute | solution.py:16
  71.4 18.5 %copy-start.2 = (bf16[256,256]{1,0:T(8,128)(2,1)S(1)}, bf16[256,256]{1,0:T(8,128)(2,1)}, u32[]{:S(2)}) copy-start(bf16[256,256]{1,0:T(8,128)(2,1)} %param.15) | copy-start | bytes 393220
  71.4 18.5 %copy-start.3 = (f32[512]{0:T(512)S(1)}, f32[512]{0:T(512)}, u32[]{:S(2)}) copy-start(f32[512]{0:T(512)} %param.17) | copy-start | bytes 6148
  72.3 19.2 %copy-start.1 = (bf16[1,1024,256]{2,1,0:T(8,128)(2,1)S(1)}, bf16[1,1024,256]{2,1,0:T(8,128)(2,1)}, u32[]{:S(2)}) copy-start(bf16[1,1024,256]{2,1,0:T(8,128)(2,1)} %param.11) | copy-start | bytes 1572868
  72.3 19.2 %copy-start.4 = (f32[512]{0:T(512)S(1)}, f32[512]{0:T(512)}, u32[]{:S(2)}) copy-start(f32[512]{0:T(512)} %param.19) | copy-start | bytes 6148
  72.4 19.2 %copy-start.5 = (f32[512]{0:T(512)S(1)}, f32[512]{0:T(512)}, u32[]{:S(2)}) copy-start(f32[512]{0:T(512)} %param.18) | copy-start | bytes 6148
  72.4 19.2 %copy-start.6 = (f32[256]{0:T(256)S(1)}, f32[256]{0:T(256)}, u32[]{:S(2)}) copy-start(f32[256]{0:T(256)} %param.21) | copy-start | bytes 3076
where the time goes:
time: 95.8 us; the launch traced here: 95.1 us
  matrix products  40.8 us (43%)
  starting transfers between devices  18.3 us (19%)
  blocking collectives  17.1 us (18%)
  other arithmetic  9.53 us (10%)
  between operations  4.11 us (4%)
  waiting for transfers between devices  3.54 us (4%)
  local copies, waits for them, and re-layouts  1.74 us (2%)
    ppermute x6, starting transfers between devices, passed_along(): return lax.ppermute(value, axis, pairs)  18.3 us
    all_to_all x1, blocking collectives, on_device(): lax.all_to_all(summed_b, 'sub', split_axis=0, concat_axis=1, tiled=True)  17.1 us
    dot_general x12, matrix products, tile_messages(): jnp.dot(row_weights, partner_values[:, lo_col:lo_col + head_width], prefe...  16.9 us
    dot_general x12, matrix products, tile_messages(): jnp.einsum('qd,kd->qk', query_part, key_part, preferred_element_type=jnp....  14.8 us
    reduce_sum x12, other arithmetic, tile_messages(): row_weights = jax.nn.softmax(scores, axis=1).astype(jnp.bfloat16)  8.99 us
    ppermute x6, waiting for transfers between devices, passed_along(): return lax.ppermute(value, axis, pairs)  3.54 us
    dot_general x1, matrix products, on_device(): jnp.dot(activated, mlp_out, preferred_element_type=jnp.float32)  3.52 us
  transfers between devices with their start and end apart: 6, of which 1 were waited for; matrix products, arithmetic and copies ran while one was open for 41% of the time, Pallas kernels for 0%

commit v1 on v0

v1 whole, which is shorter than its diff:
```python
import functools
import math

import jax
import jax.numpy as jnp
from jax import lax
from jax.experimental import pallas as pl
from jax.experimental.pallas import tpu as pltpu
from jax.sharding import PartitionSpec as P

HEADS = 4
SPAN = 3
RING = ("img", "pair", "sub")
SCORE_LIMIT = 75.0
VALUE_LIMIT = 256.0
F32 = jnp.float32
BF16 = jnp.bfloat16
VMEM = pl.BlockSpec(memory_space=pltpu.VMEM)
SMEM = pl.BlockSpec(memory_space=pltpu.SMEM)


def dot(a, b, contract=(1, 0)):
    return lax.dot_general(
        a, b, (((contract[0],), (contract[1],)), ((), ())), preferred_element_type=F32
    )


def largest_norms(keys, head_width):
    squares = keys.astype(F32)
    squares = (squares * squares * 1.01).astype(BF16)
    width = keys.shape[1]
    head_of = lax.broadcasted_iota(jnp.int32, (width, 128), 0) // head_width
    lane = lax.broadcasted_iota(jnp.int32, (width, 128), 1)
    sums = dot(squares, jnp.where(head_of == lane, 1.0, 0.0).astype(BF16))
    return jnp.max(sums, axis=0, keepdims=True)


def prologue_kernel(
    place_ref, x_ref, own_ref, other_ref, mlp_ref, bias_ref, wkv_ref, keys_ref, norm_ref, hidden_ref
):
    rows, width = x_ref.shape
    local = width // 2
    sub = lax.rem(place_ref[0], 2)
    for part in range(2):
        own = own_ref[:, part * local : (part + 1) * local]
        other = other_ref[:, part * local : (part + 1) * local]
        start = part * width
        wkv_ref[:, start : start + local] = jnp.where(sub == 0, own, other)
        wkv_ref[:, start + local : start + width] = jnp.where(sub == 0, other, own)
    keys = dot(x_ref[...], wkv_ref[:, :width]).astype(BF16)
    keys_ref[...] = keys
    norm_ref[...] = jnp.broadcast_to(largest_norms(keys, width // HEADS), norm_ref.shape)
    half = rows // 2
    own_rows = x_ref[pl.ds(pl.multiple_of(sub * half, half), half), :]
    hidden_ref[...] = dot(own_rows, mlp_ref[:width, :]) + bias_ref[...]


def partner_kernel(
    step, images, last, place_ref, links_ref, keys_ref, norm_ref, x_ref, wkv_ref, *refs
):
    if last:
        first_ref, second_ref, keep_ref, send_ref, message_ref, kh_ref, vh_ref = refs
    else:
        message_ref, kh_ref, vh_ref = refs
    rows, width = keys_ref.shape
    head_width = width // HEADS
    scale = 1.0 / math.sqrt(head_width)
    image = place_ref[0] // 2
    sub = lax.rem(place_ref[0], 2)
    lower = image - sub * step
    inside = jnp.logical_and(lower >= 0, lower + step < images)
    entry = links_ref[step - 1, jnp.clip(lower, 0, images - 1)]
    linked = jnp.logical_and(inside, entry != 0)
    tile = 256
    lane = lax.broadcasted_iota(jnp.int32, (tile, 128), 1)

    @pl.when(jnp.logical_not(linked))
    def _():
        message_ref[...] = jnp.zeros_like(message_ref)

    @pl.when(linked)
    def _():
        norms = jnp.zeros((1, 128), F32)
        largest = jnp.zeros((tile, width), F32)
        for r in range(0, rows, tile):
            both = dot(x_ref[r : r + tile, :], wkv_ref[...]).astype(BF16)
            keys, values = both[:, :width], both[:, width:]
            norms = jnp.maximum(norms, largest_norms(keys, head_width))
            largest = jnp.maximum(largest, jnp.abs(values.astype(F32)))
            for head in range(HEADS):
                block, odd = head // 2 * 128, head % 2
                mine = (lane >= 64) if odd else (lane < 64)
                ones = jnp.where(lane == (0 if odd else 64), 1.0, 0.0).astype(BF16)
                kh_ref[head, r : r + tile, :] = jnp.where(
                    mine, keys[:, block : block + 128], jnp.zeros((), BF16)
                )
                vh_ref[head, r : r + tile, :] = jnp.where(
                    mine, values[:, block : block + 128], ones
                )
        bound = jnp.max(norms * norm_ref[0:1, :]) * (scale * scale)
        safe = jnp.logical_and(
            bound <= SCORE_LIMIT * SCORE_LIMIT, jnp.max(largest) <= VALUE_LIMIT
        )

        def heads_of(r, weights):
            for block in range(HEADS // 2):
                queries = keys_ref[pl.ds(r, tile), block * 128 : (block + 1) * 128]
                parts = []
                for odd in range(2):
                    head = 2 * block + odd
                    scores = dot(queries, kh_ref[head], (1, 1))
                    product = dot(weights(scores), vh_ref[head])
                    at = 0 if odd else 64
                    parts.append(product / product[:, at : at + 1])
                message_ref[pl.ds(r, tile), block * 128 : (block + 1) * 128] = jnp.where(
                    lane < 64, parts[0], parts[1]
                ).astype(BF16)

        @pl.when(safe)
        def _():
            def body(i, carry):
                heads_of(
                    pl.multiple_of(i * tile, tile),
                    lambda s: jnp.exp2(s * (scale * math.log2(math.e))).astype(BF16),
                )
                return carry

            lax.fori_loop(0, rows // tile, body, 0)

        @pl.when(jnp.logical_not(safe))
        def _():
            def weights(s):
                s = s * scale
                e = jnp.exp(s - jnp.max(s, axis=1, keepdims=True))
                return (e / jnp.sum(e, axis=1, keepdims=True)).astype(BF16)

            def body(i, carry):
                heads_of(pl.multiple_of(i * tile, tile), weights)
                return carry

            lax.fori_loop(0, rows // tile, body, 0)

    if last:
        half = rows // 2
        for out_ref, which in ((keep_ref, sub), (send_ref, 1 - sub)):
            at = pl.ds(pl.multiple_of(which * half, half), half)
            total = first_ref[at, :].astype(F32) + second_ref[at, :].astype(F32)
            total = total + message_ref[at, :].astype(F32)
            out_ref[...] = total.astype(out_ref.dtype)


def tail_kernel(
    place_ref, keep_ref, came_ref, hidden_ref, x_ref, out_ref, mlp_ref, gain_ref, shift_ref,
    mlp_out_ref, out_bias_ref, result_ref,
):
    rows, width = keep_ref.shape
    sub = lax.rem(place_ref[0], 2)
    summed = (keep_ref[...] + came_ref[...].astype(F32)).astype(BF16)
    projected = dot(summed, out_ref[...]).astype(BF16)
    hidden = hidden_ref[...] + dot(projected, mlp_ref[width:, :])
    centered = hidden - jnp.mean(hidden, axis=1, keepdims=True)
    variance = jnp.mean(centered * centered, axis=1, keepdims=True)
    normed = centered * lax.rsqrt(variance + 1e-05) * gain_ref[...] + shift_ref[...]
    activated = (0.5 * normed * (1.0 + lax.erf(normed * math.sqrt(0.5)))).astype(BF16)
    own_rows = x_ref[pl.ds(pl.multiple_of(sub * rows, rows), rows), :].astype(F32)
    updated = dot(activated, mlp_out_ref[...]) + out_bias_ref[...]
    result_ref[...] = (updated + own_rows).astype(BF16)


def shape(dims, dtype):
    return jax.ShapeDtypeStruct(dims, dtype)


def cost(flops, moved, exps=0):
    return pl.CostEstimate(flops=flops, bytes_accessed=moved, transcendentals=exps)


def on_device(
    descriptors,
    links,
    qk_weight,
    value_weight,
    out_weight,
    mlp_in,
    mlp_in_bias,
    norm_gain,
    norm_bias,
    mlp_out,
    mlp_out_bias,
):
    own = descriptors[0]
    rows, width = own.shape
    hidden_width = mlp_in.shape[1]
    images = lax.axis_size(("img", "pair"))
    place = lax.axis_index(RING).reshape(1)
    links_t = links.T
    params = pltpu.CompilerParams(vmem_limit_bytes=40 << 20)

    own_weights = jnp.concatenate([qk_weight, value_weight], axis=1)
    other_weights = lax.ppermute(own_weights, "sub", [(0, 1), (1, 0)])

    def fetched(step):
        pairs = []
        for image in range(images):
            if image - step >= 0:
                pairs.append((2 * image, 2 * (image - step)))
            if image + step < images:
                pairs.append((2 * image + 1, 2 * (image + step) + 1))
        return lax.ppermute(own, RING, pairs)

    steps = [2, 1, 3]
    partners = [fetched(step) for step in steps]

    wkv, keys, norms, hidden = pl.pallas_call(
        prologue_kernel,
        in_specs=[SMEM] + [VMEM] * 5,
        out_specs=[VMEM] * 4,
        out_shape=[
            shape((width, 2 * width), BF16),
            shape((rows, width), BF16),
            shape((8, 128), F32),
            shape((rows // 2, hidden_width), F32),
        ],
        compiler_params=params,
        cost_estimate=cost(4 * rows * width * width, 4 << 20),
        name="prologue",
    )(place, own, own_weights, other_weights, mlp_in, mlp_in_bias.reshape(1, -1))

    messages = []
    for step, partner in zip(steps, partners):
        last = step == steps[-1]
        out_shape = [shape((rows, width), BF16)]
        if last:
            out_shape = [shape((rows // 2, width), F32), shape((rows // 2, width), BF16)]
        scratch = [pltpu.VMEM((HEADS, rows, 128), BF16)] * 2
        if last:
            scratch = [pltpu.VMEM((rows, width), BF16)] + scratch
        got = pl.pallas_call(
            functools.partial(partner_kernel, step, images, last),
            in_specs=[SMEM, SMEM] + [VMEM] * (6 if last else 4),
            out_specs=[VMEM] * len(out_shape),
            out_shape=out_shape,
            scratch_shapes=scratch,
            compiler_params=params,
            cost_estimate=cost(8 * rows * rows * width, 2 << 20, HEADS * rows * rows),
            name=f"partner_{step}",
        )(place, links_t, keys, norms, partner, wkv, *(messages if last else ()))
        messages.extend(got)
    keep, send = messages[-2:]
    came = lax.ppermute(send, "sub", [(0, 1), (1, 0)])

    result = pl.pallas_call(
        tail_kernel,
        in_specs=[SMEM] + [VMEM] * 10,
        out_specs=VMEM,
        out_shape=shape((rows // 2, width), BF16),
        compiler_params=params,
        cost_estimate=cost(4 * rows * width * width, 4 << 20),
        name="tail",
    )(
        place, keep, came, hidden, own, out_weight, mlp_in, norm_gain.reshape(1, -1),
        norm_bias.reshape(1, -1), mlp_out, mlp_out_bias.reshape(1, -1),
    )
    return result[None]


def solution(mesh):
    placed = (
        P(("groups", "img", "pair"), None, None),
        P("groups", None),
        P(None, "sub"),
        P(None, "sub"),
        P(),
        P(),
        P(),
        P(),
        P(),
        P(),
        P(),
    )
    return jax.shard_map(
        on_device,
        mesh=mesh,
        in_specs=placed,
        out_specs=P(("groups", "img", "pair"), "sub", None),
        check_vma=False,
    )
```

time: 95.8 us -> 72.7 us (0.76)
  Pallas kernels: 0 us -> 41.6 us
  matrix products: 40.8 us -> 0 us
  blocking collectives: 17.1 us -> 0 us
  other arithmetic: 9.53 us -> 0 us
  waiting for transfers between devices: 3.54 us -> 7.84 us
  between operations: 4.11 us -> 0.19 us
  local copies, waits for them, and re-layouts: 1.74 us -> 5 us
    pallas_call x0 -> x5, Pallas kernels: none -> 41.6 us  [the longest x3 39.1 us: on_device(): pl.pallas_call(functools.partial(partner_kernel, step, images, last), in_...]
    dot_general x29 -> x0, matrix products: 40.8 us -> none  [the longest x12 16.9 us: tile_messages(): jnp.dot(row_weights, partner_values[:, lo_col:lo_col + head_width], prefe...]
    all_to_all x1 -> x0, blocking collectives: 17.1 us -> none  [on_device(): lax.all_to_all(summed_b, 'sub', split_axis=0, concat_axis=1, tiled=True)]
    reduce_sum x13 -> x0, other arithmetic: 9.17 us -> none  [the longest x12 8.99 us: tile_messages(): row_weights = jax.nn.softmax(scores, axis=1).astype(jnp.bfloat16)]
    unnamed x14 -> x25, local copies, waits for them, and re-layouts: 0.04 us -> 4.98 us
    ppermute x6 -> x5, waiting for transfers between devices: 3.54 us -> 7.84 us  [the longest x3 6.68 us: fetched(): return lax.ppermute(own, RING, pairs)]
    dynamic_slice x1 -> x0, local copies, waits for them, and re-layouts: 1.58 us -> none  [link_value(): lax.dynamic_slice(links, (clipped, jnp.int32(step_size - 1)), (1, 1))[0, 0]]
    ppermute x6 -> x5, starting transfers between devices: 18.3 us -> 17.7 us  [the longest x3 9.74 us: fetched(): return lax.ppermute(own, RING, pairs)]
  transfers between devices with their start and end apart: 6 -> 5, of which waited for: 1 -> 2; matrix products, arithmetic and copies ran while one was open for 41% -> 1% of each run, Pallas kernels for 0% -> 36%
where the time goes in v1:
time: 72.7 us; the launch traced here: 72.3 us
  Pallas kernels  41.6 us (57%)
  starting transfers between devices  17.7 us (24%)
  waiting for transfers between devices  7.84 us (11%)
  local copies, waits for them, and re-layouts  5 us (7%)
    pallas_call x3, Pallas kernels, on_device(): pl.pallas_call(functools.partial(partner_kernel, step, images, last), in_...  39.1 us
    ppermute x3, starting transfers between devices, fetched(): return lax.ppermute(own, RING, pairs)  9.74 us
    ppermute x1, starting transfers between devices, on_device(): came = lax.ppermute(send, 'sub', [(0, 1), (1, 0)])  7.86 us
    ppermute x3, waiting for transfers between devices, fetched(): return lax.ppermute(own, RING, pairs)  6.68 us
    unnamed x25, local copies, waits for them, and re-layouts  4.98 us
    pallas_call x1, Pallas kernels, on_device(): pl.pallas_call(tail_kernel, in_specs=[SMEM] + [VMEM] * 10, out_specs=VMEM...  1.76 us
  transfers between devices with their start and end apart: 5, of which 2 were waited for; matrix products, arithmetic and copies ran while one was open for 1% of the time, Pallas kernels for 36%

profile of v1, /device:TPU:17, one launch (start us, length us, event | category | flops | bytes accessed | tf_op | source)
XLA Modules:
  0.0 72.3 jit_solution(17902211686226509882)
XLA Ops:
  0.0 0.0 copy-start.11
  0.0 3.2 %collective-permute-start.3 = (bf16[1024,256]{1,0:T(8,128)(2,1)}, bf16[1024,256]{1,0:T(8,128)(2,1)S(1)}, u32[]{:S(2)}, u32[]{:S(2)}) collective-permute-start(bf16[1024,256]{1,0:T(8,128)(2,1)} %bitcast.8), channel_id=1, source_target_pairs={{1,3},{2,0},{3,5},{4,2},{5,7},{6,4},{7,9},{8,6},{9,11},{10,8},{11,... | collective-permute-start | bytes 1572872 | tf_op jit(solution)/shard_map/ppermute | solution.py:209
  3.3 3.2 %collective-permute-start.2 = (bf16[1024,256]{1,0:T(8,128)(2,1)}, bf16[1024,256]{1,0:T(8,128)(2,1)S(1)}, u32[]{:S(2)}, u32[]{:S(2)}) collective-permute-start(bf16[1024,256]{1,0:T(8,128)(2,1)} %bitcast.9), channel_id=1, source_target_pairs={{1,5},{3,7},{4,0},{5,9},{6,2},{7,11},{8,4},{9,13},{10,6},{11,15},{... | collective-permute-start | bytes 1572872 | tf_op jit(solution)/shard_map/ppermute | solution.py:209
  6.5 0.9 %constant_dynamic-update-slice_fusion.1 = bf16[256,256]{1,0:T(8,128)(2,1)S(1)} fusion(bf16[256,128]{1,0:T(8,128)(2,1)} %param.13), kind=kLoop, calls=%fused_computation.1 | loop fusion | bytes 131072
  7.3 0.0 copy-done.11
  7.4 0.1 collective-permute-start
  7.4 3.3 %collective-permute-start.1 = (bf16[1024,256]{1,0:T(8,128)(2,1)}, bf16[1024,256]{1,0:T(8,128)(2,1)S(1)}, u32[]{:S(2)}, u32[]{:S(2)}) collective-permute-start(bf16[1024,256]{1,0:T(8,128)(2,1)} %bitcast.10), channel_id=1, source_target_pairs={{1,7},{3,9},{5,11},{6,0},{7,13},{8,2},{9,15},{10,4},{12,6},{14,8},... | collective-permute-start | bytes 1572872 | tf_op jit(solution)/shard_map/ppermute | solution.py:209
  10.7 0.0 copy-start.8
  10.8 0.0 collective-permute-done.other_ref
  10.8 0.7 copy-done.8
  11.4 0.0 copy-start
  11.4 1.0 %copy-done = bf16[1,1024,256]{2,1,0:T(8,128)(2,1)S(1)} copy-done((bf16[1,1024,256]{2,1,0:T(8,128)(2,1)S(1)}, bf16[1,1024,256]{2,1,0:T(8,128)(2,1)}, u32[]{:S(2)}) %copy-start) | copy-done | bytes 524312
  12.5 0.0 copy-start.2
  12.5 1.0 %copy-done.2 = bf16[512,512]{1,0:T(8,128)(2,1)S(1)} copy-done((bf16[512,512]{1,0:T(8,128)(2,1)S(1)}, bf16[512,512]{1,0:T(8,128)(2,1)}, u32[]{:S(2)}) %copy-start.2) | copy-done | bytes 524312
  13.5 0.7 prologue.1
  14.2 6.7 %collective-permute-done.3.x_ref = bf16[1024,256]{1,0:T(8,128)(2,1)S(1)} collective-permute-done((bf16[1024,256]{1,0:T(8,128)(2,1)}, bf16[1024,256]{1,0:T(8,128)(2,1)S(1)}, u32[]{:S(2)}, u32[]{:S(2)}) %collective-permute-start.3) | collective-permute-done | bytes 524320 | tf_op jit(solution)/shard_map/ppermute | solution.py:209
  20.9 0.0 copy-start.10
  20.9 0.7 copy-done.10
  21.6 12.8 %partner_1.1.refs_1_ = bf16[1024,256]{1,0:T(8,128)(2,1)S(1)} custom-call(s32[1]{0:T(128)} %bitcast.place_ref, s32[3,8]{1,0:T(4,128)S(1)} %bitcast.17, bf16[1024,256]{1,0:T(8,128)(2,1)S(1)} %get-tuple-element.11.keys_ref, f32[8,128]{1,0:T(8,128)S(1)} %get-tuple-element.12.norm_ref, bf16[1024,256]{1,0:T(8,128)(2,1)S(1)} %collective-permute-done.3.x_ref, ...), custom_call_target="tpu_custom_call" | custom-call | flops 2147483648 | bytes 2097152 | tf_op jit(solution)/shard_map/partner_1/pallas_call | solution.py:238
  34.4 0.0 collective-permute-done.2.x_ref
  34.4 12.8 %partner_2.1.refs_0_ = bf16[1024,256]{1,0:T(8,128)(2,1)S(1)} custom-call(s32[1]{0:T(128)} %bitcast.place_ref, s32[3,8]{1,0:T(4,128)S(1)} %bitcast.18, bf16[1024,256]{1,0:T(8,128)(2,1)S(1)} %get-tuple-element.11.keys_ref, f32[8,128]{1,0:T(8,128)S(1)} %get-tuple-element.12.norm_ref, bf16[1024,256]{1,0:T(8,128)(2,1)S(1)} %collective-permute-done.2.x_ref, ...), custom_call_target="tpu_custom_call" | custom-call | flops 2147483648 | bytes 2097152 | tf_op jit(solution)/shard_map/partner_2/pallas_call | solution.py:238
  47.3 0.0 copy-start.1
  47.3 0.0 copy-start.3
  47.3 0.0 copy-start.4
  47.3 0.0 copy-start.5
  47.3 0.0 collective-permute-done.1.x_ref
  47.3 13.4 %partner_3.1 = (f32[512,256]{1,0:T(8,128)S(1)}, bf16[512,256]{1,0:T(8,128)(2,1)S(1)}) custom-call(s32[1]{0:T(128)} %bitcast.place_ref, s32[3,8]{1,0:T(4,128)S(1)} %bitcast.19, bf16[1024,256]{1,0:T(8,128)(2,1)S(1)} %get-tuple-element.11.keys_ref, f32[8,128]{1,0:T(8,128)S(1)} %get-tuple-element.12.norm_ref, ...), custom_call_target="tpu_custom_call" | custom-call | flops 2147483648 | bytes 2097152 | tf_op jit(solution)/shard_map/partner_3/pallas_call | solution.py:238
  60.8 7.9 %collective-permute-start.4 = (bf16[512,256]{1,0:T(8,128)(2,1)S(1)}, bf16[512,256]{1,0:T(8,128)(2,1)S(1)}, u32[]{:S(2)}, u32[]{:S(2)}) collective-permute-start(bf16[512,256]{1,0:T(8,128)(2,1)S(1)} %get-tuple-element.15), channel_id=1, source_target_pairs={{0,1},{1,0},{2,3},{3,2},{4,5},{5,4},{6,7},{7,6},{8,9},{9,8},{10,11... | collective-permute-start | bytes 786440 | tf_op jit(solution)/shard_map/ppermute | solution.py:250
  68.6 1.2 %collective-permute-done.4.came_ref = bf16[512,256]{1,0:T(8,128)(2,1)S(1)} collective-permute-done((bf16[512,256]{1,0:T(8,128)(2,1)S(1)}, bf16[512,256]{1,0:T(8,128)(2,1)S(1)}, u32[]{:S(2)}, u32[]{:S(2)}) %collective-permute-start.4) | collective-permute-done | bytes 262176 | tf_op jit(solution)/shard_map/ppermute | solution.py:250
  69.8 0.0 copy-start.7
  69.8 0.0 copy-start.6
  69.8 0.0 copy-start.9
  69.8 0.0 copy-done.1
  69.8 0.0 copy-done.3
  69.8 0.0 copy-done.4
  69.8 0.0 copy-done.5
  69.8 0.6 copy-done.7
  70.5 0.0 copy-done.6
  70.5 0.0 copy-done.9
  70.5 1.8 %tail.1 = bf16[512,256]{1,0:T(8,128)(2,1)} custom-call(s32[1]{0:T(128)} %bitcast.place_ref, f32[512,256]{1,0:T(8,128)S(1)} %get-tuple-element.14.keep_ref, bf16[512,256]{1,0:T(8,128)(2,1)S(1)} %collective-permute-done.4.came_ref, f32[512,512]{1,0:T(8,128)S(1)} %get-tuple-element.16.hidden_ref, bf16[1024,256]{1,0:T(8,128)(2,1)S(1)} %bitcast.12, ...), custom_call_target="tpu_custom_call" | custom-call | flops 268435456 | bytes 4194304 | tf_op jit(solution)/shard_map/tail/pallas_call | solution.py:252
  (1 shorter events, 0.0 us)
Async XLA Ops:
  0.0 7.3 %copy-start.11 = (bf16[256,128]{1,0:T(8,128)(2,1)S(1)}, bf16[256,128]{1,0:T(8,128)(2,1)}, u32[]{:S(2)}) copy-start(bf16[256,128]{1,0:T(8,128)(2,1)} %param.14) | copy-start | bytes 196612
  0.0 20.9 %collective-permute-start.3 = (bf16[1024,256]{1,0:T(8,128)(2,1)}, bf16[1024,256]{1,0:T(8,128)(2,1)S(1)}, u32[]{:S(2)}, u32[]{:S(2)}) collective-permute-start(bf16[1024,256]{1,0:T(8,128)(2,1)} %bitcast.8), channel_id=1, source_target_pairs={{1,3},{2,0},{3,5},{4,2},{5,7},{6,4},{7,9},{8,6},{9,11},{10,8},{11,... | collective-permute-start | bytes 1572872 | tf_op jit(solution)/shard_map/ppermute | solution.py:209
  3.3 31.2 %collective-permute-start.2 = (bf16[1024,256]{1,0:T(8,128)(2,1)}, bf16[1024,256]{1,0:T(8,128)(2,1)S(1)}, u32[]{:S(2)}, u32[]{:S(2)}) collective-permute-start(bf16[1024,256]{1,0:T(8,128)(2,1)} %bitcast.9), channel_id=1, source_target_pairs={{1,5},{3,7},{4,0},{5,9},{6,2},{7,11},{8,4},{9,13},{10,6},{11,15},{... | collective-permute-start | bytes 1572872 | tf_op jit(solution)/shard_map/ppermute | solution.py:209
  7.4 3.4 %collective-permute-start = (bf16[256,256]{1,0:T(8,128)(2,1)S(1)}, bf16[256,256]{1,0:T(8,128)(2,1)S(1)}, u32[]{:S(2)}, u32[]{:S(2)}) collective-permute-start(bf16[256,256]{1,0:T(8,128)(2,1)S(1)} %constant_dynamic-update-slice_fusion.own_ref), channel_id=1, source_target_pairs={{0,1},{1,0},{2,3},{3,2},{4,5},{5,4},{6,7},{7,6},{8,9},{9,8},{10,11... | collective-permute-start | bytes 393224 | tf_op jit(solution)/shard_map/ppermute | solution.py:200
  7.4 39.9 %collective-permute-start.1 = (bf16[1024,256]{1,0:T(8,128)(2,1)}, bf16[1024,256]{1,0:T(8,128)(2,1)S(1)}, u32[]{:S(2)}, u32[]{:S(2)}) collective-permute-start(bf16[1024,256]{1,0:T(8,128)(2,1)} %bitcast.10), channel_id=1, source_target_pairs={{1,7},{3,9},{5,11},{6,0},{7,13},{8,2},{9,15},{10,4},{12,6},{14,8},... | collective-permute-start | bytes 1572872 | tf_op jit(solution)/shard_map/ppermute | solution.py:209
  10.7 0.7 copy-start.8
  11.4 1.0 %copy-start = (bf16[1,1024,256]{2,1,0:T(8,128)(2,1)S(1)}, bf16[1,1024,256]{2,1,0:T(8,128)(2,1)}, u32[]{:S(2)}) copy-start(bf16[1,1024,256]{2,1,0:T(8,128)(2,1)} %param.11) | copy-start | bytes 1572868
  12.5 1.0 %copy-start.2 = (bf16[512,512]{1,0:T(8,128)(2,1)S(1)}, bf16[512,512]{1,0:T(8,128)(2,1)}, u32[]{:S(2)}) copy-start(bf16[512,512]{1,0:T(8,128)(2,1)} %mlp_ref.3) | copy-start | bytes 1572868
  20.9 0.7 copy-start.10
  47.3 22.5 %copy-start.1 = (bf16[1,1024,256]{2,1,0:T(8,128)(2,1)S(1)}, bf16[1,1024,256]{2,1,0:T(8,128)(2,1)}, u32[]{:S(2)}) copy-start(bf16[1,1024,256]{2,1,0:T(8,128)(2,1)} %param.11) | copy-start | bytes 1572868
  47.3 22.5 %copy-start.3 = (bf16[512,512]{1,0:T(8,128)(2,1)S(1)}, bf16[512,512]{1,0:T(8,128)(2,1)}, u32[]{:S(2)}) copy-start(bf16[512,512]{1,0:T(8,128)(2,1)} %mlp_ref.3) | copy-start | bytes 1572868
  47.3 22.5 %copy-start.4 = (bf16[512,256]{1,0:T(8,128)(2,1)S(1)}, bf16[512,256]{1,0:T(8,128)(2,1)}, u32[]{:S(2)}) copy-start(bf16[512,256]{1,0:T(8,128)(2,1)} %mlp_out_ref.1) | copy-start | bytes 786436
  47.3 22.5 %copy-start.5 = (bf16[256,256]{1,0:T(8,128)(2,1)S(1)}, bf16[256,256]{1,0:T(8,128)(2,1)}, u32[]{:S(2)}) copy-start(bf16[256,256]{1,0:T(8,128)(2,1)} %out_ref.1) | copy-start | bytes 393220
  60.8 9.0 %collective-permute-start.4 = (bf16[512,256]{1,0:T(8,128)(2,1)S(1)}, bf16[512,256]{1,0:T(8,128)(2,1)S(1)}, u32[]{:S(2)}, u32[]{:S(2)}) collective-permute-start(bf16[512,256]{1,0:T(8,128)(2,1)S(1)} %get-tuple-element.15), channel_id=1, source_target_pairs={{0,1},{1,0},{2,3},{3,2},{4,5},{5,4},{6,7},{7,6},{8,9},{9,8},{10,11... | collective-permute-start | bytes 786440 | tf_op jit(solution)/shard_map/ppermute | solution.py:250
  69.8 0.7 copy-start.7
  69.8 0.7 copy-start.6
  69.8 0.7 copy-start.9

commit v2 on v1

v2 whole, which is shorter than its diff:
```python
import functools
import math

import jax
import jax.numpy as jnp
from jax import lax
from jax.experimental import pallas as pl
from jax.experimental.pallas import tpu as pltpu
from jax.sharding import PartitionSpec as P

HEADS = 4
SPAN = 3
RING = ("img", "pair", "sub")
SCORE_LIMIT = 75.0
VALUE_LIMIT = 256.0
F32 = jnp.float32
BF16 = jnp.bfloat16
VMEM = pl.BlockSpec(memory_space=pltpu.VMEM)
SMEM = pl.BlockSpec(memory_space=pltpu.SMEM)
HBM = pl.BlockSpec(memory_space=pltpu.HBM)


def dot(a, b, contract=(1, 0)):
    return lax.dot_general(
        a, b, (((contract[0],), (contract[1],)), ((), ())), preferred_element_type=F32
    )


def largest_norms(keys, head_width):
    squares = keys.astype(F32)
    squares = (squares * squares * 1.01).astype(BF16)
    width = keys.shape[1]
    head_of = lax.broadcasted_iota(jnp.int32, (width, 128), 0) // head_width
    lane = lax.broadcasted_iota(jnp.int32, (width, 128), 1)
    sums = dot(squares, jnp.where(head_of == lane, 1.0, 0.0).astype(BF16))
    return jnp.max(sums, axis=0, keepdims=True)


def prologue_kernel(
    images, place_ref, links_ref, x_hbm, qk_hbm, value_hbm, qk_other_ref, value_other_ref, mlp_hbm,
    bias_hbm, gain_hbm, shift_hbm, out_bias_hbm, wk_ref, wvt_ref, queries_ref, facts_ref,
    hidden_ref, rows_ref, vectors_ref, x_ref, qk_ref, value_ref, mlp_ref, bias_ref, small_ref, out_bias_ref, sems,
):
    rows, width = x_ref.shape
    head_width = width // HEADS
    local = width // 2
    sub = lax.rem(place_ref[0], 2)
    image = place_ref[0] // 2
    copies = [
        pltpu.make_async_copy(source, target, sems.at[i])
        for i, (source, target) in enumerate(
            [
                (qk_hbm, qk_ref),
                (value_hbm, value_ref),
                (x_hbm, x_ref),
                (mlp_hbm.at[0:width], mlp_ref),
                (bias_hbm, bias_ref),
                (gain_hbm, small_ref.at[0:1]),
                (shift_hbm, small_ref.at[1:2]),
                (out_bias_hbm, out_bias_ref),
            ]
        )
    ]
    for copy in copies:
        copy.start()
    copies[0].wait()
    copies[1].wait()
    values = []
    for own_ref, other_ref in ((qk_ref, qk_other_ref), (value_ref, value_other_ref)):
        own, other = own_ref[...], other_ref[...]
        values.append(jnp.where(sub == 0, own, other))
        values.append(jnp.where(sub == 0, other, own))
    wk_ref[:, :local], wk_ref[:, local:] = values[0], values[1]
    wvt_ref[:local, :], wvt_ref[local:, :] = values[2].T, values[3].T
    for copy in copies[2:]:
        copy.wait()
    keys = dot(x_ref[...], wk_ref[...]).astype(BF16)
    lane = lax.broadcasted_iota(jnp.int32, (rows, 128), 1)
    for head in range(HEADS):
        block, odd = head // 2 * 128, head % 2
        mine = (lane >= 64) if odd else (lane < 64)
        queries_ref[head] = jnp.where(mine, keys[:, block : block + 128], jnp.zeros((), BF16))
    facts_ref[0:1, :] = largest_norms(keys, head_width)
    for step in range(1, SPAN + 1):
        lower = image - sub * step
        inside = jnp.logical_and(lower >= 0, lower + step < images)
        entry = links_ref[step - 1, jnp.clip(lower, 0, images - 1)]
        linked = jnp.where(jnp.logical_and(inside, entry != 0), 1.0, 0.0)
        facts_ref[step : step + 1, :] = jnp.full((1, 128), linked, F32)
    half = rows // 2
    own_rows = x_ref[pl.ds(pl.multiple_of(sub * half, half), half), :]
    rows_ref[...] = own_rows
    hidden_ref[...] = dot(own_rows, mlp_ref[...]) + bias_ref[...]
    vectors_ref[0:2, :] = small_ref[0:2, :]
    vectors_ref[2:3, :width] = out_bias_ref[...]


def partner_kernel(step, two, last, place_ref, queries_ref, facts_ref, x_ref, *refs):
    if two:
        other_ref, *refs = refs
    wk_ref, wvt_ref, *refs = refs
    if last:
        first_ref, second_ref, keep_ref, send_ref, message_ref, keys_ref, values_ref = refs
    else:
        message_ref, keys_ref, values_ref = refs
    rows, width = keys_ref.shape
    head_width = width // HEADS
    scale = 1.0 / math.sqrt(head_width)
    place = place_ref[0]
    sub = lax.rem(place, 2)
    linked = jnp.max(facts_ref[step : step + 1, :]) > 0.0
    tile = 256

    @pl.when(jnp.logical_not(linked))
    def _():
        message_ref[...] = jnp.zeros_like(message_ref)

    @pl.when(linked)
    def _():
        norms = jnp.zeros((1, 128), F32)
        largest = jnp.zeros((width, tile), F32)
        for r in range(0, rows, tile):
            x = x_ref[r : r + tile, :]
            if two:
                x = jnp.where(lax.rem(place // 2, 2) == sub, other_ref[r : r + tile, :], x)
            keys = dot(x, wk_ref[...]).astype(BF16)
            keys_ref[r : r + tile, :] = keys
            norms = jnp.maximum(norms, largest_norms(keys, head_width))
            values = dot(wvt_ref[...], x, (1, 1)).astype(BF16)
            largest = jnp.maximum(largest, jnp.abs(values.astype(F32)))
            for head in range(HEADS):
                values_ref[head, :head_width, r : r + tile] = values[
                    head * head_width : (head + 1) * head_width, :
                ]
                values_ref[head, head_width:, r : r + tile] = jnp.ones((16, tile), BF16)
        bound = jnp.max(norms * facts_ref[0:1, :]) * (scale * scale)
        safe = jnp.logical_and(
            bound <= SCORE_LIMIT * SCORE_LIMIT, jnp.max(largest) <= VALUE_LIMIT
        )

        @pl.when(safe)
        def _():
            wide = rows // 2

            def body(i, carry):
                at = pl.ds(pl.multiple_of(i * wide, wide), wide)
                totals = {}

                def finish(head, r, scores):
                    weights = jnp.exp2(scores * (scale * math.log2(math.e))).astype(BF16)
                    product = dot(values_ref[head, :, r : r + tile], weights)
                    total = product if r == 0 else totals[head] + product
                    totals[head] = total
                    if r + tile == rows:
                        inverse = 1.0 / total[head_width : head_width + 1]
                        message_ref[head * head_width : (head + 1) * head_width, at] = (
                            total[:head_width] * inverse
                        ).astype(BF16)

                waiting = None
                for head in range(HEADS):
                    queries = queries_ref[head, at, :]
                    lanes = slice(head // 2 * 128, head // 2 * 128 + 128)
                    for r in range(0, rows, tile):
                        scores = dot(keys_ref[r : r + tile, lanes], queries, (1, 1))
                        if waiting is not None:
                            finish(*waiting)
                        waiting = (head, r, scores)
                finish(*waiting)
                return carry

            lax.fori_loop(0, rows // wide, body, 0)

        @pl.when(jnp.logical_not(safe))
        def _():
            def body(i, carry):
                head, at = i // (rows // tile), lax.rem(i, rows // tile)
                at = pl.ds(pl.multiple_of(at * tile, tile), tile)
                lanes = pl.ds(pl.multiple_of(head // 2 * 128, 128), 128)
                scores = dot(keys_ref[:, lanes], queries_ref[head, at, :], (1, 1)) * scale
                powers = jnp.exp(scores - jnp.max(scores, axis=0, keepdims=True))
                weights = powers / jnp.sum(powers, axis=0, keepdims=True)
                product = dot(values_ref[head, :head_width, :], weights.astype(BF16))
                into = pl.ds(pl.multiple_of(head * head_width, head_width), head_width)
                message_ref[into, at] = product.astype(BF16)
                return carry

            lax.fori_loop(0, HEADS * (rows // tile), body, 0)

    if last:
        half = rows // 2
        for out_ref, which in ((keep_ref, sub), (send_ref, 1 - sub)):
            at = pl.ds(pl.multiple_of(which * half, half), half)
            total = first_ref[:, at].astype(F32) + second_ref[:, at].astype(F32)
            total = total + message_ref[:, at].astype(F32)
            out_ref[...] = total.astype(out_ref.dtype)


def tail_kernel(
    keep_ref, came_ref, hidden_ref, rows_ref, out_ref, mlp_ref, vectors_ref, mlp_out_ref, result_ref
):
    width = keep_ref.shape[0]
    summed = (keep_ref[...] + came_ref[...].astype(F32)).astype(BF16)
    projected = dot(summed, out_ref[...], (0, 0)).astype(BF16)
    hidden = hidden_ref[...] + dot(projected, mlp_ref[width:, :])
    centered = hidden - jnp.mean(hidden, axis=1, keepdims=True)
    variance = jnp.mean(centered * centered, axis=1, keepdims=True)
    normed = centered * lax.rsqrt(variance + 1e-05) * vectors_ref[0:1, :] + vectors_ref[1:2, :]
    activated = (0.5 * normed * (1.0 + lax.erf(normed * math.sqrt(0.5)))).astype(BF16)
    updated = dot(activated, mlp_out_ref[...]) + vectors_ref[2:3, :width]
    result_ref[...] = (updated + rows_ref[...].astype(F32)).astype(BF16)


def shape(dims, dtype):
    return jax.ShapeDtypeStruct(dims, dtype)


def cost(flops, moved, exps=0):
    return pl.CostEstimate(flops=flops, bytes_accessed=moved, transcendentals=exps)


def on_device(
    descriptors,
    links,
    qk_weight,
    value_weight,
    out_weight,
    mlp_in,
    mlp_in_bias,
    norm_gain,
    norm_bias,
    mlp_out,
    mlp_out_bias,
):
    own = descriptors[0]
    rows, width = own.shape
    hidden_width = mlp_in.shape[1]
    half = rows // 2
    images = lax.axis_size(("img", "pair"))
    place = lax.axis_index(RING).reshape(1)
    params = pltpu.CompilerParams(vmem_limit_bytes=40 << 20)

    swap = [(0, 1), (1, 0)]
    qk_other = lax.ppermute(qk_weight, "sub", swap)
    value_other = lax.ppermute(value_weight, "sub", swap)

    def carried(value, moves):
        pairs = []
        for image in range(images):
            for sub in range(2):
                source = moves(image, sub)
                if source is not None:
                    pairs.append((2 * source[0] + source[1], 2 * image + sub))
        return lax.ppermute(value, RING, pairs)

    def ahead(image, sub, step):
        partner = image + step if sub == 0 else image - step
        return partner if 0 <= partner < images else None

    def by_two(image, sub):
        partner = ahead(image, sub, 2)
        return None if partner is None else (partner, sub)

    def within(image, sub):
        return (image ^ 1, image % 2) if image % 2 == sub else None

    def across(image, sub):
        partner = ahead(image, sub, 1)
        return None if image % 2 == sub or partner is None else (image ^ 1, sub)

    def onward(image, sub):
        return None if ahead(image, sub, 3) is None else (ahead(image, sub, 2), sub)

    def onward_inner(image, sub):
        return onward(image, sub) if image % 2 == sub else None

    def onward_outer(image, sub):
        return None if image % 2 == sub else onward(image, sub)

    two = carried(own, by_two)
    inner = carried(own, within)

    wk, wvt, queries, facts, hidden, own_half, vectors = pl.pallas_call(
        functools.partial(prologue_kernel, images),
        in_specs=[SMEM, SMEM] + [HBM] * 3 + [VMEM] * 2 + [HBM] * 5,
        out_specs=[VMEM] * 7,
        out_shape=[
            shape((width, width), BF16),
            shape((width, width), BF16),
            shape((HEADS, rows, 128), BF16),
            shape((8, 128), F32),
            shape((half, hidden_width), F32),
            shape((half, width), BF16),
            shape((8, hidden_width), F32),
        ],
        scratch_shapes=[
            pltpu.VMEM((rows, width), BF16),
            pltpu.VMEM(qk_weight.shape, BF16),
            pltpu.VMEM(qk_weight.shape, BF16),
            pltpu.VMEM((width, hidden_width), BF16),
            pltpu.VMEM((1, hidden_width), F32),
            pltpu.VMEM((8, hidden_width), F32),
            pltpu.VMEM((1, width), F32),
            pltpu.SemaphoreType.DMA((8,)),
        ],
        compiler_params=params,
        cost_estimate=cost(4 * rows * width * width, 4 << 20),
        name="prologue",
    )(
        place, links.T, own, qk_weight, value_weight, qk_other, value_other, mlp_in,
        mlp_in_bias.reshape(1, -1), norm_gain.reshape(1, -1), norm_bias.reshape(1, -1),
        mlp_out_bias.reshape(1, -1),
    )

    def attended(step, partner, before):
        last = step == SPAN
        out_shape = [shape((width, rows), BF16)]
        scratch = [pltpu.VMEM((rows, width), BF16)]
        scratch += [pltpu.VMEM((HEADS, width // HEADS + 16, rows), BF16)]
        if last:
            out_shape = [shape((width, half), F32), shape((width, half), BF16)]
            scratch = [pltpu.VMEM((width, rows), BF16)] + scratch
        args = [place, queries, facts, *partner, wk, wvt, *before]
        return pl.pallas_call(
            functools.partial(partner_kernel, step, len(partner) == 2, last),
            in_specs=[SMEM] + [VMEM] * (len(args) - 1),
            out_specs=[VMEM] * len(out_shape),
            out_shape=out_shape,
            scratch_shapes=scratch,
            compiler_params=params,
            cost_estimate=cost(8 * rows * rows * width, 2 << 20, HEADS * rows * rows),
            name=f"partner_{step}",
        )(*args)

    two, inner, facts = lax.optimization_barrier((two, inner, facts))
    outer = carried(two, across)
    inner_far = carried(inner, onward_inner)
    (message_two,) = attended(2, [two], [])
    outer, message_two = lax.optimization_barrier((outer, message_two))
    outer_far = carried(outer, onward_outer)
    (message_one,) = attended(1, [outer, inner], [])
    inner_far, outer_far, message_one = lax.optimization_barrier(
        (inner_far, outer_far, message_one)
    )
    keep, send = attended(3, [outer_far, inner_far], [message_two, message_one])
    came = lax.ppermute(send, "sub", swap)

    result = pl.pallas_call(
        tail_kernel,
        in_specs=[VMEM] * 8,
        out_specs=VMEM,
        out_shape=shape((half, width), BF16),
        compiler_params=params,
        cost_estimate=cost(4 * rows * width * width, 4 << 20),
        name="tail",
    )(keep, came, hidden, own_half, out_weight, mlp_in, vectors, mlp_out)
    return result[None]


def solution(mesh):
    placed = (
        P(("groups", "img", "pair"), None, None),
        P("groups", None),
        P(None, "sub"),
        P(None, "sub"),
        P(),
        P(),
        P(),
        P(),
        P(),
        P(),
        P(),
    )
    return jax.shard_map(
        on_device,
        mesh=mesh,
        in_specs=placed,
        out_specs=P(("groups", "img", "pair"), "sub", None),
        check_vma=False,
    )
```

time: 72.7 us -> 70.6 us (0.971)
  the two profiles are of different devices: /device:TPU:17 before, /device:TPU:21 now
where the time goes in v2:
time: 70.6 us; the launch traced here: 70.2 us
  Pallas kernels  34.5 us (49%)
  starting transfers between devices  20.7 us (29%)
  waiting for transfers between devices  10.3 us (15%)
  local copies, waits for them, and re-layouts  4.51 us (6%)
    pallas_call x3, Pallas kernels, attended(): pl.pallas_call(functools.partial(partner_kernel, step, len(partner) == 2,...  31 us
    ppermute x5, starting transfers between devices, carried(): return lax.ppermute(value, RING, pairs)  17.6 us
    ppermute x5, waiting for transfers between devices, carried(): return lax.ppermute(value, RING, pairs)  8.06 us
    unnamed x24, local copies, waits for them, and re-layouts  4.51 us
    ppermute x1, starting transfers between devices, on_device(): came = lax.ppermute(send, 'sub', swap)  2.5 us
    pallas_call x1, Pallas kernels, on_device(): pl.pallas_call(tail_kernel, in_specs=[VMEM] * 8, out_specs=VMEM, out_shap...  1.82 us
    pallas_call x1, Pallas kernels, on_device(): pl.pallas_call(functools.partial(prologue_kernel, images), in_specs=[SMEM...  1.69 us
  transfers between devices with their start and end apart: 8, of which 4 were waited for; matrix products, arithmetic and copies ran while one was open for 0% of the time, Pallas kernels for 24%

profile of v2, /device:TPU:21, one launch (start us, length us, event | category | flops | bytes accessed | tf_op | source)
XLA Modules:
  0.0 70.2 jit_solution(7018535057197720841)
XLA Ops:
  0.0 3.1 %collective-permute-start.3 = (bf16[1024,256]{1,0:T(8,128)(2,1)}, bf16[1024,256]{1,0:T(8,128)(2,1)S(1)}, u32[]{:S(2)}, u32[]{:S(2)}) collective-permute-start(bf16[1024,256]{1,0:T(8,128)(2,1)} %bitcast.8), channel_id=1, source_target_pairs={{2,0},{1,3},{6,4},{5,7},{10,8},{9,11},{14,12},{13,15},{18,16},{17,... | collective-permute-start | bytes 1572872 | tf_op jit(solution)/shard_map/ppermute | solution.py:254
  3.1 3.2 %collective-permute-start.2 = (bf16[1024,256]{1,0:T(8,128)(2,1)}, bf16[1024,256]{1,0:T(8,128)(2,1)S(1)}, u32[]{:S(2)}, u32[]{:S(2)}) collective-permute-start(bf16[1024,256]{1,0:T(8,128)(2,1)} %bitcast.9), channel_id=1, source_target_pairs={{4,0},{6,2},{8,4},{1,5},{10,6},{3,7},{12,8},{5,9},{14,10},{7,11},{... | collective-permute-start | bytes 1572872 | tf_op jit(solution)/shard_map/ppermute | solution.py:254
  6.4 0.1 collective-permute-start
  6.4 0.5 collective-permute-start.1
  6.9 1.0 %collective-permute-done.qk_other_ref = bf16[256,128]{1,0:T(8,128)(2,1)S(1)} collective-permute-done((bf16[256,128]{1,0:T(8,128)(2,1)}, bf16[256,128]{1,0:T(8,128)(2,1)S(1)}, u32[]{:S(2)}, u32[]{:S(2)}) %collective-permute-start) | collective-permute-done | bytes 65568 | tf_op jit(solution)/shard_map/ppermute | solution.py:244
  7.9 0.2 collective-permute-done.1.value_other_ref
  8.0 0.0 copy-start.10
  8.0 0.0 copy-start.9
  8.0 0.0 copy-start.8
  8.1 0.0 copy-start.7
  8.1 0.0 copy-start.11
  8.1 0.7 copy-done.10
  8.7 0.0 copy-done.9
  8.7 0.0 copy-done.8
  8.8 0.0 copy-done.7
  8.8 0.0 copy-done.11
  8.8 0.0 copy-start
  8.8 1.0 %copy-done = bf16[512,512]{1,0:T(8,128)(2,1)S(1)} copy-done((bf16[512,512]{1,0:T(8,128)(2,1)S(1)}, bf16[512,512]{1,0:T(8,128)(2,1)}, u32[]{:S(2)}) %copy-start) | copy-done | bytes 524312
  9.8 0.0 copy-start.2
  9.8 1.0 %copy-done.2 = bf16[1,1024,256]{2,1,0:T(8,128)(2,1)S(1)} copy-done((bf16[1,1024,256]{2,1,0:T(8,128)(2,1)S(1)}, bf16[1,1024,256]{2,1,0:T(8,128)(2,1)}, u32[]{:S(2)}) %copy-start.2) | copy-done | bytes 524312
  10.9 0.0 copy-start.5
  10.9 0.8 %copy-done.5 = bf16[256,128]{1,0:T(8,128)(2,1)S(1)} copy-done((bf16[256,128]{1,0:T(8,128)(2,1)S(1)}, bf16[256,128]{1,0:T(8,128)(2,1)}, u32[]{:S(2)}) %copy-start.5) | copy-done | bytes 65560
  11.7 0.0 copy-start.6
  11.7 0.8 %copy-done.6 = bf16[256,128]{1,0:T(8,128)(2,1)S(1)} copy-done((bf16[256,128]{1,0:T(8,128)(2,1)S(1)}, bf16[256,128]{1,0:T(8,128)(2,1)}, u32[]{:S(2)}) %copy-start.6) | copy-done | bytes 65560
  12.6 1.7 %prologue.1 = (bf16[256,256]{1,0:T(8,128)(2,1)S(1)}, bf16[256,256]{1,0:T(8,128)(2,1)S(1)}, bf16[4,1024,128]{2,1,0:T(8,128)(2,1)S(1)}, f32[8,128]{1,0:T(8,128)S(1...) custom-call(s32[1]{0:T(128)} %bitcast.place_ref, s32[3,8]{1,0:T(4,128)S(1)} %bitcast.11, ...), custom_call_target="tpu_custom_call" | custom-call | flops 268435456 | bytes 4194304 | tf_op jit(solution)/shard_map/prologue/pallas_call | solution.py:283
  14.2 0.0 collective-permute-done.3.refs_0_
  14.3 0.0 collective-permute-done.2.x_ref
  14.3 1.3 %collective-permute-start.5 = (bf16[1024,256]{1,0:T(8,128)(2,1)S(1)}, bf16[1024,256]{1,0:T(8,128)(2,1)S(1)}, u32[]{:S(2)}, u32[]{:S(2)}) collective-permute-start(bf16[1024,256]{1,0:T(8,128)(2,1)S(1)} %collective-permute-done.2.x_ref), channel_id=1, source_target_pairs={{0,2},{7,5},{4,6},{11,9},{8,10},{15,13},{16,18},{23,21},{20,22},{2... | collective-permute-start | bytes 1572872 | tf_op jit(solution)/shard_map/ppermute | solution.py:254
  15.6 0.7 collective-permute-start.4
  16.3 0.2 partner_2.1.refs_3_
  16.4 8.1 %collective-permute-done.5.x_ref = bf16[1024,256]{1,0:T(8,128)(2,1)S(1)} collective-permute-done((bf16[1024,256]{1,0:T(8,128)(2,1)S(1)}, bf16[1024,256]{1,0:T(8,128)(2,1)S(1)}, u32[]{:S(2)}, u32[]{:S(2)}) %collective-permute-start.5) | collective-permute-done | bytes 524320 | tf_op jit(solution)/shard_map/ppermute | solution.py:254
  24.5 9.3 %collective-permute-start.6 = (bf16[1024,256]{1,0:T(8,128)(2,1)S(1)}, bf16[1024,256]{1,0:T(8,128)(2,1)S(1)}, u32[]{:S(2)}, u32[]{:S(2)}) collective-permute-start(bf16[1024,256]{1,0:T(8,128)(2,1)S(1)} %collective-permute-done.5.x_ref), channel_id=1, source_target_pairs={{6,2},{10,6},{5,9},{9,13},{22,18},{26,22},{21,25},{25,29}} | collective-permute-start | bytes 1572872 | tf_op jit(solution)/shard_map/ppermute | solution.py:254
  33.8 15.3 %partner_1.1.refs_4_ = bf16[256,1024]{1,0:T(8,128)(2,1)S(1)} custom-call(s32[1]{0:T(128)} %bitcast.place_ref, bf16[4,1024,128]{2,1,0:T(8,128)(2,1)S(1)} %get-tuple-element.22.queries_ref, f32[8,128]{1,0:T(8,128)S(1)} %get-tuple-element.24.facts_ref, bf16[1024,256]{1,0:T(8,128)(2,1)S(1)} %collective-permute-done.5.x_ref, ...), custom_call_target="tpu_custom_call" | custom-call | flops 2147483648 | bytes 2097152 | tf_op jit(solution)/shard_map/partner_1/pallas_call | solution.py:324
  49.1 0.0 copy-start.1
  49.1 0.0 copy-start.3
  49.2 0.0 copy-start.4
  49.2 0.0 collective-permute-done.4.refs_0_
  49.2 0.0 collective-permute-done.6.x_ref
  49.2 15.5 %partner_3.1 = (f32[256,512]{1,0:T(8,128)S(1)}, bf16[256,512]{1,0:T(8,128)(2,1)S(1)}) custom-call(s32[1]{0:T(128)} %bitcast.place_ref, bf16[4,1024,128]{2,1,0:T(8,128)(2,1)S(1)} %get-tuple-element.22.queries_ref, f32[8,128]{1,0:T(8,128)S(1)} %get-tuple-element.24.facts_ref, bf16[1024,256]{1,0:T(8,128)(2,1)S(1)} %collective-permute-done.6.x_ref, ...), custom_call_target="tpu_custom_call" | custom-call | flops 2147483648 | bytes 2097152 | tf_op jit(solution)/shard_map/partner_3/pallas_call | solution.py:324
  64.7 2.5 %collective-permute-start.7 = (bf16[256,512]{1,0:T(8,128)(2,1)S(1)}, bf16[256,512]{1,0:T(8,128)(2,1)S(1)}, u32[]{:S(2)}, u32[]{:S(2)}) collective-permute-start(bf16[256,512]{1,0:T(8,128)(2,1)S(1)} %get-tuple-element.35), channel_id=1, source_target_pairs={{0,1},{1,0},{2,3},{3,2},{4,5},{5,4},{6,7},{7,6},{8,9},{9,8},{10,11... | collective-permute-start | bytes 786440 | tf_op jit(solution)/shard_map/ppermute | solution.py:346
  67.2 1.2 %collective-permute-done.7.came_ref = bf16[256,512]{1,0:T(8,128)(2,1)S(1)} collective-permute-done((bf16[256,512]{1,0:T(8,128)(2,1)S(1)}, bf16[256,512]{1,0:T(8,128)(2,1)S(1)}, u32[]{:S(2)}, u32[]{:S(2)}) %collective-permute-start.7) | collective-permute-done | bytes 262176 | tf_op jit(solution)/shard_map/ppermute | solution.py:346
  68.4 0.0 copy-done.1
  68.4 0.0 copy-done.3
  68.4 0.0 copy-done.4
  68.4 1.8 %tail.1 = bf16[512,256]{1,0:T(8,128)(2,1)} custom-call(f32[256,512]{1,0:T(8,128)S(1)} %get-tuple-element.34.keep_ref, bf16[256,512]{1,0:T(8,128)(2,1)S(1)} %collective-permute-done.7.came_ref, f32[512,512]{1,0:T(8,128)S(1)} %get-tuple-element.36.hidden_ref, bf16[512,256]{1,0:T(8,128)(2,1)S(1)} %get-tuple-element.37.rows_ref, bf16[256,256]{1,0:T(8,128)(2,1)S(1)} %copy-done.4, ...), custom_call_target="tpu_custom_call" | custom-call | flops 268435456 | bytes 4194304 | tf_op jit(solution)/shard_map/tail/pallas_call | solution.py:348
Async XLA Ops:
  0.0 14.2 %collective-permute-start.3 = (bf16[1024,256]{1,0:T(8,128)(2,1)}, bf16[1024,256]{1,0:T(8,128)(2,1)S(1)}, u32[]{:S(2)}, u32[]{:S(2)}) collective-permute-start(bf16[1024,256]{1,0:T(8,128)(2,1)} %bitcast.8), channel_id=1, source_target_pairs={{2,0},{1,3},{6,4},{5,7},{10,8},{9,11},{14,12},{13,15},{18,16},{17,... | collective-permute-start | bytes 1572872 | tf_op jit(solution)/shard_map/ppermute | solution.py:254
  3.1 11.1 %collective-permute-start.2 = (bf16[1024,256]{1,0:T(8,128)(2,1)}, bf16[1024,256]{1,0:T(8,128)(2,1)S(1)}, u32[]{:S(2)}, u32[]{:S(2)}) collective-permute-start(bf16[1024,256]{1,0:T(8,128)(2,1)} %bitcast.9), channel_id=1, source_target_pairs={{4,0},{6,2},{8,4},{1,5},{10,6},{3,7},{12,8},{5,9},{14,10},{7,11},{... | collective-permute-start | bytes 1572872 | tf_op jit(solution)/shard_map/ppermute | solution.py:254
  6.4 1.5 %collective-permute-start = (bf16[256,128]{1,0:T(8,128)(2,1)}, bf16[256,128]{1,0:T(8,128)(2,1)S(1)}, u32[]{:S(2)}, u32[]{:S(2)}) collective-permute-start(bf16[256,128]{1,0:T(8,128)(2,1)} %qk_hbm.1), channel_id=1, source_target_pairs={{0,1},{1,0},{2,3},{3,2},{4,5},{5,4},{6,7},{7,6},{8,9},{9,8},{10,11... | collective-permute-start | bytes 196616 | tf_op jit(solution)/shard_map/ppermute | solution.py:244
  6.4 1.6 %collective-permute-start.1 = (bf16[256,128]{1,0:T(8,128)(2,1)}, bf16[256,128]{1,0:T(8,128)(2,1)S(1)}, u32[]{:S(2)}, u32[]{:S(2)}) collective-permute-start(bf16[256,128]{1,0:T(8,128)(2,1)} %value_hbm.1), channel_id=1, source_target_pairs={{0,1},{1,0},{2,3},{3,2},{4,5},{5,4},{6,7},{7,6},{8,9},{9,8},{10,11... | collective-permute-start | bytes 196616 | tf_op jit(solution)/shard_map/ppermute | solution.py:245
  8.0 0.7 copy-start.10
  8.0 0.7 copy-start.9
  8.0 0.7 %copy-start.8 = (f32[512]{0:T(512)S(1)}, f32[512]{0:T(512)}, u32[]{:S(2)}) copy-start(f32[512]{0:T(512)} %param.17) | copy-start | bytes 6148
  8.1 0.7 %copy-start.7 = (s32[8,3]{0,1:T(4,128)S(1)}, s32[8,3]{0,1:T(4,128)}, u32[]{:S(2)}) copy-start(s32[8,3]{0,1:T(4,128)} %param.12) | copy-start | bytes 292
  8.1 0.7 %copy-start.11 = (f32[256]{0:T(256)S(1)}, f32[256]{0:T(256)}, u32[]{:S(2)}) copy-start(f32[256]{0:T(256)} %param.21) | copy-start | bytes 3076
  8.8 1.0 %copy-start = (bf16[512,512]{1,0:T(8,128)(2,1)S(1)}, bf16[512,512]{1,0:T(8,128)(2,1)}, u32[]{:S(2)}) copy-start(bf16[512,512]{1,0:T(8,128)(2,1)} %mlp_ref.1) | copy-start | bytes 1572868
  9.8 1.0 %copy-start.2 = (bf16[1,1024,256]{2,1,0:T(8,128)(2,1)S(1)}, bf16[1,1024,256]{2,1,0:T(8,128)(2,1)}, u32[]{:S(2)}) copy-start(bf16[1,1024,256]{2,1,0:T(8,128)(2,1)} %param.11) | copy-start | bytes 1572868
  10.9 0.8 %copy-start.5 = (bf16[256,128]{1,0:T(8,128)(2,1)S(1)}, bf16[256,128]{1,0:T(8,128)(2,1)}, u32[]{:S(2)}) copy-start(bf16[256,128]{1,0:T(8,128)(2,1)} %qk_hbm.1) | copy-start | bytes 196612
  11.7 0.8 %copy-start.6 = (bf16[256,128]{1,0:T(8,128)(2,1)S(1)}, bf16[256,128]{1,0:T(8,128)(2,1)}, u32[]{:S(2)}) copy-start(bf16[256,128]{1,0:T(8,128)(2,1)} %value_hbm.1) | copy-start | bytes 196612
  14.3 10.2 %collective-permute-start.5 = (bf16[1024,256]{1,0:T(8,128)(2,1)S(1)}, bf16[1024,256]{1,0:T(8,128)(2,1)S(1)}, u32[]{:S(2)}, u32[]{:S(2)}) collective-permute-start(bf16[1024,256]{1,0:T(8,128)(2,1)S(1)} %collective-permute-done.2.x_ref), channel_id=1, source_target_pairs={{0,2},{7,5},{4,6},{11,9},{8,10},{15,13},{16,18},{23,21},{20,22},{2... | collective-permute-start | bytes 1572872 | tf_op jit(solution)/shard_map/ppermute | solution.py:254
  15.6 33.6 %collective-permute-start.4 = (bf16[1024,256]{1,0:T(8,128)(2,1)S(1)}, bf16[1024,256]{1,0:T(8,128)(2,1)S(1)}, u32[]{:S(2)}, u32[]{:S(2)}) collective-permute-start(bf16[1024,256]{1,0:T(8,128)(2,1)S(1)} %collective-permute-done.3.refs_0_), channel_id=1, source_target_pairs={{4,0},{8,4},{3,7},{12,8},{7,11},{11,15},{20,16},{24,20},{19,23},{2... | collective-permute-start | bytes 1572872 | tf_op jit(solution)/shard_map/ppermute | solution.py:254
  24.5 24.7 %collective-permute-start.6 = (bf16[1024,256]{1,0:T(8,128)(2,1)S(1)}, bf16[1024,256]{1,0:T(8,128)(2,1)S(1)}, u32[]{:S(2)}, u32[]{:S(2)}) collective-permute-start(bf16[1024,256]{1,0:T(8,128)(2,1)S(1)} %collective-permute-done.5.x_ref), channel_id=1, source_target_pairs={{6,2},{10,6},{5,9},{9,13},{22,18},{26,22},{21,25},{25,29}} | collective-permute-start | bytes 1572872 | tf_op jit(solution)/shard_map/ppermute | solution.py:254
  49.1 19.2 %copy-start.1 = (bf16[512,512]{1,0:T(8,128)(2,1)S(1)}, bf16[512,512]{1,0:T(8,128)(2,1)}, u32[]{:S(2)}) copy-start(bf16[512,512]{1,0:T(8,128)(2,1)} %mlp_ref.1) | copy-start | bytes 1572868
  49.1 19.2 %copy-start.3 = (bf16[512,256]{1,0:T(8,128)(2,1)S(1)}, bf16[512,256]{1,0:T(8,128)(2,1)}, u32[]{:S(2)}) copy-start(bf16[512,256]{1,0:T(8,128)(2,1)} %mlp_out_ref.1) | copy-start | bytes 786436
  49.2 19.2 %copy-start.4 = (bf16[256,256]{1,0:T(8,128)(2,1)S(1)}, bf16[256,256]{1,0:T(8,128)(2,1)}, u32[]{:S(2)}) copy-start(bf16[256,256]{1,0:T(8,128)(2,1)} %out_ref.1) | copy-start | bytes 393220
  64.7 3.7 %collective-permute-start.7 = (bf16[256,512]{1,0:T(8,128)(2,1)S(1)}, bf16[256,512]{1,0:T(8,128)(2,1)S(1)}, u32[]{:S(2)}, u32[]{:S(2)}) collective-permute-start(bf16[256,512]{1,0:T(8,128)(2,1)S(1)} %get-tuple-element.35), channel_id=1, source_target_pairs={{0,1},{1,0},{2,3},{3,2},{4,5},{5,4},{6,7},{7,6},{8,9},{9,8},{10,11... | collective-permute-start | bytes 786440 | tf_op jit(solution)/shard_map/ppermute | solution.py:346

commit v3 on v0

v3 whole, which is shorter than its diff:
```python
import functools
import math

import jax
import jax.numpy as jnp
from jax import lax
from jax.experimental import pallas as pl
from jax.experimental.pallas import tpu as pltpu
from jax.sharding import PartitionSpec as P


HEADS = 4
SPAN = 3
RING = ("img", "pair", "sub")
LEAST_SUM, LARGEST_SUM = 1e-20, 1e20
LARGEST_PRODUCT = 1e37
F32 = jnp.float32
BF16 = jnp.bfloat16
VMEM = pl.BlockSpec(memory_space=pltpu.VMEM)
SMEM = pl.BlockSpec(memory_space=pltpu.SMEM)


def dot(a, b, contract=(1, 0)):
    return lax.dot_general(
        a, b, (((contract[0],), (contract[1],)), ((), ())), preferred_element_type=F32
    )


def prologue_kernel(
    images, place_ref, links_ref, x_ref, qk_ref, value_ref, qk_other_ref, value_other_ref, gain_ref,
    shift_ref, bias_ref, out_bias_ref, wk_ref, wvt_ref, queries_ref, facts_ref, vectors_ref,
):
    rows, width = x_ref.shape
    local = width // 2
    sub = lax.rem(place_ref[0], 2)
    image = place_ref[0] // 2
    parts = []
    for own_ref, other_ref in ((qk_ref, qk_other_ref), (value_ref, value_other_ref)):
        own, other = own_ref[...], other_ref[...]
        parts.append(jnp.where(sub == 0, own, other))
        parts.append(jnp.where(sub == 0, other, own))
    wk_ref[:, :local], wk_ref[:, local:] = parts[0], parts[1]
    wvt_ref[:local, :], wvt_ref[local:, :] = parts[2].T, parts[3].T
    keys = dot(x_ref[...], wk_ref[...]).astype(BF16)
    lane = lax.broadcasted_iota(jnp.int32, (rows, 128), 1)
    for head in range(HEADS):
        block, odd = head // 2 * 128, head % 2
        mine = (lane >= 64) if odd else (lane < 64)
        queries_ref[head] = jnp.where(mine, keys[:, block : block + 128], jnp.zeros((), BF16))
    for step in range(1, SPAN + 1):
        lower = image - sub * step
        inside = jnp.logical_and(lower >= 0, lower + step < images)
        entry = links_ref[step - 1, jnp.clip(lower, 0, images - 1)]
        linked = jnp.where(jnp.logical_and(inside, entry != 0), 1.0, 0.0)
        facts_ref[step : step + 1, :] = jnp.full((1, 128), linked, F32)
    vectors_ref[0:1, :] = gain_ref[...]
    vectors_ref[1:2, :] = shift_ref[...]
    vectors_ref[2:3, :] = bias_ref[...]
    vectors_ref[3:4, :width] = out_bias_ref[...]


def project(x_ref, other_ref, take_other, wk_ref, wvt_ref, keys_ref, values_ref):
    rows, width = keys_ref.shape
    head_width = width // HEADS
    tile = 256
    for r in range(0, rows, tile):
        x = x_ref[r : r + tile, :]
        if other_ref is not None:
            x = jnp.where(take_other, other_ref[r : r + tile, :], x)
        keys_ref[r : r + tile, :] = dot(x, wk_ref[...]).astype(BF16)
        values = dot(wvt_ref[...], x, (1, 1)).astype(BF16)
        for head in range(HEADS):
            values_ref[head, :head_width, r : r + tile] = values[
                head * head_width : (head + 1) * head_width, :
            ]
            values_ref[head, head_width:, r : r + tile] = jnp.ones((16, tile), BF16)


def attend(queries_ref, at, span, keys_ref, values_ref, message_ref, into):
    rows, width = keys_ref.shape
    head_width = width // HEADS
    scale = 1.0 / math.sqrt(head_width)
    tile = 256
    queries_at = pl.ds(pl.multiple_of(at, span), span)
    totals = {}
    wrong = []

    def finish(head, r, scores):
        weights = jnp.exp2(scores * (scale * math.log2(math.e))).astype(BF16)
        product = dot(values_ref[head, :, r : r + tile], weights)
        total = product if r == 0 else totals[head] + product
        totals[head] = total
        if r + tile == rows:
            sums = total[head_width : head_width + 1]
            message_ref[head * head_width : (head + 1) * head_width, into] = (
                total[:head_width] * (1.0 / sums)
            ).astype(BF16)
            top = jnp.max(jnp.abs(total[:head_width]), axis=0, keepdims=True)
            fine = jnp.logical_and(sums > LEAST_SUM, sums < LARGEST_SUM)
            fine = jnp.logical_and(fine, top < LARGEST_PRODUCT)
            wrong.append(jnp.where(fine, 0.0, 1.0))

    waiting = []
    for head in range(HEADS):
        queries = queries_ref[head, queries_at, :]
        lanes = slice(head // 2 * 128, head // 2 * 128 + 128)
        for r in range(0, rows, tile):
            waiting.append((head, r, dot(keys_ref[r : r + tile, lanes], queries, (1, 1))))
            if len(waiting) > 2:
                finish(*waiting.pop(0))
    for item in waiting:
        finish(*item)

    @pl.when(jnp.max(sum(wrong)) > 0.0)
    def _():
        def body(i, carry):
            head, part = i // (span // tile), lax.rem(i, span // tile)
            part_at = pl.ds(pl.multiple_of(at + part * tile, tile), tile)
            lanes = pl.ds(pl.multiple_of(head // 2 * 128, 128), 128)
            scores = dot(keys_ref[:, lanes], queries_ref[head, part_at, :], (1, 1)) * scale
            powers = jnp.exp(scores - jnp.max(scores, axis=0, keepdims=True))
            weights = powers / jnp.sum(powers, axis=0, keepdims=True)
            product = dot(values_ref[head, :head_width, :], weights.astype(BF16))
            head_rows = pl.ds(pl.multiple_of(head * head_width, head_width), head_width)
            columns = pl.ds(pl.multiple_of(into.start + part * tile, tile), tile)
            message_ref[head_rows, columns] = product.astype(BF16)
            return carry

        lax.fori_loop(0, HEADS * (span // tile), body, 0)


def takes_other(place):
    return lax.rem(place // 2, 2) == lax.rem(place, 2)


def partner_kernel(step, two, place_ref, queries_ref, facts_ref, x_ref, *refs):
    other_ref, *refs = refs if two else (None, *refs)
    wk_ref, wvt_ref, message_ref, keys_ref, values_ref = refs
    rows, _ = keys_ref.shape
    linked = jnp.max(facts_ref[step : step + 1, :]) > 0.0

    @pl.when(jnp.logical_not(linked))
    def _():
        message_ref[...] = jnp.zeros_like(message_ref)

    @pl.when(linked)
    def _():
        take = takes_other(place_ref[0])
        project(x_ref, other_ref, take, wk_ref, wvt_ref, keys_ref, values_ref)
        wide = rows // 2

        def body(i, carry):
            at = pl.multiple_of(i * wide, wide)
            attend(queries_ref, at, wide, keys_ref, values_ref, message_ref, pl.ds(at, wide))
            return carry

        lax.fori_loop(0, rows // wide, body, 0)


def last_kernel(
    step, place_ref, queries_ref, facts_ref, x_ref, other_ref, wk_ref, wvt_ref, first_ref,
    second_ref, keys_ref, values_ref, send_ref, message_ref,
):
    half = message_ref.shape[1]
    place = place_ref[0]
    at = pl.multiple_of((1 - lax.rem(place, 2)) * half, half)
    here = pl.ds(at, half)
    linked = jnp.max(facts_ref[step : step + 1, :]) > 0.0
    total = first_ref[:, here].astype(F32) + second_ref[:, here].astype(F32)

    @pl.when(jnp.logical_not(linked))
    def _():
        send_ref[...] = total.astype(BF16)

    @pl.when(linked)
    def _():
        project(x_ref, other_ref, takes_other(place), wk_ref, wvt_ref, keys_ref, values_ref)
        attend(queries_ref, at, half, keys_ref, values_ref, message_ref, pl.ds(0, half))
        total = first_ref[:, here].astype(F32) + second_ref[:, here].astype(F32)
        send_ref[...] = (total + message_ref[...].astype(F32)).astype(BF16)


def own_kernel(
    step, place_ref, queries_ref, facts_ref, keys_ref, values_ref, first_ref, second_ref, keep_ref,
    message_ref,
):
    half = message_ref.shape[1]
    at = pl.multiple_of(lax.rem(place_ref[0], 2) * half, half)
    here = pl.ds(at, half)
    linked = jnp.max(facts_ref[step : step + 1, :]) > 0.0

    @pl.when(jnp.logical_not(linked))
    def _():
        keep_ref[...] = first_ref[:, here].astype(F32) + second_ref[:, here].astype(F32)

    @pl.when(linked)
    def _():
        attend(queries_ref, at, half, keys_ref, values_ref, message_ref, pl.ds(0, half))
        total = first_ref[:, here].astype(F32) + second_ref[:, here].astype(F32)
        keep_ref[...] = total + message_ref[...].astype(F32)


def tail_kernel(
    place_ref, keep_ref, came_ref, x_ref, out_ref, mlp_ref, vectors_ref, mlp_out_ref, result_ref
):
    width, rows = keep_ref.shape
    sub = lax.rem(place_ref[0], 2)
    own_rows = x_ref[pl.ds(pl.multiple_of(sub * rows, rows), rows), :]
    hidden = dot(own_rows, mlp_ref[:width, :]) + vectors_ref[2:3, :]
    summed = (keep_ref[...] + came_ref[...].astype(F32)).astype(BF16)
    projected = dot(summed, out_ref[...], (0, 0)).astype(BF16)
    hidden = hidden + dot(projected, mlp_ref[width:, :])
    centered = hidden - jnp.mean(hidden, axis=1, keepdims=True)
    variance = jnp.mean(centered * centered, axis=1, keepdims=True)
    normed = centered * lax.rsqrt(variance + 1e-05) * vectors_ref[0:1, :] + vectors_ref[1:2, :]
    activated = (0.5 * normed * (1.0 + lax.erf(normed * math.sqrt(0.5)))).astype(BF16)
    updated = dot(activated, mlp_out_ref[...]) + vectors_ref[3:4, :width]
    result_ref[...] = (updated + own_rows.astype(F32)).astype(BF16)


def shape(dims, dtype):
    return jax.ShapeDtypeStruct(dims, dtype)


def cost(flops, moved, exps=0):
    return pl.CostEstimate(flops=flops, bytes_accessed=moved, transcendentals=exps)


def on_device(
    descriptors,
    links,
    qk_weight,
    value_weight,
    out_weight,
    mlp_in,
    mlp_in_bias,
    norm_gain,
    norm_bias,
    mlp_out,
    mlp_out_bias,
):
    own = descriptors[0]
    rows, width = own.shape
    hidden_width = mlp_in.shape[1]
    half = rows // 2
    images = lax.axis_size(("img", "pair"))
    place = lax.axis_index(RING).reshape(1)
    params = pltpu.CompilerParams(vmem_limit_bytes=40 << 20)

    swap = [(0, 1), (1, 0)]
    qk_other = lax.ppermute(qk_weight, "sub", swap)
    value_other = lax.ppermute(value_weight, "sub", swap)

    def carried(value, moves):
        pairs = []
        for image in range(images):
            for sub in range(2):
                source = moves(image, sub)
                if source is not None:
                    pairs.append((2 * source[0] + source[1], 2 * image + sub))
        return lax.ppermute(value, RING, pairs)

    def ahead(image, sub, step):
        partner = image + step if sub == 0 else image - step
        return partner if 0 <= partner < images else None

    def by_two(image, sub):
        partner = ahead(image, sub, 2)
        return None if partner is None else (partner, sub)

    def within(image, sub):
        return (image ^ 1, image % 2) if image % 2 == sub else None

    def across(image, sub):
        partner = ahead(image, sub, 1)
        return None if image % 2 == sub or partner is None else (image ^ 1, sub)

    def onward(image, sub):
        return None if ahead(image, sub, 3) is None else (ahead(image, sub, 2), sub)

    def onward_inner(image, sub):
        return onward(image, sub) if image % 2 == sub else None

    def onward_outer(image, sub):
        return None if image % 2 == sub else onward(image, sub)

    two = carried(own, by_two)

    def called(kernel, args, out_shape, scratch, cost_estimate, scalars=1):
        return pl.pallas_call(
            kernel,
            in_specs=[SMEM] * scalars + [VMEM] * (len(args) - scalars),
            out_specs=[VMEM] * len(out_shape),
            out_shape=out_shape,
            scratch_shapes=scratch,
            compiler_params=params,
            cost_estimate=cost_estimate,
        )(*args)

    wk, wvt, queries, facts, vectors = called(
        functools.partial(prologue_kernel, images),
        [
            place, links.T, own, qk_weight, value_weight, qk_other, value_other,
            norm_gain.reshape(1, -1), norm_bias.reshape(1, -1), mlp_in_bias.reshape(1, -1),
            mlp_out_bias.reshape(1, -1),
        ],
        [
            shape((width, width), BF16),
            shape((width, width), BF16),
            shape((HEADS, rows, 128), BF16),
            shape((8, 128), F32),
            shape((8, hidden_width), F32),
        ],
        [],
        cost(4 * rows * width * width, 4 << 20),
        scalars=2,
    )

    own_later, facts = lax.optimization_barrier((own, facts))
    inner = carried(own_later, within)
    outer = carried(two, across)
    projected = [
        shape((rows, width), BF16),
        shape((HEADS, width // HEADS + 16, rows), BF16),
    ]
    scratch = [pltpu.VMEM(x.shape, x.dtype) for x in projected]
    message = [shape((width, rows), BF16)]
    work = cost(8 * rows * rows * width, 2 << 20, HEADS * rows * rows)
    half_work = cost(4 * rows * rows * width, 2 << 20, HEADS * rows * half)
    (message_two,) = called(
        functools.partial(partner_kernel, 2, False),
        [place, queries, facts, two, wk, wvt],
        message,
        scratch,
        work,
    )
    outer, inner, message_two = lax.optimization_barrier((outer, inner, message_two))
    outer_far = carried(outer, onward_outer)
    inner_far = carried(inner, onward_inner)
    (message_one,) = called(
        functools.partial(partner_kernel, 1, True),
        [place, queries, facts, outer, inner, wk, wvt],
        message,
        scratch,
        work,
    )
    inner_far, outer_far, message_one = lax.optimization_barrier(
        (inner_far, outer_far, message_one)
    )
    keys, values, send = called(
        functools.partial(last_kernel, 3),
        [place, queries, facts, outer_far, inner_far, wk, wvt, message_two, message_one],
        [*projected, shape((width, half), BF16)],
        [pltpu.VMEM((width, half), BF16)],
        half_work,
    )
    came = lax.ppermute(send, "sub", swap)
    (keep,) = called(
        functools.partial(own_kernel, 3),
        [place, queries, facts, keys, values, message_two, message_one],
        [shape((width, half), F32)],
        [pltpu.VMEM((width, half), BF16)],
        half_work,
    )
    came, keep = lax.optimization_barrier((came, keep))
    (result,) = called(
        tail_kernel,
        [place, keep, came, own, out_weight, mlp_in, vectors, mlp_out],
        [shape((half, width), BF16)],
        [],
        cost(4 * rows * width * width, 4 << 20),
    )
    return result[None]


def solution(mesh):
    placed = (
        P(("groups", "img", "pair"), None, None),
        P("groups", None),
        P(None, "sub"),
        P(None, "sub"),
        P(),
        P(),
        P(),
        P(),
        P(),
        P(),
        P(),
    )

    return jax.shard_map(
        on_device,
        mesh=mesh,
        in_specs=placed,
        out_specs=P(("groups", "img", "pair"), "sub", None),
        check_vma=False,
    )
```

time: 95.8 us -> 80.1 us (0.84)
  Pallas kernels: 0 us -> 62.5 us
  matrix products: 40.8 us -> 0 us
  blocking collectives: 17.1 us -> 0 us
  other arithmetic: 9.53 us -> 0 us
  starting transfers between devices: 18.3 us -> 13.5 us
  between operations: 4.11 us -> 0.17 us
  waiting for transfers between devices: 3.54 us -> 1.13 us
    pallas_call x0 -> x6, Pallas kernels: none -> 62.5 us  [called(): pl.pallas_call(kernel, in_specs=[SMEM] * scalars + [VMEM] * (len(args) -...]
    dot_general x29 -> x0, matrix products: 40.8 us -> none  [the longest x12 16.9 us: tile_messages(): jnp.dot(row_weights, partner_values[:, lo_col:lo_col + head_width], prefe...]
    all_to_all x1 -> x0, blocking collectives: 17.1 us -> none  [on_device(): lax.all_to_all(summed_b, 'sub', split_axis=0, concat_axis=1, tiled=True)]
    reduce_sum x13 -> x0, other arithmetic: 9.17 us -> none  [the longest x12 8.99 us: tile_messages(): row_weights = jax.nn.softmax(scores, axis=1).astype(jnp.bfloat16)]
    ppermute x6 -> x8, starting transfers between devices: 18.3 us -> 13.5 us  [the longest x5 11.2 us: carried(): return lax.ppermute(value, RING, pairs)]
    ppermute x6 -> x8, waiting for transfers between devices: 3.54 us -> 1.13 us  [the longest x1 0.95 us: on_device(): qk_other = lax.ppermute(qk_weight, 'sub', swap)]
    unnamed x14 -> x20, local copies, waits for them, and re-layouts: 0.04 us -> 2.42 us
    dynamic_slice x1 -> x0, local copies, waits for them, and re-layouts: 1.58 us -> none  [link_value(): lax.dynamic_slice(links, (clipped, jnp.int32(step_size - 1)), (1, 1))[0, 0]]
  transfers between devices with their start and end apart: 6 -> 8, of which waited for: 1 -> 2; matrix products, arithmetic and copies ran while one was open for 41% -> 0% of each run, Pallas kernels for 0% -> 62%
where the time goes in v3:
time: 80.1 us; the launch traced here: 79.7 us
  Pallas kernels  62.5 us (78%)
  starting transfers between devices  13.5 us (17%)
  local copies, waits for them, and re-layouts  2.42 us (3%)
  waiting for transfers between devices  1.13 us (1%)
    pallas_call x6, Pallas kernels, called(): pl.pallas_call(kernel, in_specs=[SMEM] * scalars + [VMEM] * (len(args) -...  62.5 us
    ppermute x5, starting transfers between devices, carried(): return lax.ppermute(value, RING, pairs)  11.2 us
    unnamed x20, local copies, waits for them, and re-layouts  2.42 us
    ppermute x1, starting transfers between devices, on_device(): came = lax.ppermute(send, 'sub', swap)  1.74 us
  transfers between devices with their start and end apart: 8, of which 2 were waited for; matrix products, arithmetic and copies ran while one was open for 0% of the time, Pallas kernels for 62%

profile of v3, /device:TPU:17, one launch (start us, length us, event | category | flops | bytes accessed | tf_op | source)
XLA Modules:
  0.0 79.7 jit_solution(15286794952908804016)
XLA Ops:
  0.0 3.2 %collective-permute-start.2 = (bf16[1024,256]{1,0:T(8,128)(2,1)}, bf16[1024,256]{1,0:T(8,128)(2,1)S(1)}, u32[]{:S(2)}, u32[]{:S(2)}) collective-permute-start(bf16[1024,256]{1,0:T(8,128)(2,1)} %bitcast.2.x_ref), channel_id=1, source_target_pairs={{4,0},{6,2},{8,4},{1,5},{10,6},{3,7},{12,8},{5,9},{14,10},{7,11},{... | collective-permute-start | bytes 1572872 | tf_op jit(solution)/shard_map/ppermute | solution.py:261
  3.2 0.1 collective-permute-start
  3.3 0.5 collective-permute-start.1
  3.8 1.0 %collective-permute-done.qk_other_ref = bf16[256,128]{1,0:T(8,128)(2,1)S(1)} collective-permute-done((bf16[256,128]{1,0:T(8,128)(2,1)}, bf16[256,128]{1,0:T(8,128)(2,1)S(1)}, u32[]{:S(2)}, u32[]{:S(2)}) %collective-permute-start) | collective-permute-done | bytes 65568 | tf_op jit(solution)/shard_map/ppermute | solution.py:251
  4.7 0.2 collective-permute-done.1.value_other_ref
  4.9 0.0 copy-start.8
  4.9 0.0 copy-start.7
  4.9 0.0 copy-start.6
  4.9 0.0 copy-start.5
  4.9 0.0 copy-start.9
  4.9 0.7 copy-done.8
  5.6 0.0 copy-done.7
  5.6 0.0 copy-done.6
  5.6 0.0 copy-done.5
  5.6 0.0 copy-done.9
  5.6 0.0 copy-start.3
  5.6 0.8 %copy-done.3 = bf16[256,128]{1,0:T(8,128)(2,1)S(1)} copy-done((bf16[256,128]{1,0:T(8,128)(2,1)S(1)}, bf16[256,128]{1,0:T(8,128)(2,1)}, u32[]{:S(2)}) %copy-start.3) | copy-done | bytes 65560
  6.5 0.0 copy-start.4
  6.5 0.8 %copy-done.4 = bf16[256,128]{1,0:T(8,128)(2,1)S(1)} copy-done((bf16[256,128]{1,0:T(8,128)(2,1)S(1)}, bf16[256,128]{1,0:T(8,128)(2,1)}, u32[]{:S(2)}) %copy-start.4) | copy-done | bytes 65560
  7.3 1.4 %shard_map.109 = (bf16[256,256]{1,0:T(8,128)(2,1)S(1)}, bf16[256,256]{1,0:T(8,128)(2,1)S(1)}, bf16[4,1024,128]{2,1,0:T(8,128)(2,1)S(1)}, f32[8,128]{1,0:T(8,128)S(1)}, f32[8,512]{1,0:T(8,128)S(1)}) custom-call(s32[1]{0:T(128)} %bitcast.place_ref, s32[3,8]{1,0:T(4,128)S(1)} %bitcast.8, bf16[1024,256]{1,0:T(8,128)(2,1)} %bitcast.2.x_ref, ...), custom_call_target="tpu_custom_call" | custom-call | flops 268435456 | bytes 4194304 | tf_op jit(solution)/shard_map/pallas_call | solution.py:290
  8.7 3.1 %collective-permute-start.4 = (bf16[1024,256]{1,0:T(8,128)(2,1)}, bf16[1024,256]{1,0:T(8,128)(2,1)S(1)}, u32[]{:S(2)}, u32[]{:S(2)}) collective-permute-start(bf16[1024,256]{1,0:T(8,128)(2,1)} %bitcast.2.x_ref), channel_id=1, source_target_pairs={{2,0},{1,3},{6,4},{5,7},{10,8},{9,11},{14,12},{13,15},{18,16},{17,... | collective-permute-start | bytes 1572872 | tf_op jit(solution)/shard_map/ppermute | solution.py:261
  11.9 0.0 collective-permute-done.2.x_ref
  11.9 1.3 %collective-permute-start.3 = (bf16[1024,256]{1,0:T(8,128)(2,1)S(1)}, bf16[1024,256]{1,0:T(8,128)(2,1)S(1)}, u32[]{:S(2)}, u32[]{:S(2)}) collective-permute-start(bf16[1024,256]{1,0:T(8,128)(2,1)S(1)} %collective-permute-done.2.x_ref), channel_id=1, source_target_pairs={{0,2},{7,5},{4,6},{11,9},{8,10},{15,13},{16,18},{23,21},{20,22},{2... | collective-permute-start | bytes 1572872 | tf_op jit(solution)/shard_map/ppermute | solution.py:261
  13.2 19.2 %shard_map.110.first_ref = bf16[256,1024]{1,0:T(8,128)(2,1)S(1)} custom-call(s32[1]{0:T(128)} %bitcast.place_ref, bf16[4,1024,128]{2,1,0:T(8,128)(2,1)S(1)} %get-tuple-element.23.queries_ref, f32[8,128]{1,0:T(8,128)S(1)} %get-tuple-element.25.facts_ref, bf16[1024,256]{1,0:T(8,128)(2,1)S(1)} %collective-permute-done.2.x_ref, ...), custom_call_target="tpu_custom_call" | custom-call | flops 2147483648 | bytes 2097152 | tf_op jit(solution)/shard_map/pallas_call | solution.py:290
  32.4 0.0 collective-permute-done.4.refs_0_
  32.4 0.0 collective-permute-done.3.x_ref
  32.4 0.7 collective-permute-start.5
  33.1 2.9 %collective-permute-start.6 = (bf16[1024,256]{1,0:T(8,128)(2,1)S(1)}, bf16[1024,256]{1,0:T(8,128)(2,1)S(1)}, u32[]{:S(2)}, u32[]{:S(2)}) collective-permute-start(bf16[1024,256]{1,0:T(8,128)(2,1)S(1)} %collective-permute-done.3.x_ref), channel_id=1, source_target_pairs={{6,2},{10,6},{5,9},{9,13},{22,18},{26,22},{21,25},{25,29}} | collective-permute-start | bytes 1572872 | tf_op jit(solution)/shard_map/ppermute | solution.py:261
  36.0 19.3 %shard_map.111.second_ref = bf16[256,1024]{1,0:T(8,128)(2,1)S(1)} custom-call(s32[1]{0:T(128)} %bitcast.place_ref, bf16[4,1024,128]{2,1,0:T(8,128)(2,1)S(1)} %get-tuple-element.23.queries_ref, f32[8,128]{1,0:T(8,128)S(1)} %get-tuple-element.25.facts_ref, bf16[1024,256]{1,0:T(8,128)(2,1)S(1)} %collective-permute-done.3.x_ref, ...), custom_call_target="tpu_custom_call" | custom-call | flops 2147483648 | bytes 2097152 | tf_op jit(solution)/shard_map/pallas_call | solution.py:290
  55.3 0.0 collective-permute-done.5.other_ref
  55.3 0.0 collective-permute-done.6.x_ref
  55.3 10.0 %shard_map.112 = (bf16[1024,256]{1,0:T(8,128)(2,1)S(1)}, bf16[4,80,1024]{2,1,0:T(8,128)(2,1)S(1)}, bf16[256,512]{1,0:T(8,128)(2,1)S(1)}) custom-call(s32[1]{0:T(128)} %bitcast.place_ref, bf16[4,1024,128]{2,1,0:T(8,128)(2,1)S(1)} %get-tuple-element.23.queries_ref, f32[8,128]{1,0:T(8,128)S(1)} %get-tuple-element.25.facts_ref, ...), custom_call_target="tpu_custom_call" | custom-call | flops 1073741824 | bytes 2097152 | tf_op jit(solution)/shard_map/pallas_call | solution.py:290
  65.3 1.7 %collective-permute-start.7 = (bf16[256,512]{1,0:T(8,128)(2,1)S(1)}, bf16[256,512]{1,0:T(8,128)(2,1)S(1)}, u32[]{:S(2)}, u32[]{:S(2)}) collective-permute-start(bf16[256,512]{1,0:T(8,128)(2,1)S(1)} %get-tuple-element.35), channel_id=1, source_target_pairs={{0,1},{1,0},{2,3},{3,2},{4,5},{5,4},{6,7},{7,6},{8,9},{9,8},{10,11... | collective-permute-start | bytes 786440 | tf_op jit(solution)/shard_map/ppermute | solution.py:357
  67.1 0.0 copy-start
  67.1 0.0 copy-start.1
  67.1 0.0 copy-start.2
  67.1 9.6 %shard_map.113.keep_ref = f32[256,512]{1,0:T(8,128)S(1)} custom-call(s32[1]{0:T(128)} %bitcast.place_ref, bf16[4,1024,128]{2,1,0:T(8,128)(2,1)S(1)} %get-tuple-element.23.queries_ref, f32[8,128]{1,0:T(8,128)S(1)} %get-tuple-element.25.facts_ref, bf16[1024,256]{1,0:T(8,128)(2,1)S(1)} %get-tuple-element.36.keys_ref, ...), custom_call_target="tpu_custom_call" | custom-call | flops 1073741824 | bytes 2097152 | tf_op jit(solution)/shard_map/pallas_call | solution.py:290
  76.7 0.0 collective-permute-done.7.came_ref
  76.7 0.0 copy-done
  76.7 0.0 copy-done.1
  76.7 0.0 copy-done.2
  76.7 3.0 %shard_map.114 = bf16[512,256]{1,0:T(8,128)(2,1)} custom-call(s32[1]{0:T(128)} %bitcast.place_ref, f32[256,512]{1,0:T(8,128)S(1)} %shard_map.113.keep_ref, bf16[256,512]{1,0:T(8,128)(2,1)S(1)} %collective-permute-done.7.came_ref, bf16[1024,256]{1,0:T(8,128)(2,1)} %bitcast.2.x_ref, bf16[256,256]{1,0:T(8,128)(2,1)S(1)} %copy-done.2, ...), custom_call_target="tpu_custom_call" | custom-call | flops 268435456 | bytes 4194304 | tf_op jit(solution)/shard_map/pallas_call | solution.py:290
Async XLA Ops:
  0.0 11.9 %collective-permute-start.2 = (bf16[1024,256]{1,0:T(8,128)(2,1)}, bf16[1024,256]{1,0:T(8,128)(2,1)S(1)}, u32[]{:S(2)}, u32[]{:S(2)}) collective-permute-start(bf16[1024,256]{1,0:T(8,128)(2,1)} %bitcast.2.x_ref), channel_id=1, source_target_pairs={{4,0},{6,2},{8,4},{1,5},{10,6},{3,7},{12,8},{5,9},{14,10},{7,11},{... | collective-permute-start | bytes 1572872 | tf_op jit(solution)/shard_map/ppermute | solution.py:261
  3.2 1.5 %collective-permute-start = (bf16[256,128]{1,0:T(8,128)(2,1)}, bf16[256,128]{1,0:T(8,128)(2,1)S(1)}, u32[]{:S(2)}, u32[]{:S(2)}) collective-permute-start(bf16[256,128]{1,0:T(8,128)(2,1)} %qk_ref.1), channel_id=1, source_target_pairs={{0,1},{1,0},{2,3},{3,2},{4,5},{5,4},{6,7},{7,6},{8,9},{9,8},{10,11... | collective-permute-start | bytes 196616 | tf_op jit(solution)/shard_map/ppermute | solution.py:251
  3.3 1.6 %collective-permute-start.1 = (bf16[256,128]{1,0:T(8,128)(2,1)}, bf16[256,128]{1,0:T(8,128)(2,1)S(1)}, u32[]{:S(2)}, u32[]{:S(2)}) collective-permute-start(bf16[256,128]{1,0:T(8,128)(2,1)} %value_ref.1), channel_id=1, source_target_pairs={{0,1},{1,0},{2,3},{3,2},{4,5},{5,4},{6,7},{7,6},{8,9},{9,8},{10,11... | collective-permute-start | bytes 196616 | tf_op jit(solution)/shard_map/ppermute | solution.py:252
  4.9 0.7 copy-start.8
  4.9 0.7 copy-start.7
  4.9 0.7 copy-start.6
  4.9 0.7 copy-start.5
  4.9 0.7 copy-start.9
  5.6 0.8 %copy-start.3 = (bf16[256,128]{1,0:T(8,128)(2,1)S(1)}, bf16[256,128]{1,0:T(8,128)(2,1)}, u32[]{:S(2)}) copy-start(bf16[256,128]{1,0:T(8,128)(2,1)} %qk_ref.1) | copy-start | bytes 196612
  6.5 0.8 %copy-start.4 = (bf16[256,128]{1,0:T(8,128)(2,1)S(1)}, bf16[256,128]{1,0:T(8,128)(2,1)}, u32[]{:S(2)}) copy-start(bf16[256,128]{1,0:T(8,128)(2,1)} %value_ref.1) | copy-start | bytes 196612
  8.7 23.7 %collective-permute-start.4 = (bf16[1024,256]{1,0:T(8,128)(2,1)}, bf16[1024,256]{1,0:T(8,128)(2,1)S(1)}, u32[]{:S(2)}, u32[]{:S(2)}) collective-permute-start(bf16[1024,256]{1,0:T(8,128)(2,1)} %bitcast.2.x_ref), channel_id=1, source_target_pairs={{2,0},{1,3},{6,4},{5,7},{10,8},{9,11},{14,12},{13,15},{18,16},{17,... | collective-permute-start | bytes 1572872 | tf_op jit(solution)/shard_map/ppermute | solution.py:261
  11.9 20.6 %collective-permute-start.3 = (bf16[1024,256]{1,0:T(8,128)(2,1)S(1)}, bf16[1024,256]{1,0:T(8,128)(2,1)S(1)}, u32[]{:S(2)}, u32[]{:S(2)}) collective-permute-start(bf16[1024,256]{1,0:T(8,128)(2,1)S(1)} %collective-permute-done.2.x_ref), channel_id=1, source_target_pairs={{0,2},{7,5},{4,6},{11,9},{8,10},{15,13},{16,18},{23,21},{20,22},{2... | collective-permute-start | bytes 1572872 | tf_op jit(solution)/shard_map/ppermute | solution.py:261
  32.4 22.9 %collective-permute-start.5 = (bf16[1024,256]{1,0:T(8,128)(2,1)S(1)}, bf16[1024,256]{1,0:T(8,128)(2,1)S(1)}, u32[]{:S(2)}, u32[]{:S(2)}) collective-permute-start(bf16[1024,256]{1,0:T(8,128)(2,1)S(1)} %collective-permute-done.4.refs_0_), channel_id=1, source_target_pairs={{4,0},{8,4},{3,7},{12,8},{7,11},{11,15},{20,16},{24,20},{19,23},{2... | collective-permute-start | bytes 1572872 | tf_op jit(solution)/shard_map/ppermute | solution.py:261
  33.1 22.2 %collective-permute-start.6 = (bf16[1024,256]{1,0:T(8,128)(2,1)S(1)}, bf16[1024,256]{1,0:T(8,128)(2,1)S(1)}, u32[]{:S(2)}, u32[]{:S(2)}) collective-permute-start(bf16[1024,256]{1,0:T(8,128)(2,1)S(1)} %collective-permute-done.3.x_ref), channel_id=1, source_target_pairs={{6,2},{10,6},{5,9},{9,13},{22,18},{26,22},{21,25},{25,29}} | collective-permute-start | bytes 1572872 | tf_op jit(solution)/shard_map/ppermute | solution.py:261
  65.3 11.4 %collective-permute-start.7 = (bf16[256,512]{1,0:T(8,128)(2,1)S(1)}, bf16[256,512]{1,0:T(8,128)(2,1)S(1)}, u32[]{:S(2)}, u32[]{:S(2)}) collective-permute-start(bf16[256,512]{1,0:T(8,128)(2,1)S(1)} %get-tuple-element.35), channel_id=1, source_target_pairs={{0,1},{1,0},{2,3},{3,2},{4,5},{5,4},{6,7},{7,6},{8,9},{9,8},{10,11... | collective-permute-start | bytes 786440 | tf_op jit(solution)/shard_map/ppermute | solution.py:357
  67.1 9.6 %copy-start = (bf16[512,512]{1,0:T(8,128)(2,1)S(1)}, bf16[512,512]{1,0:T(8,128)(2,1)}, u32[]{:S(2)}) copy-start(bf16[512,512]{1,0:T(8,128)(2,1)} %mlp_ref.1) | copy-start | bytes 1572868
  67.1 9.6 %copy-start.1 = (bf16[512,256]{1,0:T(8,128)(2,1)S(1)}, bf16[512,256]{1,0:T(8,128)(2,1)}, u32[]{:S(2)}) copy-start(bf16[512,256]{1,0:T(8,128)(2,1)} %mlp_out_ref.1) | copy-start | bytes 786436
  67.1 9.7 %copy-start.2 = (bf16[256,256]{1,0:T(8,128)(2,1)S(1)}, bf16[256,256]{1,0:T(8,128)(2,1)}, u32[]{:S(2)}) copy-start(bf16[256,256]{1,0:T(8,128)(2,1)} %out_ref.1) | copy-start | bytes 393220

commit v4 on v3

--- a/solution.py
+++ b/solution.py
@@ -28,7 +28,7 @@
 
 def prologue_kernel(
     images, place_ref, links_ref, x_ref, qk_ref, value_ref, qk_other_ref, value_other_ref, gain_ref,
-    shift_ref, bias_ref, out_bias_ref, wk_ref, wvt_ref, queries_ref, facts_ref, vectors_ref,
+    shift_ref, bias_ref, out_bias_ref, wk_ref, wvt_ref, queries_ref, facts_ref, rows_ref, vectors_ref,
 ):
     rows, width = x_ref.shape
     local = width // 2
@@ -53,20 +53,20 @@
         entry = links_ref[step - 1, jnp.clip(lower, 0, images - 1)]
         linked = jnp.where(jnp.logical_and(inside, entry != 0), 1.0, 0.0)
         facts_ref[step : step + 1, :] = jnp.full((1, 128), linked, F32)
+    half = rows // 2
+    rows_ref[...] = x_ref[pl.ds(pl.multiple_of(sub * half, half), half), :]
     vectors_ref[0:1, :] = gain_ref[...]
     vectors_ref[1:2, :] = shift_ref[...]
     vectors_ref[2:3, :] = bias_ref[...]
     vectors_ref[3:4, :width] = out_bias_ref[...]
 
 
-def project(x_ref, other_ref, take_other, wk_ref, wvt_ref, keys_ref, values_ref):
+def project(x_ref, wk_ref, wvt_ref, keys_ref, values_ref):
     rows, width = keys_ref.shape
     head_width = width // HEADS
     tile = 256
     for r in range(0, rows, tile):
         x = x_ref[r : r + tile, :]
-        if other_ref is not None:
-            x = jnp.where(take_other, other_ref[r : r + tile, :], x)
         keys_ref[r : r + tile, :] = dot(x, wk_ref[...]).astype(BF16)
         values = dot(wvt_ref[...], x, (1, 1)).astype(BF16)
         for head in range(HEADS):
@@ -129,13 +129,9 @@
         lax.fori_loop(0, HEADS * (span // tile), body, 0)
 
 
-def takes_other(place):
-    return lax.rem(place // 2, 2) == lax.rem(place, 2)
-
-
-def partner_kernel(step, two, place_ref, queries_ref, facts_ref, x_ref, *refs):
-    other_ref, *refs = refs if two else (None, *refs)
-    wk_ref, wvt_ref, message_ref, keys_ref, values_ref = refs
+def partner_kernel(
+    step, queries_ref, facts_ref, x_ref, wk_ref, wvt_ref, message_ref, keys_ref, values_ref
+):
     rows, _ = keys_ref.shape
     linked = jnp.max(facts_ref[step : step + 1, :]) > 0.0
 
@@ -145,8 +141,7 @@
 
     @pl.when(linked)
     def _():
-        take = takes_other(place_ref[0])
-        project(x_ref, other_ref, take, wk_ref, wvt_ref, keys_ref, values_ref)
+        project(x_ref, wk_ref, wvt_ref, keys_ref, values_ref)
         wide = rows // 2
 
         def body(i, carry):
@@ -158,8 +153,8 @@
 
 
 def last_kernel(
-    step, place_ref, queries_ref, facts_ref, x_ref, other_ref, wk_ref, wvt_ref, first_ref,
-    second_ref, keys_ref, values_ref, send_ref, message_ref,
+    step, place_ref, queries_ref, facts_ref, x_ref, wk_ref, wvt_ref, first_ref, second_ref,
+    keys_ref, values_ref, send_ref, message_ref,
 ):
     half = message_ref.shape[1]
     place = place_ref[0]
@@ -174,7 +169,7 @@
 
     @pl.when(linked)
     def _():
-        project(x_ref, other_ref, takes_other(place), wk_ref, wvt_ref, keys_ref, values_ref)
+        project(x_ref, wk_ref, wvt_ref, keys_ref, values_ref)
         attend(queries_ref, at, half, keys_ref, values_ref, message_ref, pl.ds(0, half))
         total = first_ref[:, here].astype(F32) + second_ref[:, here].astype(F32)
         send_ref[...] = (total + message_ref[...].astype(F32)).astype(BF16)
@@ -201,11 +196,10 @@
 
 
 def tail_kernel(
-    place_ref, keep_ref, came_ref, x_ref, out_ref, mlp_ref, vectors_ref, mlp_out_ref, result_ref
-):
-    width, rows = keep_ref.shape
-    sub = lax.rem(place_ref[0], 2)
-    own_rows = x_ref[pl.ds(pl.multiple_of(sub * rows, rows), rows), :]
+    keep_ref, came_ref, rows_ref, out_ref, mlp_ref, vectors_ref, mlp_out_ref, result_ref
+):
+    width = keep_ref.shape[0]
+    own_rows = rows_ref[...]
     hidden = dot(own_rows, mlp_ref[:width, :]) + vectors_ref[2:3, :]
     summed = (keep_ref[...] + came_ref[...].astype(F32)).astype(BF16)
     projected = dot(summed, out_ref[...], (0, 0)).astype(BF16)
@@ -251,40 +245,16 @@
     qk_other = lax.ppermute(qk_weight, "sub", swap)
     value_other = lax.ppermute(value_weight, "sub", swap)
 
-    def carried(value, moves):
+    def fetched(step):
         pairs = []
         for image in range(images):
-            for sub in range(2):
-                source = moves(image, sub)
-                if source is not None:
-                    pairs.append((2 * source[0] + source[1], 2 * image + sub))
-        return lax.ppermute(value, RING, pairs)
-
-    def ahead(image, sub, step):
-        partner = image + step if sub == 0 else image - step
-        return partner if 0 <= partner < images else None
-
-    def by_two(image, sub):
-        partner = ahead(image, sub, 2)
-        return None if partner is None else (partner, sub)
-
-    def within(image, sub):
-        return (image ^ 1, image % 2) if image % 2 == sub else None
-
-    def across(image, sub):
-        partner = ahead(image, sub, 1)
-        return None if image % 2 == sub or partner is None else (image ^ 1, sub)
-
-    def onward(image, sub):
-        return None if ahead(image, sub, 3) is None else (ahead(image, sub, 2), sub)
-
-    def onward_inner(image, sub):
-        return onward(image, sub) if image % 2 == sub else None
-
-    def onward_outer(image, sub):
-        return None if image % 2 == sub else onward(image, sub)
-
-    two = carried(own, by_two)
+            if image >= step:
+                pairs.append((2 * image, 2 * (image - step)))
+            if image + step < images:
+                pairs.append((2 * image + 1, 2 * (image + step) + 1))
+        return lax.ppermute(own, RING, pairs)
+
+    three, two, one = (fetched(step) for step in (3, 2, 1))
 
     def called(kernel, args, out_shape, scratch, cost_estimate, scalars=1):
         return pl.pallas_call(
@@ -297,7 +267,7 @@
             cost_estimate=cost_estimate,
         )(*args)
 
-    wk, wvt, queries, facts, vectors = called(
+    wk, wvt, queries, facts, own_half, vectors = called(
         functools.partial(prologue_kernel, images),
         [
             place, links.T, own, qk_weight, value_weight, qk_other, value_other,
@@ -309,6 +279,7 @@
             shape((width, width), BF16),
             shape((HEADS, rows, 128), BF16),
             shape((8, 128), F32),
+            shape((half, width), BF16),
             shape((8, hidden_width), F32),
         ],
         [],
@@ -316,9 +287,6 @@
         scalars=2,
     )
 
-    own_later, facts = lax.optimization_barrier((own, facts))
-    inner = carried(own_later, within)
-    outer = carried(two, across)
     projected = [
         shape((rows, width), BF16),
         shape((HEADS, width // HEADS + 16, rows), BF16),
@@ -327,37 +295,30 @@
     message = [shape((width, rows), BF16)]
     work = cost(8 * rows * rows * width, 2 << 20, HEADS * rows * rows)
     half_work = cost(4 * rows * rows * width, 2 << 20, HEADS * rows * half)
-    (message_two,) = called(
-        functools.partial(partner_kernel, 2, False),
-        [place, queries, facts, two, wk, wvt],
-        message,
-        scratch,
-        work,
-    )
-    outer, inner, message_two = lax.optimization_barrier((outer, inner, message_two))
-    outer_far = carried(outer, onward_outer)
-    inner_far = carried(inner, onward_inner)
-    (message_one,) = called(
-        functools.partial(partner_kernel, 1, True),
-        [place, queries, facts, outer, inner, wk, wvt],
-        message,
-        scratch,
-        work,
-    )
-    inner_far, outer_far, message_one = lax.optimization_barrier(
-        (inner_far, outer_far, message_one)
-    )
+    messages = []
+    for step, partner in ((3, three), (2, two)):
+        if messages:
+            partner, messages = lax.optimization_barrier((partner, messages))
+        messages += called(
+            functools.partial(partner_kernel, step),
+            [queries, facts, partner, wk, wvt],
+            message,
+            scratch,
+            work,
+            scalars=0,
+        )
+    one, messages = lax.optimization_barrier((one, messages))
     keys, values, send = called(
-        functools.partial(last_kernel, 3),
-        [place, queries, facts, outer_far, inner_far, wk, wvt, message_two, message_one],
+        functools.partial(last_kernel, 1),
+        [place, queries, facts, one, wk, wvt, *messages],
         [*projected, shape((width, half), BF16)],
         [pltpu.VMEM((width, half), BF16)],
         half_work,
     )
     came = lax.ppermute(send, "sub", swap)
     (keep,) = called(
-        functools.partial(own_kernel, 3),
-        [place, queries, facts, keys, values, message_two, message_one],
+        functools.partial(own_kernel, 1),
+        [place, queries, facts, keys, values, *messages],
         [shape((width, half), F32)],
         [pltpu.VMEM((width, half), BF16)],
         half_work,
@@ -365,10 +326,11 @@
     came, keep = lax.optimization_barrier((came, keep))
     (result,) = called(
         tail_kernel,
-        [place, keep, came, own, out_weight, mlp_in, vectors, mlp_out],
+        [keep, came, own_half, out_weight, mlp_in, vectors, mlp_out],
         [shape((half, width), BF16)],
         [],
         cost(4 * rows * width * width, 4 << 20),
+        scalars=0,
     )
     return result[None]
 

time: 80.1 us -> 80 us (level); the launches traced: 79.7 us -> 78.5 us
  starting transfers between devices: 13.5 us -> 10.4 us
  waiting for transfers between devices: 1.13 us -> 3.61 us
  Pallas kernels: 62.5 us -> 60.9 us
  local copies, waits for them, and re-layouts: 2.42 us -> 3.46 us
    ppermute x5 -> x3, starting transfers between devices: 11.2 us -> 7.96 us  [fetched(): return lax.ppermute(own, RING, pairs)]
    ppermute x5 -> x3, waiting for transfers between devices: 0.01 us -> 2.49 us  [fetched(): return lax.ppermute(own, RING, pairs)]
    pallas_call x6, Pallas kernels: 62.5 us -> 60.9 us  [called(): pl.pallas_call(kernel, in_specs=[SMEM] * scalars + [VMEM] * (len(args) -...]
    unnamed x20 -> x22, local copies, waits for them, and re-layouts: 2.42 us -> 3.46 us
  transfers between devices with their start and end apart: 8 -> 6, of which waited for: 2 -> 3; matrix products, arithmetic and copies ran while one was open for 0% -> 0% of each run, Pallas kernels for 62% -> 62%
where the time goes in v4:
time: 80 us; the launch traced here: 78.5 us
  Pallas kernels  60.9 us (76%)
  starting transfers between devices  10.4 us (13%)
  waiting for transfers between devices  3.61 us (5%)
  local copies, waits for them, and re-layouts  3.46 us (4%)
    pallas_call x6, Pallas kernels, called(): pl.pallas_call(kernel, in_specs=[SMEM] * scalars + [VMEM] * (len(args) -...  60.9 us
    ppermute x3, starting transfers between devices, fetched(): return lax.ppermute(own, RING, pairs)  7.96 us
    unnamed x22, local copies, waits for them, and re-layouts  3.46 us
    ppermute x3, waiting for transfers between devices, fetched(): return lax.ppermute(own, RING, pairs)  2.49 us
    ppermute x1, starting transfers between devices, on_device(): came = lax.ppermute(send, 'sub', swap)  1.85 us
  transfers between devices with their start and end apart: 6, of which 3 were waited for; matrix products, arithmetic and copies ran while one was open for 0% of the time, Pallas kernels for 62%

profile of v4, /device:TPU:17, one launch (start us, length us, event | category | flops | bytes accessed | tf_op | source)
XLA Modules:
  0.0 78.5 jit_solution(16557167354803683269)
XLA Ops:
  0.0 4.1 %collective-permute-start.4 = (bf16[1024,256]{1,0:T(8,128)(2,1)}, bf16[1024,256]{1,0:T(8,128)(2,1)S(1)}, u32[]{:S(2)}, u32[]{:S(2)}) collective-permute-start(bf16[1024,256]{1,0:T(8,128)(2,1)} %bitcast.8), channel_id=1, source_target_pairs={{1,7},{3,9},{5,11},{6,0},{7,13},{8,2},{9,15},{10,4},{12,6},{14,8},... | collective-permute-start | bytes 1572872 | tf_op jit(solution)/shard_map/ppermute | solution.py:255
  4.1 1.9 %collective-permute-start.3 = (bf16[1024,256]{1,0:T(8,128)(2,1)}, bf16[1024,256]{1,0:T(8,128)(2,1)S(1)}, u32[]{:S(2)}, u32[]{:S(2)}) collective-permute-start(bf16[1024,256]{1,0:T(8,128)(2,1)} %bitcast.9), channel_id=1, source_target_pairs={{1,5},{3,7},{4,0},{5,9},{6,2},{7,11},{8,4},{9,13},{10,6},{11,15},{... | collective-permute-start | bytes 1572872 | tf_op jit(solution)/shard_map/ppermute | solution.py:255
  6.1 1.9 %collective-permute-start.2 = (bf16[1024,256]{1,0:T(8,128)(2,1)}, bf16[1024,256]{1,0:T(8,128)(2,1)S(1)}, u32[]{:S(2)}, u32[]{:S(2)}) collective-permute-start(bf16[1024,256]{1,0:T(8,128)(2,1)} %bitcast.10), channel_id=1, source_target_pairs={{1,3},{2,0},{3,5},{4,2},{5,7},{6,4},{7,9},{8,6},{9,11},{10,8},{11,... | collective-permute-start | bytes 1572872 | tf_op jit(solution)/shard_map/ppermute | solution.py:255
  8.0 0.1 collective-permute-start
  8.1 0.5 collective-permute-start.1
  8.6 1.0 %collective-permute-done.qk_other_ref = bf16[256,128]{1,0:T(8,128)(2,1)S(1)} collective-permute-done((bf16[256,128]{1,0:T(8,128)(2,1)}, bf16[256,128]{1,0:T(8,128)(2,1)S(1)}, u32[]{:S(2)}, u32[]{:S(2)}) %collective-permute-start) | collective-permute-done | bytes 65568 | tf_op jit(solution)/shard_map/ppermute | solution.py:245
  9.5 0.2 collective-permute-done.1.value_other_ref
  9.7 0.0 copy-start.9
  9.7 0.0 copy-start.8
  9.7 0.0 copy-start.7
  9.7 0.0 copy-start.6
  9.7 0.0 copy-start.10
  9.7 0.7 copy-done.9
  10.4 0.0 copy-done.8
  10.4 0.0 copy-done.7
  10.4 0.0 copy-done.6
  10.4 0.0 copy-done.10
  10.4 0.0 copy-start.3
  10.4 1.0 %copy-done.3 = bf16[1,1024,256]{2,1,0:T(8,128)(2,1)S(1)} copy-done((bf16[1,1024,256]{2,1,0:T(8,128)(2,1)S(1)}, bf16[1,1024,256]{2,1,0:T(8,128)(2,1)}, u32[]{:S(2)}) %copy-start.3) | copy-done | bytes 524312
  11.5 0.0 copy-start.4
  11.5 0.8 %copy-done.4 = bf16[256,128]{1,0:T(8,128)(2,1)S(1)} copy-done((bf16[256,128]{1,0:T(8,128)(2,1)S(1)}, bf16[256,128]{1,0:T(8,128)(2,1)}, u32[]{:S(2)}) %copy-start.4) | copy-done | bytes 65560
  12.3 0.0 copy-start.5
  12.3 0.8 %copy-done.5 = bf16[256,128]{1,0:T(8,128)(2,1)S(1)} copy-done((bf16[256,128]{1,0:T(8,128)(2,1)S(1)}, bf16[256,128]{1,0:T(8,128)(2,1)}, u32[]{:S(2)}) %copy-start.5) | copy-done | bytes 65560
  13.1 0.9 %shard_map.109 = (bf16[256,256]{1,0:T(8,128)(2,1)S(1)}, bf16[256,256]{1,0:T(8,128)(2,1)S(1)}, bf16[4,1024,128]{2,1,0:T(8,128)(2,1)S(1)}, f32[8,128]{1,0:T(8,128)...) custom-call(s32[1]{0:T(128)} %bitcast.place_ref, s32[3,8]{1,0:T(4,128)S(1)} %bitcast.12, ...), custom_call_target="tpu_custom_call" | custom-call | flops 268435456 | bytes 4194304 | tf_op jit(solution)/shard_map/pallas_call | solution.py:260
  14.1 2.5 %collective-permute-done.4.x_ref = bf16[1024,256]{1,0:T(8,128)(2,1)S(1)} collective-permute-done((bf16[1024,256]{1,0:T(8,128)(2,1)}, bf16[1024,256]{1,0:T(8,128)(2,1)S(1)}, u32[]{:S(2)}, u32[]{:S(2)}) %collective-permute-start.4) | collective-permute-done | bytes 524320 | tf_op jit(solution)/shard_map/ppermute | solution.py:255
  16.5 19.3 %shard_map.110.first_ref = bf16[256,1024]{1,0:T(8,128)(2,1)S(1)} custom-call(bf16[4,1024,128]{2,1,0:T(8,128)(2,1)S(1)} %get-tuple-element.21.queries_ref, f32[8,128]{1,0:T(8,128)S(1)} %get-tuple-element.22.facts_ref, bf16[1024,256]{1,0:T(8,128)(2,1)S(1)} %collective-permute-done.4.x_ref, bf16[256,256]{1,0:T(8,128)(2,1)S(1)} %get-tuple-element.23.wk_ref, ...), custom_call_target="tpu_custom_call" | custom-call | flops 2147483648 | bytes 2097152 | tf_op jit(solution)/shard_map/pallas_call | solution.py:260
  35.8 0.0 collective-permute-done.3.x_ref
  35.8 19.2 %shard_map.111.second_ref = bf16[256,1024]{1,0:T(8,128)(2,1)S(1)} custom-call(bf16[4,1024,128]{2,1,0:T(8,128)(2,1)S(1)} %get-tuple-element.21.queries_ref, f32[8,128]{1,0:T(8,128)S(1)} %get-tuple-element.22.facts_ref, bf16[1024,256]{1,0:T(8,128)(2,1)S(1)} %collective-permute-done.3.x_ref, bf16[256,256]{1,0:T(8,128)(2,1)S(1)} %get-tuple-element.23.wk_ref, ...), custom_call_target="tpu_custom_call" | custom-call | flops 2147483648 | bytes 2097152 | tf_op jit(solution)/shard_map/pallas_call | solution.py:260
  55.1 0.0 collective-permute-done.2.x_ref
  55.1 10.0 %shard_map.112 = (bf16[1024,256]{1,0:T(8,128)(2,1)S(1)}, bf16[4,80,1024]{2,1,0:T(8,128)(2,1)S(1)}, bf16[256,512]{1,0:T(8,128)(2,1)S(1)}) custom-call(s32[1]{0:T(128)} %bitcast.place_ref, bf16[4,1024,128]{2,1,0:T(8,128)(2,1)S(1)} %get-tuple-element.21.queries_ref, f32[8,128]{1,0:T(8,128)S(1)} %get-tuple-element.22.facts_ref, ...), custom_call_target="tpu_custom_call" | custom-call | flops 1073741824 | bytes 2097152 | tf_op jit(solution)/shard_map/pallas_call | solution.py:260
  65.1 1.9 %collective-permute-start.5 = (bf16[256,512]{1,0:T(8,128)(2,1)S(1)}, bf16[256,512]{1,0:T(8,128)(2,1)S(1)}, u32[]{:S(2)}, u32[]{:S(2)}) collective-permute-start(bf16[256,512]{1,0:T(8,128)(2,1)S(1)} %get-tuple-element.30), channel_id=1, source_target_pairs={{0,1},{1,0},{2,3},{3,2},{4,5},{5,4},{6,7},{7,6},{8,9},{9,8},{10,11... | collective-permute-start | bytes 786440 | tf_op jit(solution)/shard_map/ppermute | solution.py:318
  66.9 0.0 copy-start
  66.9 0.0 copy-start.1
  66.9 0.0 copy-start.2
  66.9 9.6 %shard_map.113.keep_ref = f32[256,512]{1,0:T(8,128)S(1)} custom-call(s32[1]{0:T(128)} %bitcast.place_ref, bf16[4,1024,128]{2,1,0:T(8,128)(2,1)S(1)} %get-tuple-element.21.queries_ref, f32[8,128]{1,0:T(8,128)S(1)} %get-tuple-element.22.facts_ref, bf16[1024,256]{1,0:T(8,128)(2,1)S(1)} %get-tuple-element.31.keys_ref, ...), custom_call_target="tpu_custom_call" | custom-call | flops 1073741824 | bytes 2097152 | tf_op jit(solution)/shard_map/pallas_call | solution.py:260
  76.5 0.0 collective-permute-done.5.came_ref
  76.5 0.0 copy-done
  76.5 0.0 copy-done.1
  76.5 0.0 copy-done.2
  76.5 1.9 %shard_map.114 = bf16[512,256]{1,0:T(8,128)(2,1)} custom-call(f32[256,512]{1,0:T(8,128)S(1)} %shard_map.113.keep_ref, bf16[256,512]{1,0:T(8,128)(2,1)S(1)} %collective-permute-done.5.came_ref, bf16[512,256]{1,0:T(8,128)(2,1)S(1)} %get-tuple-element.35.rows_ref, bf16[256,256]{1,0:T(8,128)(2,1)S(1)} %copy-done.2, bf16[512,512]{1,0:T(8,128)(2,1)S(1)} %copy-done, ...), custom_call_target="tpu_custom_call" | custom-call | flops 268435456 | bytes 4194304 | tf_op jit(solution)/shard_map/pallas_call | solution.py:260
Async XLA Ops:
  0.0 16.5 %collective-permute-start.4 = (bf16[1024,256]{1,0:T(8,128)(2,1)}, bf16[1024,256]{1,0:T(8,128)(2,1)S(1)}, u32[]{:S(2)}, u32[]{:S(2)}) collective-permute-start(bf16[1024,256]{1,0:T(8,128)(2,1)} %bitcast.8), channel_id=1, source_target_pairs={{1,7},{3,9},{5,11},{6,0},{7,13},{8,2},{9,15},{10,4},{12,6},{14,8},... | collective-permute-start | bytes 1572872 | tf_op jit(solution)/shard_map/ppermute | solution.py:255
  4.1 31.7 %collective-permute-start.3 = (bf16[1024,256]{1,0:T(8,128)(2,1)}, bf16[1024,256]{1,0:T(8,128)(2,1)S(1)}, u32[]{:S(2)}, u32[]{:S(2)}) collective-permute-start(bf16[1024,256]{1,0:T(8,128)(2,1)} %bitcast.9), channel_id=1, source_target_pairs={{1,5},{3,7},{4,0},{5,9},{6,2},{7,11},{8,4},{9,13},{10,6},{11,15},{... | collective-permute-start | bytes 1572872 | tf_op jit(solution)/shard_map/ppermute | solution.py:255
  6.1 49.0 %collective-permute-start.2 = (bf16[1024,256]{1,0:T(8,128)(2,1)}, bf16[1024,256]{1,0:T(8,128)(2,1)S(1)}, u32[]{:S(2)}, u32[]{:S(2)}) collective-permute-start(bf16[1024,256]{1,0:T(8,128)(2,1)} %bitcast.10), channel_id=1, source_target_pairs={{1,3},{2,0},{3,5},{4,2},{5,7},{6,4},{7,9},{8,6},{9,11},{10,8},{11,... | collective-permute-start | bytes 1572872 | tf_op jit(solution)/shard_map/ppermute | solution.py:255
  8.0 1.5 %collective-permute-start = (bf16[256,128]{1,0:T(8,128)(2,1)}, bf16[256,128]{1,0:T(8,128)(2,1)S(1)}, u32[]{:S(2)}, u32[]{:S(2)}) collective-permute-start(bf16[256,128]{1,0:T(8,128)(2,1)} %qk_ref.1), channel_id=1, source_target_pairs={{0,1},{1,0},{2,3},{3,2},{4,5},{5,4},{6,7},{7,6},{8,9},{9,8},{10,11... | collective-permute-start | bytes 196616 | tf_op jit(solution)/shard_map/ppermute | solution.py:245
  8.1 1.6 %collective-permute-start.1 = (bf16[256,128]{1,0:T(8,128)(2,1)}, bf16[256,128]{1,0:T(8,128)(2,1)S(1)}, u32[]{:S(2)}, u32[]{:S(2)}) collective-permute-start(bf16[256,128]{1,0:T(8,128)(2,1)} %value_ref.1), channel_id=1, source_target_pairs={{0,1},{1,0},{2,3},{3,2},{4,5},{5,4},{6,7},{7,6},{8,9},{9,8},{10,11... | collective-permute-start | bytes 196616 | tf_op jit(solution)/shard_map/ppermute | solution.py:246
  9.7 0.7 copy-start.9
  9.7 0.7 copy-start.8
  9.7 0.7 copy-start.7
  9.7 0.7 copy-start.6
  9.7 0.7 copy-start.10
  10.4 1.0 %copy-start.3 = (bf16[1,1024,256]{2,1,0:T(8,128)(2,1)S(1)}, bf16[1,1024,256]{2,1,0:T(8,128)(2,1)}, u32[]{:S(2)}) copy-start(bf16[1,1024,256]{2,1,0:T(8,128)(2,1)} %param.11) | copy-start | bytes 1572868
  11.5 0.8 %copy-start.4 = (bf16[256,128]{1,0:T(8,128)(2,1)S(1)}, bf16[256,128]{1,0:T(8,128)(2,1)}, u32[]{:S(2)}) copy-start(bf16[256,128]{1,0:T(8,128)(2,1)} %qk_ref.1) | copy-start | bytes 196612
  12.3 0.8 %copy-start.5 = (bf16[256,128]{1,0:T(8,128)(2,1)S(1)}, bf16[256,128]{1,0:T(8,128)(2,1)}, u32[]{:S(2)}) copy-start(bf16[256,128]{1,0:T(8,128)(2,1)} %value_ref.1) | copy-start | bytes 196612
  65.1 11.4 %collective-permute-start.5 = (bf16[256,512]{1,0:T(8,128)(2,1)S(1)}, bf16[256,512]{1,0:T(8,128)(2,1)S(1)}, u32[]{:S(2)}, u32[]{:S(2)}) collective-permute-start(bf16[256,512]{1,0:T(8,128)(2,1)S(1)} %get-tuple-element.30), channel_id=1, source_target_pairs={{0,1},{1,0},{2,3},{3,2},{4,5},{5,4},{6,7},{7,6},{8,9},{9,8},{10,11... | collective-permute-start | bytes 786440 | tf_op jit(solution)/shard_map/ppermute | solution.py:318
  66.9 9.6 %copy-start = (bf16[512,512]{1,0:T(8,128)(2,1)S(1)}, bf16[512,512]{1,0:T(8,128)(2,1)}, u32[]{:S(2)}) copy-start(bf16[512,512]{1,0:T(8,128)(2,1)} %mlp_ref.1) | copy-start | bytes 1572868
  66.9 9.6 %copy-start.1 = (bf16[512,256]{1,0:T(8,128)(2,1)S(1)}, bf16[512,256]{1,0:T(8,128)(2,1)}, u32[]{:S(2)}) copy-start(bf16[512,256]{1,0:T(8,128)(2,1)} %mlp_out_ref.1) | copy-start | bytes 786436
  66.9 9.6 %copy-start.2 = (bf16[256,256]{1,0:T(8,128)(2,1)S(1)}, bf16[256,256]{1,0:T(8,128)(2,1)}, u32[]{:S(2)}) copy-start(bf16[256,256]{1,0:T(8,128)(2,1)} %out_ref.1) | copy-start | bytes 393220

commit v5 on v3

--- a/solution.py
+++ b/solution.py
@@ -28,7 +28,7 @@
 
 def prologue_kernel(
     images, place_ref, links_ref, x_ref, qk_ref, value_ref, qk_other_ref, value_other_ref, gain_ref,
-    shift_ref, bias_ref, out_bias_ref, wk_ref, wvt_ref, queries_ref, facts_ref, vectors_ref,
+    shift_ref, bias_ref, out_bias_ref, wk_ref, wvt_ref, queries_ref, facts_ref, rows_ref, vectors_ref,
 ):
     rows, width = x_ref.shape
     local = width // 2
@@ -53,6 +53,8 @@
         entry = links_ref[step - 1, jnp.clip(lower, 0, images - 1)]
         linked = jnp.where(jnp.logical_and(inside, entry != 0), 1.0, 0.0)
         facts_ref[step : step + 1, :] = jnp.full((1, 128), linked, F32)
+    half = rows // 2
+    rows_ref[...] = x_ref[pl.ds(pl.multiple_of(sub * half, half), half), :]
     vectors_ref[0:1, :] = gain_ref[...]
     vectors_ref[1:2, :] = shift_ref[...]
     vectors_ref[2:3, :] = bias_ref[...]
@@ -129,7 +131,7 @@
         lax.fori_loop(0, HEADS * (span // tile), body, 0)
 
 
-def takes_other(place):
+def near_first(place):
     return lax.rem(place // 2, 2) == lax.rem(place, 2)
 
 
@@ -145,7 +147,7 @@
 
     @pl.when(linked)
     def _():
-        take = takes_other(place_ref[0])
+        take = near_first(place_ref[0])
         project(x_ref, other_ref, take, wk_ref, wvt_ref, keys_ref, values_ref)
         wide = rows // 2
 
@@ -174,7 +176,7 @@
 
     @pl.when(linked)
     def _():
-        project(x_ref, other_ref, takes_other(place), wk_ref, wvt_ref, keys_ref, values_ref)
+        project(x_ref, other_ref, near_first(place), wk_ref, wvt_ref, keys_ref, values_ref)
         attend(queries_ref, at, half, keys_ref, values_ref, message_ref, pl.ds(0, half))
         total = first_ref[:, here].astype(F32) + second_ref[:, here].astype(F32)
         send_ref[...] = (total + message_ref[...].astype(F32)).astype(BF16)
@@ -201,11 +203,10 @@
 
 
 def tail_kernel(
-    place_ref, keep_ref, came_ref, x_ref, out_ref, mlp_ref, vectors_ref, mlp_out_ref, result_ref
+    keep_ref, came_ref, rows_ref, out_ref, mlp_ref, vectors_ref, mlp_out_ref, result_ref
 ):
-    width, rows = keep_ref.shape
-    sub = lax.rem(place_ref[0], 2)
-    own_rows = x_ref[pl.ds(pl.multiple_of(sub * rows, rows), rows), :]
+    width = keep_ref.shape[0]
+    own_rows = rows_ref[...]
     hidden = dot(own_rows, mlp_ref[:width, :]) + vectors_ref[2:3, :]
     summed = (keep_ref[...] + came_ref[...].astype(F32)).astype(BF16)
     projected = dot(summed, out_ref[...], (0, 0)).astype(BF16)
@@ -251,40 +252,47 @@
     qk_other = lax.ppermute(qk_weight, "sub", swap)
     value_other = lax.ppermute(value_weight, "sub", swap)
 
-    def carried(value, moves):
+    def carried(value, source):
         pairs = []
         for image in range(images):
             for sub in range(2):
-                source = moves(image, sub)
-                if source is not None:
-                    pairs.append((2 * source[0] + source[1], 2 * image + sub))
+                origin = source(image, sub)
+                if origin is not None:
+                    pairs.append((2 * origin[0] + origin[1], 2 * image + sub))
         return lax.ppermute(value, RING, pairs)
 
     def ahead(image, sub, step):
         partner = image + step if sub == 0 else image - step
         return partner if 0 <= partner < images else None
 
+    def near(image, sub):
+        return image % 2 == sub
+
+    def within(image, sub):
+        return (image ^ 1, image % 2) if near(image, sub) else None
+
     def by_two(image, sub):
         partner = ahead(image, sub, 2)
         return None if partner is None else (partner, sub)
 
-    def within(image, sub):
-        return (image ^ 1, image % 2) if image % 2 == sub else None
-
-    def across(image, sub):
+    def outer(image, sub):
         partner = ahead(image, sub, 1)
-        return None if image % 2 == sub or partner is None else (image ^ 1, sub)
-
-    def onward(image, sub):
-        return None if ahead(image, sub, 3) is None else (ahead(image, sub, 2), sub)
-
-    def onward_inner(image, sub):
-        return onward(image, sub) if image % 2 == sub else None
-
-    def onward_outer(image, sub):
-        return None if image % 2 == sub else onward(image, sub)
-
+        return None if near(image, sub) or partner is None else (partner, 1 - sub)
+
+    def far_outer(image, sub):
+        partner = ahead(image, sub, 3)
+        if near(image, sub) or partner is None:
+            return None
+        return (partner ^ 1, (partner ^ 1) % 2)
+
+    def far_inner(image, sub):
+        if not near(image, sub) or ahead(image, sub, 3) is None:
+            return None
+        return (ahead(image, sub, 2), sub)
+
+    one_inner = carried(own, within)
     two = carried(own, by_two)
+    one_outer = carried(own, outer)
 
     def called(kernel, args, out_shape, scratch, cost_estimate, scalars=1):
         return pl.pallas_call(
@@ -297,7 +305,7 @@
             cost_estimate=cost_estimate,
         )(*args)
 
-    wk, wvt, queries, facts, vectors = called(
+    wk, wvt, queries, facts, own_half, vectors = called(
         functools.partial(prologue_kernel, images),
         [
             place, links.T, own, qk_weight, value_weight, qk_other, value_other,
@@ -309,6 +317,7 @@
             shape((width, width), BF16),
             shape((HEADS, rows, 128), BF16),
             shape((8, 128), F32),
+            shape((half, width), BF16),
             shape((8, hidden_width), F32),
         ],
         [],
@@ -316,40 +325,40 @@
         scalars=2,
     )
 
-    own_later, facts = lax.optimization_barrier((own, facts))
-    inner = carried(own_later, within)
-    outer = carried(two, across)
+    one_inner, facts = lax.optimization_barrier((one_inner, facts))
+    three_outer = carried(one_inner, far_outer)
+    three_inner = carried(one_inner, far_inner)
+
     projected = [
         shape((rows, width), BF16),
         shape((HEADS, width // HEADS + 16, rows), BF16),
     ]
     scratch = [pltpu.VMEM(x.shape, x.dtype) for x in projected]
-    message = [shape((width, rows), BF16)]
+    message_shape = [shape((width, rows), BF16)]
     work = cost(8 * rows * rows * width, 2 << 20, HEADS * rows * rows)
     half_work = cost(4 * rows * rows * width, 2 << 20, HEADS * rows * half)
-    (message_two,) = called(
+    (message,) = called(
         functools.partial(partner_kernel, 2, False),
         [place, queries, facts, two, wk, wvt],
-        message,
+        message_shape,
         scratch,
         work,
     )
-    outer, inner, message_two = lax.optimization_barrier((outer, inner, message_two))
-    outer_far = carried(outer, onward_outer)
-    inner_far = carried(inner, onward_inner)
-    (message_one,) = called(
+    one_outer, message = lax.optimization_barrier((one_outer, message))
+    messages = [message]
+    messages += called(
         functools.partial(partner_kernel, 1, True),
-        [place, queries, facts, outer, inner, wk, wvt],
-        message,
+        [place, queries, facts, one_outer, one_inner, wk, wvt],
+        message_shape,
         scratch,
         work,
     )
-    inner_far, outer_far, message_one = lax.optimization_barrier(
-        (inner_far, outer_far, message_one)
+    three_outer, three_inner, messages = lax.optimization_barrier(
+        (three_outer, three_inner, messages)
     )
     keys, values, send = called(
         functools.partial(last_kernel, 3),
-        [place, queries, facts, outer_far, inner_far, wk, wvt, message_two, message_one],
+        [place, queries, facts, three_outer, three_inner, wk, wvt, *messages],
         [*projected, shape((width, half), BF16)],
         [pltpu.VMEM((width, half), BF16)],
         half_work,
@@ -357,7 +366,7 @@
     came = lax.ppermute(send, "sub", swap)
     (keep,) = called(
         functools.partial(own_kernel, 3),
-        [place, queries, facts, keys, values, message_two, message_one],
+        [place, queries, facts, keys, values, *messages],
         [shape((width, half), F32)],
         [pltpu.VMEM((width, half), BF16)],
         half_work,
@@ -365,10 +374,11 @@
     came, keep = lax.optimization_barrier((came, keep))
     (result,) = called(
         tail_kernel,
-        [place, keep, came, own, out_weight, mlp_in, vectors, mlp_out],
+        [keep, came, own_half, out_weight, mlp_in, vectors, mlp_out],
         [shape((half, width), BF16)],
         [],
         cost(4 * rows * width * width, 4 << 20),
+        scalars=0,
     )
     return result[None]
 

time: 80.1 us -> 79.8 us (level)
  the two profiles are of different devices: /device:TPU:17 before, /device:TPU:8 now
where the time goes in v5:
time: 79.8 us; the launch traced here: 79.4 us
  Pallas kernels  60.9 us (76%)
  starting transfers between devices  13.4 us (17%)
  local copies, waits for them, and re-layouts  3.47 us (4%)
  waiting for transfers between devices  1.4 us (2%)
    pallas_call x6, Pallas kernels, called(): pl.pallas_call(kernel, in_specs=[SMEM] * scalars + [VMEM] * (len(args) -...  60.9 us
    ppermute x5, starting transfers between devices, carried(): return lax.ppermute(value, RING, pairs)  9.01 us
    ppermute x1, starting transfers between devices, on_device(): qk_other = lax.ppermute(qk_weight, 'sub', swap)  4.27 us
    unnamed x22, local copies, waits for them, and re-layouts  3.47 us
  transfers between devices with their start and end apart: 8, of which 2 were waited for; matrix products, arithmetic and copies ran while one was open for 0% of the time, Pallas kernels for 62%

profile of v5, /device:TPU:8, one launch (start us, length us, event | category | flops | bytes accessed | tf_op | source)
XLA Modules:
  0.0 79.4 jit_solution(15742932959799854127)
XLA Ops:
  0.0 1.3 %collective-permute-start.2 = (bf16[1024,256]{1,0:T(8,128)(2,1)}, bf16[1024,256]{1,0:T(8,128)(2,1)S(1)}, u32[]{:S(2)}, u32[]{:S(2)}) collective-permute-start(bf16[1024,256]{1,0:T(8,128)(2,1)} %bitcast.8), channel_id=1, source_target_pairs={{2,0},{1,3},{6,4},{5,7},{10,8},{9,11},{14,12},{13,15},{18,16},{17,... | collective-permute-start | bytes 1572872 | tf_op jit(solution)/shard_map/ppermute | solution.py:262
  1.3 1.9 %collective-permute-start.6 = (bf16[1024,256]{1,0:T(8,128)(2,1)}, bf16[1024,256]{1,0:T(8,128)(2,1)S(1)}, u32[]{:S(2)}, u32[]{:S(2)}) collective-permute-start(bf16[1024,256]{1,0:T(8,128)(2,1)} %bitcast.9), channel_id=1, source_target_pairs={{4,0},{6,2},{8,4},{1,5},{10,6},{3,7},{12,8},{5,9},{14,10},{7,11},{... | collective-permute-start | bytes 1572872 | tf_op jit(solution)/shard_map/ppermute | solution.py:262
  3.2 0.7 collective-permute-start.5
  3.9 4.3 %collective-permute-start = (bf16[256,128]{1,0:T(8,128)(2,1)}, bf16[256,128]{1,0:T(8,128)(2,1)S(1)}, u32[]{:S(2)}, u32[]{:S(2)}) collective-permute-start(bf16[256,128]{1,0:T(8,128)(2,1)} %qk_ref.1), channel_id=1, source_target_pairs={{0,1},{1,0},{2,3},{3,2},{4,5},{5,4},{6,7},{7,6},{8,9},{9,8},{10,11... | collective-permute-start | bytes 196616 | tf_op jit(solution)/shard_map/ppermute | solution.py:252
  8.2 0.1 collective-permute-start.1
  8.3 1.0 %collective-permute-done.qk_other_ref = bf16[256,128]{1,0:T(8,128)(2,1)S(1)} collective-permute-done((bf16[256,128]{1,0:T(8,128)(2,1)}, bf16[256,128]{1,0:T(8,128)(2,1)S(1)}, u32[]{:S(2)}, u32[]{:S(2)}) %collective-permute-start) | collective-permute-done | bytes 65568 | tf_op jit(solution)/shard_map/ppermute | solution.py:252
  9.3 0.4 collective-permute-done.1.value_other_ref
  9.7 0.0 copy-start.9
  9.7 0.0 copy-start.8
  9.7 0.0 copy-start.7
  9.7 0.0 copy-start.6
  9.7 0.0 copy-start.10
  9.7 0.7 copy-done.9
  10.3 0.0 copy-done.8
  10.3 0.0 copy-done.7
  10.4 0.0 copy-done.6
  10.4 0.0 copy-done.10
  10.4 0.0 copy-start.3
  10.4 1.0 %copy-done.3 = bf16[1,1024,256]{2,1,0:T(8,128)(2,1)S(1)} copy-done((bf16[1,1024,256]{2,1,0:T(8,128)(2,1)S(1)}, bf16[1,1024,256]{2,1,0:T(8,128)(2,1)}, u32[]{:S(2)}) %copy-start.3) | copy-done | bytes 524312
  11.4 0.0 copy-start.4
  11.4 0.8 %copy-done.4 = bf16[256,128]{1,0:T(8,128)(2,1)S(1)} copy-done((bf16[256,128]{1,0:T(8,128)(2,1)S(1)}, bf16[256,128]{1,0:T(8,128)(2,1)}, u32[]{:S(2)}) %copy-start.4) | copy-done | bytes 65560
  12.3 0.0 copy-start.5
  12.3 0.8 %copy-done.5 = bf16[256,128]{1,0:T(8,128)(2,1)S(1)} copy-done((bf16[256,128]{1,0:T(8,128)(2,1)S(1)}, bf16[256,128]{1,0:T(8,128)(2,1)}, u32[]{:S(2)}) %copy-start.5) | copy-done | bytes 65560
  13.1 0.9 %shard_map.109 = (bf16[256,256]{1,0:T(8,128)(2,1)S(1)}, bf16[256,256]{1,0:T(8,128)(2,1)S(1)}, bf16[4,1024,128]{2,1,0:T(8,128)(2,1)S(1)}, f32[8,128]{1,0:T(8,128)...) custom-call(s32[1]{0:T(128)} %bitcast.place_ref, s32[3,8]{1,0:T(4,128)S(1)} %bitcast.12, ...), custom_call_target="tpu_custom_call" | custom-call | flops 268435456 | bytes 4194304 | tf_op jit(solution)/shard_map/pallas_call | solution.py:298
  14.0 0.0 collective-permute-done.2.refs_0_
  14.0 1.9 %collective-permute-start.4 = (bf16[1024,256]{1,0:T(8,128)(2,1)S(1)}, bf16[1024,256]{1,0:T(8,128)(2,1)S(1)}, u32[]{:S(2)}, u32[]{:S(2)}) collective-permute-start(bf16[1024,256]{1,0:T(8,128)(2,1)S(1)} %collective-permute-done.2.refs_0_), channel_id=1, source_target_pairs={{4,0},{8,4},{3,7},{12,8},{7,11},{11,15},{20,16},{24,20},{19,23},{2... | collective-permute-start | bytes 1572872 | tf_op jit(solution)/shard_map/ppermute | solution.py:262
  16.0 3.2 %collective-permute-start.3 = (bf16[1024,256]{1,0:T(8,128)(2,1)S(1)}, bf16[1024,256]{1,0:T(8,128)(2,1)S(1)}, u32[]{:S(2)}, u32[]{:S(2)}) collective-permute-start(bf16[1024,256]{1,0:T(8,128)(2,1)S(1)} %collective-permute-done.2.refs_0_), channel_id=1, source_target_pairs={{11,2},{15,6},{0,9},{4,13},{27,18},{31,22},{16,25},{20,29}} | collective-permute-start | bytes 1572872 | tf_op jit(solution)/shard_map/ppermute | solution.py:262
  19.2 0.0 collective-permute-done.6.x_ref
  19.2 19.3 %shard_map.110.first_ref = bf16[256,1024]{1,0:T(8,128)(2,1)S(1)} custom-call(s32[1]{0:T(128)} %bitcast.place_ref, bf16[4,1024,128]{2,1,0:T(8,128)(2,1)S(1)} %get-tuple-element.24.queries_ref, f32[8,128]{1,0:T(8,128)S(1)} %get-tuple-element.26.facts_ref, bf16[1024,256]{1,0:T(8,128)(2,1)S(1)} %collective-permute-done.6.x_ref, ...), custom_call_target="tpu_custom_call" | custom-call | flops 2147483648 | bytes 2097152 | tf_op jit(solution)/shard_map/pallas_call | solution.py:298
  38.4 0.0 collective-permute-done.5.x_ref
  38.5 19.3 %shard_map.111.second_ref = bf16[256,1024]{1,0:T(8,128)(2,1)S(1)} custom-call(s32[1]{0:T(128)} %bitcast.place_ref, bf16[4,1024,128]{2,1,0:T(8,128)(2,1)S(1)} %get-tuple-element.24.queries_ref, f32[8,128]{1,0:T(8,128)S(1)} %get-tuple-element.26.facts_ref, bf16[1024,256]{1,0:T(8,128)(2,1)S(1)} %collective-permute-done.5.x_ref, ...), custom_call_target="tpu_custom_call" | custom-call | flops 2147483648 | bytes 2097152 | tf_op jit(solution)/shard_map/pallas_call | solution.py:298
  57.7 0.0 collective-permute-done.4.other_ref
  57.7 0.0 collective-permute-done.3.x_ref
  57.8 10.0 %shard_map.112 = (bf16[1024,256]{1,0:T(8,128)(2,1)S(1)}, bf16[4,80,1024]{2,1,0:T(8,128)(2,1)S(1)}, bf16[256,512]{1,0:T(8,128)(2,1)S(1)}) custom-call(s32[1]{0:T(128)} %bitcast.place_ref, bf16[4,1024,128]{2,1,0:T(8,128)(2,1)S(1)} %get-tuple-element.24.queries_ref, f32[8,128]{1,0:T(8,128)S(1)} %get-tuple-element.26.facts_ref, ...), custom_call_target="tpu_custom_call" | custom-call | flops 1073741824 | bytes 2097152 | tf_op jit(solution)/shard_map/pallas_call | solution.py:298
  67.8 0.1 collective-permute-start.7
  67.9 0.0 copy-start
  67.9 0.0 copy-start.1
  67.9 0.0 copy-start.2
  67.9 9.6 %shard_map.113.keep_ref = f32[256,512]{1,0:T(8,128)S(1)} custom-call(s32[1]{0:T(128)} %bitcast.place_ref, bf16[4,1024,128]{2,1,0:T(8,128)(2,1)S(1)} %get-tuple-element.24.queries_ref, f32[8,128]{1,0:T(8,128)S(1)} %get-tuple-element.26.facts_ref, bf16[1024,256]{1,0:T(8,128)(2,1)S(1)} %get-tuple-element.37.keys_ref, ...), custom_call_target="tpu_custom_call" | custom-call | flops 1073741824 | bytes 2097152 | tf_op jit(solution)/shard_map/pallas_call | solution.py:298
  77.5 0.0 collective-permute-done.7.came_ref
  77.5 0.0 copy-done
  77.5 0.0 copy-done.1
  77.5 0.0 copy-done.2
  77.5 1.9 %shard_map.114 = bf16[512,256]{1,0:T(8,128)(2,1)} custom-call(f32[256,512]{1,0:T(8,128)S(1)} %shard_map.113.keep_ref, bf16[256,512]{1,0:T(8,128)(2,1)S(1)} %collective-permute-done.7.came_ref, bf16[512,256]{1,0:T(8,128)(2,1)S(1)} %get-tuple-element.41.rows_ref, bf16[256,256]{1,0:T(8,128)(2,1)S(1)} %copy-done.2, bf16[512,512]{1,0:T(8,128)(2,1)S(1)} %copy-done, ...), custom_call_target="tpu_custom_call" | custom-call | flops 268435456 | bytes 4194304 | tf_op jit(solution)/shard_map/pallas_call | solution.py:298
Async XLA Ops:
  0.0 14.0 %collective-permute-start.2 = (bf16[1024,256]{1,0:T(8,128)(2,1)}, bf16[1024,256]{1,0:T(8,128)(2,1)S(1)}, u32[]{:S(2)}, u32[]{:S(2)}) collective-permute-start(bf16[1024,256]{1,0:T(8,128)(2,1)} %bitcast.8), channel_id=1, source_target_pairs={{2,0},{1,3},{6,4},{5,7},{10,8},{9,11},{14,12},{13,15},{18,16},{17,... | collective-permute-start | bytes 1572872 | tf_op jit(solution)/shard_map/ppermute | solution.py:262
  1.3 17.9 %collective-permute-start.6 = (bf16[1024,256]{1,0:T(8,128)(2,1)}, bf16[1024,256]{1,0:T(8,128)(2,1)S(1)}, u32[]{:S(2)}, u32[]{:S(2)}) collective-permute-start(bf16[1024,256]{1,0:T(8,128)(2,1)} %bitcast.9), channel_id=1, source_target_pairs={{4,0},{6,2},{8,4},{1,5},{10,6},{3,7},{12,8},{5,9},{14,10},{7,11},{... | collective-permute-start | bytes 1572872 | tf_op jit(solution)/shard_map/ppermute | solution.py:262
  3.2 35.2 %collective-permute-start.5 = (bf16[1024,256]{1,0:T(8,128)(2,1)}, bf16[1024,256]{1,0:T(8,128)(2,1)S(1)}, u32[]{:S(2)}, u32[]{:S(2)}) collective-permute-start(bf16[1024,256]{1,0:T(8,128)(2,1)} %bitcast.10), channel_id=1, source_target_pairs={{5,2},{2,5},{9,6},{6,9},{13,10},{10,13},{21,18},{18,21},{25,22},{2... | collective-permute-start | bytes 1572872 | tf_op jit(solution)/shard_map/ppermute | solution.py:262
  3.9 5.4 %collective-permute-start = (bf16[256,128]{1,0:T(8,128)(2,1)}, bf16[256,128]{1,0:T(8,128)(2,1)S(1)}, u32[]{:S(2)}, u32[]{:S(2)}) collective-permute-start(bf16[256,128]{1,0:T(8,128)(2,1)} %qk_ref.1), channel_id=1, source_target_pairs={{0,1},{1,0},{2,3},{3,2},{4,5},{5,4},{6,7},{7,6},{8,9},{9,8},{10,11... | collective-permute-start | bytes 196616 | tf_op jit(solution)/shard_map/ppermute | solution.py:252
  8.2 1.5 %collective-permute-start.1 = (bf16[256,128]{1,0:T(8,128)(2,1)}, bf16[256,128]{1,0:T(8,128)(2,1)S(1)}, u32[]{:S(2)}, u32[]{:S(2)}) collective-permute-start(bf16[256,128]{1,0:T(8,128)(2,1)} %value_ref.1), channel_id=1, source_target_pairs={{0,1},{1,0},{2,3},{3,2},{4,5},{5,4},{6,7},{7,6},{8,9},{9,8},{10,11... | collective-permute-start | bytes 196616 | tf_op jit(solution)/shard_map/ppermute | solution.py:253
  9.7 0.7 copy-start.9
  9.7 0.7 copy-start.8
  9.7 0.7 copy-start.7
  9.7 0.7 copy-start.6
  9.7 0.7 copy-start.10
  10.4 1.0 %copy-start.3 = (bf16[1,1024,256]{2,1,0:T(8,128)(2,1)S(1)}, bf16[1,1024,256]{2,1,0:T(8,128)(2,1)}, u32[]{:S(2)}) copy-start(bf16[1,1024,256]{2,1,0:T(8,128)(2,1)} %param.11) | copy-start | bytes 1572868
  11.4 0.8 %copy-start.4 = (bf16[256,128]{1,0:T(8,128)(2,1)S(1)}, bf16[256,128]{1,0:T(8,128)(2,1)}, u32[]{:S(2)}) copy-start(bf16[256,128]{1,0:T(8,128)(2,1)} %qk_ref.1) | copy-start | bytes 196612
  12.3 0.8 %copy-start.5 = (bf16[256,128]{1,0:T(8,128)(2,1)S(1)}, bf16[256,128]{1,0:T(8,128)(2,1)}, u32[]{:S(2)}) copy-start(bf16[256,128]{1,0:T(8,128)(2,1)} %value_ref.1) | copy-start | bytes 196612
  14.0 43.7 %collective-permute-start.4 = (bf16[1024,256]{1,0:T(8,128)(2,1)S(1)}, bf16[1024,256]{1,0:T(8,128)(2,1)S(1)}, u32[]{:S(2)}, u32[]{:S(2)}) collective-permute-start(bf16[1024,256]{1,0:T(8,128)(2,1)S(1)} %collective-permute-done.2.refs_0_), channel_id=1, source_target_pairs={{4,0},{8,4},{3,7},{12,8},{7,11},{11,15},{20,16},{24,20},{19,23},{2... | collective-permute-start | bytes 1572872 | tf_op jit(solution)/shard_map/ppermute | solution.py:262
  16.0 41.8 %collective-permute-start.3 = (bf16[1024,256]{1,0:T(8,128)(2,1)S(1)}, bf16[1024,256]{1,0:T(8,128)(2,1)S(1)}, u32[]{:S(2)}, u32[]{:S(2)}) collective-permute-start(bf16[1024,256]{1,0:T(8,128)(2,1)S(1)} %collective-permute-done.2.refs_0_), channel_id=1, source_target_pairs={{11,2},{15,6},{0,9},{4,13},{27,18},{31,22},{16,25},{20,29}} | collective-permute-start | bytes 1572872 | tf_op jit(solution)/shard_map/ppermute | solution.py:262
  67.8 9.7 %collective-permute-start.7 = (bf16[256,512]{1,0:T(8,128)(2,1)S(1)}, bf16[256,512]{1,0:T(8,128)(2,1)S(1)}, u32[]{:S(2)}, u32[]{:S(2)}) collective-permute-start(bf16[256,512]{1,0:T(8,128)(2,1)S(1)} %get-tuple-element.36), channel_id=1, source_target_pairs={{0,1},{1,0},{2,3},{3,2},{4,5},{5,4},{6,7},{7,6},{8,9},{9,8},{10,11... | collective-permute-start | bytes 786440 | tf_op jit(solution)/shard_map/ppermute | solution.py:366
  67.9 9.6 %copy-start = (bf16[512,512]{1,0:T(8,128)(2,1)S(1)}, bf16[512,512]{1,0:T(8,128)(2,1)}, u32[]{:S(2)}) copy-start(bf16[512,512]{1,0:T(8,128)(2,1)} %mlp_ref.1) | copy-start | bytes 1572868
  67.9 9.6 %copy-start.1 = (bf16[512,256]{1,0:T(8,128)(2,1)S(1)}, bf16[512,256]{1,0:T(8,128)(2,1)}, u32[]{:S(2)}) copy-start(bf16[512,256]{1,0:T(8,128)(2,1)} %mlp_out_ref.1) | copy-start | bytes 786436
  67.9 9.6 %copy-start.2 = (bf16[256,256]{1,0:T(8,128)(2,1)S(1)}, bf16[256,256]{1,0:T(8,128)(2,1)}, u32[]{:S(2)}) copy-start(bf16[256,256]{1,0:T(8,128)(2,1)} %out_ref.1) | copy-start | bytes 393220

commit v6 on v5

--- a/solution.py
+++ b/solution.py
@@ -27,7 +27,7 @@
 
 
 def prologue_kernel(
-    images, place_ref, links_ref, x_ref, qk_ref, value_ref, qk_other_ref, value_other_ref, gain_ref,
+    images, place_ref, links_ref, x_ref, own_ref, qk_other_ref, value_other_ref, gain_ref,
     shift_ref, bias_ref, out_bias_ref, wk_ref, wvt_ref, queries_ref, facts_ref, rows_ref, vectors_ref,
 ):
     rows, width = x_ref.shape
@@ -35,8 +35,8 @@
     sub = lax.rem(place_ref[0], 2)
     image = place_ref[0] // 2
     parts = []
-    for own_ref, other_ref in ((qk_ref, qk_other_ref), (value_ref, value_other_ref)):
-        own, other = own_ref[...], other_ref[...]
+    for i, other_ref in enumerate((qk_other_ref, value_other_ref)):
+        own, other = own_ref[:, i * local : (i + 1) * local], other_ref[...]
         parts.append(jnp.where(sub == 0, own, other))
         parts.append(jnp.where(sub == 0, other, own))
     wk_ref[:, :local], wk_ref[:, local:] = parts[0], parts[1]
@@ -248,6 +248,7 @@
     place = lax.axis_index(RING).reshape(1)
     params = pltpu.CompilerParams(vmem_limit_bytes=40 << 20)
 
+    own_weights = jnp.concatenate([qk_weight, value_weight], axis=1)
     swap = [(0, 1), (1, 0)]
     qk_other = lax.ppermute(qk_weight, "sub", swap)
     value_other = lax.ppermute(value_weight, "sub", swap)
@@ -292,7 +293,6 @@
 
     one_inner = carried(own, within)
     two = carried(own, by_two)
-    one_outer = carried(own, outer)
 
     def called(kernel, args, out_shape, scratch, cost_estimate, scalars=1):
         return pl.pallas_call(
@@ -308,7 +308,7 @@
     wk, wvt, queries, facts, own_half, vectors = called(
         functools.partial(prologue_kernel, images),
         [
-            place, links.T, own, qk_weight, value_weight, qk_other, value_other,
+            place, links.T, own, own_weights, qk_other, value_other,
             norm_gain.reshape(1, -1), norm_bias.reshape(1, -1), mlp_in_bias.reshape(1, -1),
             mlp_out_bias.reshape(1, -1),
         ],
@@ -325,6 +325,8 @@
         scalars=2,
     )
 
+    own_later, facts = lax.optimization_barrier((own, facts))
+    one_outer = carried(own_later, outer)
     one_inner, facts = lax.optimization_barrier((one_inner, facts))
     three_outer = carried(one_inner, far_outer)
     three_inner = carried(one_inner, far_inner)

time: 79.8 us -> 77.5 us (0.971)
  local copies, waits for them, and re-layouts: 3.47 us -> 0.75 us
  other arithmetic: 0 us -> 0.89 us
    unnamed x22 -> x16, local copies, waits for them, and re-layouts: 3.47 us -> 0.75 us
    ppermute x1, starting transfers between devices: 4.27 us -> 3.04 us  [on_device(): qk_other = lax.ppermute(qk_weight, 'sub', swap)]
    ppermute x1, waiting for transfers between devices: 1.03 us -> 0.14 us  [on_device(): qk_other = lax.ppermute(qk_weight, 'sub', swap)]
    concatenate x0 -> x1, other arithmetic: none -> 0.89 us  [on_device(): own_weights = jnp.concatenate([qk_weight, value_weight], axis=1)]
  transfers between devices with their start and end apart: 8 -> 8, of which waited for: 2 -> 3; matrix products, arithmetic and copies ran while one was open for 0% -> 1% of each run, Pallas kernels for 62% -> 64%
where the time goes in v6:
time: 77.5 us; the launch traced here: 77.2 us
  Pallas kernels  61.4 us (79%)
  starting transfers between devices  12.7 us (16%)
  waiting for transfers between devices  1.22 us (2%)
  other arithmetic  0.89 us (1%)
    pallas_call x6, Pallas kernels, called(): pl.pallas_call(kernel, in_specs=[SMEM] * scalars + [VMEM] * (len(args) -...  61.4 us
    ppermute x5, starting transfers between devices, carried(): return lax.ppermute(value, RING, pairs)  9.54 us
    ppermute x1, starting transfers between devices, on_device(): qk_other = lax.ppermute(qk_weight, 'sub', swap)  3.04 us
  transfers between devices with their start and end apart: 8, of which 3 were waited for; matrix products, arithmetic and copies ran while one was open for 1% of the time, Pallas kernels for 64%

profile of v6, /device:TPU:8, one launch (start us, length us, event | category | flops | bytes accessed | tf_op | source)
XLA Modules:
  0.0 77.2 jit_solution(8369785254820292942)
XLA Ops:
  0.0 1.3 %collective-permute-start.2 = (bf16[1024,256]{1,0:T(8,128)(2,1)}, bf16[1024,256]{1,0:T(8,128)(2,1)S(1)}, u32[]{:S(2)}, u32[]{:S(2)}) collective-permute-start(bf16[1024,256]{1,0:T(8,128)(2,1)} %bitcast.2.x_ref), channel_id=1, source_target_pairs={{2,0},{1,3},{6,4},{5,7},{10,8},{9,11},{14,12},{13,15},{18,16},{17,... | collective-permute-start | bytes 1572872 | tf_op jit(solution)/shard_map/ppermute | solution.py:263
  1.3 1.9 %collective-permute-start.6 = (bf16[1024,256]{1,0:T(8,128)(2,1)}, bf16[1024,256]{1,0:T(8,128)(2,1)S(1)}, u32[]{:S(2)}, u32[]{:S(2)}) collective-permute-start(bf16[1024,256]{1,0:T(8,128)(2,1)} %bitcast.2.x_ref), channel_id=1, source_target_pairs={{4,0},{6,2},{8,4},{1,5},{10,6},{3,7},{12,8},{5,9},{14,10},{7,11},{... | collective-permute-start | bytes 1572872 | tf_op jit(solution)/shard_map/ppermute | solution.py:263
  3.2 3.0 %collective-permute-start = (bf16[256,128]{1,0:T(8,128)(2,1)}, bf16[256,128]{1,0:T(8,128)(2,1)S(1)}, u32[]{:S(2)}, u32[]{:S(2)}) collective-permute-start(bf16[256,128]{1,0:T(8,128)(2,1)} %param.13), channel_id=1, source_target_pairs={{0,1},{1,0},{2,3},{3,2},{4,5},{5,4},{6,7},{7,6},{8,9},{9,8},{10,11... | collective-permute-start | bytes 196616 | tf_op jit(solution)/shard_map/ppermute | solution.py:253
  6.3 0.1 collective-permute-start.1
  6.3 0.9 %pad_maximum_fusion.own_ref = bf16[256,256]{1,0:T(8,128)(2,1)S(1)} fusion(bf16[256,128]{1,0:T(8,128)(2,1)} %param.14, bf16[256,128]{1,0:T(8,128)(2,1)} %param.13), kind=kLoop, calls=%fused_computation | loop fusion | flops 262144 | bytes 262144 | tf_op jit(solution)/shard_map/concatenate | solution.py:251
  7.2 0.1 collective-permute-done.qk_other_ref
  7.4 0.4 collective-permute-done.1.value_other_ref
  7.7 0.0 copy-start.6
  7.7 0.0 copy-start.4
  7.7 0.0 copy-start.5
  7.7 0.0 copy-start.3
  7.7 0.0 copy-start.7
  7.8 0.7 copy-done.6
  8.4 0.0 copy-done.4
  8.4 0.0 copy-done.5
  8.4 0.0 copy-done.3
  8.5 0.0 copy-done.7
  8.5 1.4 %shard_map.109 = (bf16[256,256]{1,0:T(8,128)(2,1)S(1)}, bf16[256,256]{1,0:T(8,128)(2,1)S(1)}, bf16[4,1024,128]{2,1,0:T(8,128)(2,1)S(1)}, f32[8,128]{1,0:T(8,128)...) custom-call(s32[1]{0:T(128)} %bitcast.place_ref, s32[3,8]{1,0:T(4,128)S(1)} %bitcast.8, ...), custom_call_target="tpu_custom_call" | custom-call | flops 268435456 | bytes 4194304 | tf_op jit(solution)/shard_map/pallas_call | solution.py:298
  9.9 0.7 collective-permute-start.5
  10.6 0.7 collective-permute-done.2.refs_0_
  11.3 1.9 %collective-permute-start.4 = (bf16[1024,256]{1,0:T(8,128)(2,1)S(1)}, bf16[1024,256]{1,0:T(8,128)(2,1)S(1)}, u32[]{:S(2)}, u32[]{:S(2)}) collective-permute-start(bf16[1024,256]{1,0:T(8,128)(2,1)S(1)} %collective-permute-done.2.refs_0_), channel_id=1, source_target_pairs={{4,0},{8,4},{3,7},{12,8},{7,11},{11,15},{20,16},{24,20},{19,23},{2... | collective-permute-start | bytes 1572872 | tf_op jit(solution)/shard_map/ppermute | solution.py:263
  13.2 3.7 %collective-permute-start.3 = (bf16[1024,256]{1,0:T(8,128)(2,1)S(1)}, bf16[1024,256]{1,0:T(8,128)(2,1)S(1)}, u32[]{:S(2)}, u32[]{:S(2)}) collective-permute-start(bf16[1024,256]{1,0:T(8,128)(2,1)S(1)} %collective-permute-done.2.refs_0_), channel_id=1, source_target_pairs={{11,2},{15,6},{0,9},{4,13},{27,18},{31,22},{16,25},{20,29}} | collective-permute-start | bytes 1572872 | tf_op jit(solution)/shard_map/ppermute | solution.py:263
  16.9 0.0 collective-permute-done.6.x_ref
  16.9 19.3 %shard_map.110.first_ref = bf16[256,1024]{1,0:T(8,128)(2,1)S(1)} custom-call(s32[1]{0:T(128)} %bitcast.place_ref, bf16[4,1024,128]{2,1,0:T(8,128)(2,1)S(1)} %get-tuple-element.26.queries_ref, f32[8,128]{1,0:T(8,128)S(1)} %get-tuple-element.29.facts_ref, bf16[1024,256]{1,0:T(8,128)(2,1)S(1)} %collective-permute-done.6.x_ref, ...), custom_call_target="tpu_custom_call" | custom-call | flops 2147483648 | bytes 2097152 | tf_op jit(solution)/shard_map/pallas_call | solution.py:298
  36.2 0.0 collective-permute-done.5.x_ref
  36.2 19.3 %shard_map.111.second_ref = bf16[256,1024]{1,0:T(8,128)(2,1)S(1)} custom-call(s32[1]{0:T(128)} %bitcast.place_ref, bf16[4,1024,128]{2,1,0:T(8,128)(2,1)S(1)} %get-tuple-element.26.queries_ref, f32[8,128]{1,0:T(8,128)S(1)} %get-tuple-element.29.facts_ref, bf16[1024,256]{1,0:T(8,128)(2,1)S(1)} %collective-permute-done.5.x_ref, ...), custom_call_target="tpu_custom_call" | custom-call | flops 2147483648 | bytes 2097152 | tf_op jit(solution)/shard_map/pallas_call | solution.py:298
  55.5 0.0 collective-permute-done.4.other_ref
  55.5 0.0 collective-permute-done.3.x_ref
  55.5 10.0 %shard_map.112 = (bf16[1024,256]{1,0:T(8,128)(2,1)S(1)}, bf16[4,80,1024]{2,1,0:T(8,128)(2,1)S(1)}, bf16[256,512]{1,0:T(8,128)(2,1)S(1)}) custom-call(s32[1]{0:T(128)} %bitcast.place_ref, bf16[4,1024,128]{2,1,0:T(8,128)(2,1)S(1)} %get-tuple-element.26.queries_ref, f32[8,128]{1,0:T(8,128)S(1)} %get-tuple-element.29.facts_ref, ...), custom_call_target="tpu_custom_call" | custom-call | flops 1073741824 | bytes 2097152 | tf_op jit(solution)/shard_map/pallas_call | solution.py:298
  65.5 0.1 collective-permute-start.7
  65.6 0.0 copy-start
  65.6 0.0 copy-start.1
  65.6 0.0 copy-start.2
  65.7 9.6 %shard_map.113.keep_ref = f32[256,512]{1,0:T(8,128)S(1)} custom-call(s32[1]{0:T(128)} %bitcast.place_ref, bf16[4,1024,128]{2,1,0:T(8,128)(2,1)S(1)} %get-tuple-element.26.queries_ref, f32[8,128]{1,0:T(8,128)S(1)} %get-tuple-element.29.facts_ref, bf16[1024,256]{1,0:T(8,128)(2,1)S(1)} %get-tuple-element.41.keys_ref, ...), custom_call_target="tpu_custom_call" | custom-call | flops 1073741824 | bytes 2097152 | tf_op jit(solution)/shard_map/pallas_call | solution.py:298
  75.2 0.0 collective-permute-done.7.came_ref
  75.2 0.0 copy-done
  75.3 0.0 copy-done.1
  75.3 0.0 copy-done.2
  75.3 1.9 %shard_map.114 = bf16[512,256]{1,0:T(8,128)(2,1)} custom-call(f32[256,512]{1,0:T(8,128)S(1)} %shard_map.113.keep_ref, bf16[256,512]{1,0:T(8,128)(2,1)S(1)} %collective-permute-done.7.came_ref, bf16[512,256]{1,0:T(8,128)(2,1)S(1)} %get-tuple-element.45.rows_ref, bf16[256,256]{1,0:T(8,128)(2,1)S(1)} %copy-done.2, bf16[512,512]{1,0:T(8,128)(2,1)S(1)} %copy-done, ...), custom_call_target="tpu_custom_call" | custom-call | flops 268435456 | bytes 4194304 | tf_op jit(solution)/shard_map/pallas_call | solution.py:298
Async XLA Ops:
  0.0 11.3 %collective-permute-start.2 = (bf16[1024,256]{1,0:T(8,128)(2,1)}, bf16[1024,256]{1,0:T(8,128)(2,1)S(1)}, u32[]{:S(2)}, u32[]{:S(2)}) collective-permute-start(bf16[1024,256]{1,0:T(8,128)(2,1)} %bitcast.2.x_ref), channel_id=1, source_target_pairs={{2,0},{1,3},{6,4},{5,7},{10,8},{9,11},{14,12},{13,15},{18,16},{17,... | collective-permute-start | bytes 1572872 | tf_op jit(solution)/shard_map/ppermute | solution.py:263
  1.3 15.7 %collective-permute-start.6 = (bf16[1024,256]{1,0:T(8,128)(2,1)}, bf16[1024,256]{1,0:T(8,128)(2,1)S(1)}, u32[]{:S(2)}, u32[]{:S(2)}) collective-permute-start(bf16[1024,256]{1,0:T(8,128)(2,1)} %bitcast.2.x_ref), channel_id=1, source_target_pairs={{4,0},{6,2},{8,4},{1,5},{10,6},{3,7},{12,8},{5,9},{14,10},{7,11},{... | collective-permute-start | bytes 1572872 | tf_op jit(solution)/shard_map/ppermute | solution.py:263
  3.2 4.2 %collective-permute-start = (bf16[256,128]{1,0:T(8,128)(2,1)}, bf16[256,128]{1,0:T(8,128)(2,1)S(1)}, u32[]{:S(2)}, u32[]{:S(2)}) collective-permute-start(bf16[256,128]{1,0:T(8,128)(2,1)} %param.13), channel_id=1, source_target_pairs={{0,1},{1,0},{2,3},{3,2},{4,5},{5,4},{6,7},{7,6},{8,9},{9,8},{10,11... | collective-permute-start | bytes 196616 | tf_op jit(solution)/shard_map/ppermute | solution.py:253
  6.3 1.5 %collective-permute-start.1 = (bf16[256,128]{1,0:T(8,128)(2,1)}, bf16[256,128]{1,0:T(8,128)(2,1)S(1)}, u32[]{:S(2)}, u32[]{:S(2)}) collective-permute-start(bf16[256,128]{1,0:T(8,128)(2,1)} %param.14), channel_id=1, source_target_pairs={{0,1},{1,0},{2,3},{3,2},{4,5},{5,4},{6,7},{7,6},{8,9},{9,8},{10,11... | collective-permute-start | bytes 196616 | tf_op jit(solution)/shard_map/ppermute | solution.py:254
  7.7 0.7 copy-start.6
  7.7 0.7 copy-start.4
  7.7 0.7 copy-start.5
  7.7 0.7 copy-start.3
  7.7 0.7 copy-start.7
  9.9 26.3 %collective-permute-start.5 = (bf16[1024,256]{1,0:T(8,128)(2,1)}, bf16[1024,256]{1,0:T(8,128)(2,1)S(1)}, u32[]{:S(2)}, u32[]{:S(2)}) collective-permute-start(bf16[1024,256]{1,0:T(8,128)(2,1)} %bitcast.2.x_ref), channel_id=1, source_target_pairs={{5,2},{2,5},{9,6},{6,9},{13,10},{10,13},{21,18},{18,21},{25,22},{2... | collective-permute-start | bytes 1572872 | tf_op jit(solution)/shard_map/ppermute | solution.py:263
  11.3 44.2 %collective-permute-start.4 = (bf16[1024,256]{1,0:T(8,128)(2,1)S(1)}, bf16[1024,256]{1,0:T(8,128)(2,1)S(1)}, u32[]{:S(2)}, u32[]{:S(2)}) collective-permute-start(bf16[1024,256]{1,0:T(8,128)(2,1)S(1)} %collective-permute-done.2.refs_0_), channel_id=1, source_target_pairs={{4,0},{8,4},{3,7},{12,8},{7,11},{11,15},{20,16},{24,20},{19,23},{2... | collective-permute-start | bytes 1572872 | tf_op jit(solution)/shard_map/ppermute | solution.py:263
  13.2 42.3 %collective-permute-start.3 = (bf16[1024,256]{1,0:T(8,128)(2,1)S(1)}, bf16[1024,256]{1,0:T(8,128)(2,1)S(1)}, u32[]{:S(2)}, u32[]{:S(2)}) collective-permute-start(bf16[1024,256]{1,0:T(8,128)(2,1)S(1)} %collective-permute-done.2.refs_0_), channel_id=1, source_target_pairs={{11,2},{15,6},{0,9},{4,13},{27,18},{31,22},{16,25},{20,29}} | collective-permute-start | bytes 1572872 | tf_op jit(solution)/shard_map/ppermute | solution.py:263
  65.5 9.7 %collective-permute-start.7 = (bf16[256,512]{1,0:T(8,128)(2,1)S(1)}, bf16[256,512]{1,0:T(8,128)(2,1)S(1)}, u32[]{:S(2)}, u32[]{:S(2)}) collective-permute-start(bf16[256,512]{1,0:T(8,128)(2,1)S(1)} %get-tuple-element.40), channel_id=1, source_target_pairs={{0,1},{1,0},{2,3},{3,2},{4,5},{5,4},{6,7},{7,6},{8,9},{9,8},{10,11... | collective-permute-start | bytes 786440 | tf_op jit(solution)/shard_map/ppermute | solution.py:368
  65.6 9.6 %copy-start = (bf16[512,512]{1,0:T(8,128)(2,1)S(1)}, bf16[512,512]{1,0:T(8,128)(2,1)}, u32[]{:S(2)}) copy-start(bf16[512,512]{1,0:T(8,128)(2,1)} %mlp_ref.1) | copy-start | bytes 1572868
  65.6 9.6 %copy-start.1 = (bf16[512,256]{1,0:T(8,128)(2,1)S(1)}, bf16[512,256]{1,0:T(8,128)(2,1)}, u32[]{:S(2)}) copy-start(bf16[512,256]{1,0:T(8,128)(2,1)} %mlp_out_ref.1) | copy-start | bytes 786436
  65.6 9.6 %copy-start.2 = (bf16[256,256]{1,0:T(8,128)(2,1)S(1)}, bf16[256,256]{1,0:T(8,128)(2,1)}, u32[]{:S(2)}) copy-start(bf16[256,256]{1,0:T(8,128)(2,1)} %out_ref.1) | copy-start | bytes 393220

commit v7 on v4

--- a/solution.py
+++ b/solution.py
@@ -27,7 +27,7 @@
 
 
 def prologue_kernel(
-    images, place_ref, links_ref, x_ref, qk_ref, value_ref, qk_other_ref, value_other_ref, gain_ref,
+    images, place_ref, links_ref, x_ref, own_ref, qk_other_ref, value_other_ref, gain_ref,
     shift_ref, bias_ref, out_bias_ref, wk_ref, wvt_ref, queries_ref, facts_ref, rows_ref, vectors_ref,
 ):
     rows, width = x_ref.shape
@@ -35,8 +35,8 @@
     sub = lax.rem(place_ref[0], 2)
     image = place_ref[0] // 2
     parts = []
-    for own_ref, other_ref in ((qk_ref, qk_other_ref), (value_ref, value_other_ref)):
-        own, other = own_ref[...], other_ref[...]
+    for i, other_ref in enumerate((qk_other_ref, value_other_ref)):
+        own, other = own_ref[:, i * local : (i + 1) * local], other_ref[...]
         parts.append(jnp.where(sub == 0, own, other))
         parts.append(jnp.where(sub == 0, other, own))
     wk_ref[:, :local], wk_ref[:, local:] = parts[0], parts[1]
@@ -76,29 +76,20 @@
             values_ref[head, head_width:, r : r + tile] = jnp.ones((16, tile), BF16)
 
 
-def attend(queries_ref, at, span, keys_ref, values_ref, message_ref, into):
+def weigh(queries_ref, at, span, keys_ref, values_ref, done):
     rows, width = keys_ref.shape
     head_width = width // HEADS
-    scale = 1.0 / math.sqrt(head_width)
+    scale = math.log2(math.e) / math.sqrt(head_width)
     tile = 256
     queries_at = pl.ds(pl.multiple_of(at, span), span)
-    totals = {}
-    wrong = []
+    sums = {}
 
     def finish(head, r, scores):
-        weights = jnp.exp2(scores * (scale * math.log2(math.e))).astype(BF16)
+        weights = jnp.exp2(scores * scale).astype(BF16)
         product = dot(values_ref[head, :, r : r + tile], weights)
-        total = product if r == 0 else totals[head] + product
-        totals[head] = total
+        sums[head] = product if r == 0 else sums[head] + product
         if r + tile == rows:
-            sums = total[head_width : head_width + 1]
-            message_ref[head * head_width : (head + 1) * head_width, into] = (
-                total[:head_width] * (1.0 / sums)
-            ).astype(BF16)
-            top = jnp.max(jnp.abs(total[:head_width]), axis=0, keepdims=True)
-            fine = jnp.logical_and(sums > LEAST_SUM, sums < LARGEST_SUM)
-            fine = jnp.logical_and(fine, top < LARGEST_PRODUCT)
-            wrong.append(jnp.where(fine, 0.0, 1.0))
+            done(head, sums[head])
 
     waiting = []
     for head in range(HEADS):
@@ -111,16 +102,43 @@
     for item in waiting:
         finish(*item)
 
+
+def attend(queries_ref, at, span, pieces, message_ref, into, before_ref=None):
+    width = pieces[0][0].shape[1]
+    head_width = width // HEADS
+    wrong = []
+
+    def done(head, sums):
+        if before_ref is not None:
+            sums = sums + before_ref[head, :, pl.ds(pl.multiple_of(at, span), span)]
+        total = sums[head_width : head_width + 1]
+        message_ref[head * head_width : (head + 1) * head_width, into] = (
+            sums[:head_width] * (1.0 / total)
+        ).astype(BF16)
+        top = jnp.max(jnp.abs(sums[:head_width]), axis=0, keepdims=True)
+        fine = jnp.logical_and(total > LEAST_SUM, total < LARGEST_SUM)
+        fine = jnp.logical_and(fine, top < LARGEST_PRODUCT)
+        wrong.append(jnp.where(fine, 0.0, 1.0))
+
+    weigh(queries_ref, at, span, *pieces[-1], done)
+
     @pl.when(jnp.max(sum(wrong)) > 0.0)
     def _():
+        tile = 256
+
         def body(i, carry):
             head, part = i // (span // tile), lax.rem(i, span // tile)
-            part_at = pl.ds(pl.multiple_of(at + part * tile, tile), tile)
+            queries = queries_ref[head, pl.ds(pl.multiple_of(at + part * tile, tile), tile), :]
             lanes = pl.ds(pl.multiple_of(head // 2 * 128, 128), 128)
-            scores = dot(keys_ref[:, lanes], queries_ref[head, part_at, :], (1, 1)) * scale
+            scores = [dot(keys_ref[:, lanes], queries, (1, 1)) for keys_ref, _ in pieces]
+            scores = jnp.concatenate(scores, axis=0) * (1.0 / math.sqrt(head_width))
             powers = jnp.exp(scores - jnp.max(scores, axis=0, keepdims=True))
-            weights = powers / jnp.sum(powers, axis=0, keepdims=True)
-            product = dot(values_ref[head, :head_width, :], weights.astype(BF16))
+            weights = (powers / jnp.sum(powers, axis=0, keepdims=True)).astype(BF16)
+            product, start = 0.0, 0
+            for keys_ref, values_ref in pieces:
+                stop = start + keys_ref.shape[0]
+                product = product + dot(values_ref[head, :head_width, :], weights[start:stop])
+                start = stop
             head_rows = pl.ds(pl.multiple_of(head * head_width, head_width), head_width)
             columns = pl.ds(pl.multiple_of(into.start + part * tile, tile), tile)
             message_ref[head_rows, columns] = product.astype(BF16)
@@ -129,11 +147,15 @@
         lax.fori_loop(0, HEADS * (span // tile), body, 0)
 
 
+def is_linked(facts_ref, step):
+    return jnp.max(facts_ref[step : step + 1, :]) > 0.0
+
+
 def partner_kernel(
     step, queries_ref, facts_ref, x_ref, wk_ref, wvt_ref, message_ref, keys_ref, values_ref
 ):
-    rows, _ = keys_ref.shape
-    linked = jnp.max(facts_ref[step : step + 1, :]) > 0.0
+    rows = keys_ref.shape[0]
+    linked = is_linked(facts_ref, step)
 
     @pl.when(jnp.logical_not(linked))
     def _():
@@ -146,43 +168,64 @@
 
         def body(i, carry):
             at = pl.multiple_of(i * wide, wide)
-            attend(queries_ref, at, wide, keys_ref, values_ref, message_ref, pl.ds(at, wide))
+            pieces = [(keys_ref, values_ref)]
+            attend(queries_ref, at, wide, pieces, message_ref, pl.ds(at, wide))
             return carry
 
         lax.fori_loop(0, rows // wide, body, 0)
 
 
-def last_kernel(
-    step, place_ref, queries_ref, facts_ref, x_ref, wk_ref, wvt_ref, first_ref, second_ref,
-    keys_ref, values_ref, send_ref, message_ref,
+def first_half_kernel(
+    step, queries_ref, facts_ref, x_ref, wk_ref, wvt_ref, keys_ref, values_ref, sums_ref
+):
+    @pl.when(is_linked(facts_ref, step))
+    def _():
+        project(x_ref, wk_ref, wvt_ref, keys_ref, values_ref)
+        wide = keys_ref.shape[0]
+
+        def body(i, carry):
+            at = pl.multiple_of(i * wide, wide)
+
+            def done(head, sums):
+                sums_ref[head, :, pl.ds(at, wide)] = sums
+
+            weigh(queries_ref, at, wide, keys_ref, values_ref, done)
+            return carry
+
+        lax.fori_loop(0, sums_ref.shape[2] // wide, body, 0)
+
+
+def second_half_kernel(
+    step, place_ref, queries_ref, facts_ref, x_ref, wk_ref, wvt_ref, keys_before_ref,
+    values_before_ref, sums_ref, first_ref, second_ref, keys_ref, values_ref, send_ref, message_ref,
 ):
     half = message_ref.shape[1]
-    place = place_ref[0]
-    at = pl.multiple_of((1 - lax.rem(place, 2)) * half, half)
+    at = pl.multiple_of((1 - lax.rem(place_ref[0], 2)) * half, half)
     here = pl.ds(at, half)
-    linked = jnp.max(facts_ref[step : step + 1, :]) > 0.0
-    total = first_ref[:, here].astype(F32) + second_ref[:, here].astype(F32)
+    linked = is_linked(facts_ref, step)
 
     @pl.when(jnp.logical_not(linked))
     def _():
+        total = first_ref[:, here].astype(F32) + second_ref[:, here].astype(F32)
         send_ref[...] = total.astype(BF16)
 
     @pl.when(linked)
     def _():
         project(x_ref, wk_ref, wvt_ref, keys_ref, values_ref)
-        attend(queries_ref, at, half, keys_ref, values_ref, message_ref, pl.ds(0, half))
+        pieces = [(keys_before_ref, values_before_ref), (keys_ref, values_ref)]
+        attend(queries_ref, at, half, pieces, message_ref, pl.ds(0, half), sums_ref)
         total = first_ref[:, here].astype(F32) + second_ref[:, here].astype(F32)
         send_ref[...] = (total + message_ref[...].astype(F32)).astype(BF16)
 
 
 def own_kernel(
-    step, place_ref, queries_ref, facts_ref, keys_ref, values_ref, first_ref, second_ref, keep_ref,
-    message_ref,
+    step, place_ref, queries_ref, facts_ref, keys_before_ref, values_before_ref, sums_ref, keys_ref,
+    values_ref, first_ref, second_ref, keep_ref, message_ref,
 ):
     half = message_ref.shape[1]
     at = pl.multiple_of(lax.rem(place_ref[0], 2) * half, half)
     here = pl.ds(at, half)
-    linked = jnp.max(facts_ref[step : step + 1, :]) > 0.0
+    linked = is_linked(facts_ref, step)
 
     @pl.when(jnp.logical_not(linked))
     def _():
@@ -190,7 +233,8 @@
 
     @pl.when(linked)
     def _():
-        attend(queries_ref, at, half, keys_ref, values_ref, message_ref, pl.ds(0, half))
+        pieces = [(keys_before_ref, values_before_ref), (keys_ref, values_ref)]
+        attend(queries_ref, at, half, pieces, message_ref, pl.ds(0, half), sums_ref)
         total = first_ref[:, here].astype(F32) + second_ref[:, here].astype(F32)
         keep_ref[...] = total + message_ref[...].astype(F32)
 
@@ -241,20 +285,24 @@
     place = lax.axis_index(RING).reshape(1)
     params = pltpu.CompilerParams(vmem_limit_bytes=40 << 20)
 
+    own_weights = jnp.concatenate([qk_weight, value_weight], axis=1)
     swap = [(0, 1), (1, 0)]
     qk_other = lax.ppermute(qk_weight, "sub", swap)
     value_other = lax.ppermute(value_weight, "sub", swap)
 
-    def fetched(step):
+    def fetched(value, step):
         pairs = []
         for image in range(images):
             if image >= step:
                 pairs.append((2 * image, 2 * (image - step)))
             if image + step < images:
                 pairs.append((2 * image + 1, 2 * (image + step) + 1))
-        return lax.ppermute(own, RING, pairs)
-
-    three, two, one = (fetched(step) for step in (3, 2, 1))
+        return lax.ppermute(value, RING, pairs)
+
+    three, two = fetched(own, 3), fetched(own, 2)
+    own_later, qk_other = lax.optimization_barrier((own, qk_other))
+    one_first = fetched(own_later[:half], 1)
+    one_second = fetched(own_later[half:], 1)
 
     def called(kernel, args, out_shape, scratch, cost_estimate, scalars=1):
         return pl.pallas_call(
@@ -270,7 +318,7 @@
     wk, wvt, queries, facts, own_half, vectors = called(
         functools.partial(prologue_kernel, images),
         [
-            place, links.T, own, qk_weight, value_weight, qk_other, value_other,
+            place, links.T, own, own_weights, qk_other, value_other,
             norm_gain.reshape(1, -1), norm_bias.reshape(1, -1), mlp_in_bias.reshape(1, -1),
             mlp_out_bias.reshape(1, -1),
         ],
@@ -287,14 +335,17 @@
         scalars=2,
     )
 
-    projected = [
-        shape((rows, width), BF16),
-        shape((HEADS, width // HEADS + 16, rows), BF16),
-    ]
-    scratch = [pltpu.VMEM(x.shape, x.dtype) for x in projected]
+    def projected(count):
+        return [
+            shape((count, width), BF16),
+            shape((HEADS, width // HEADS + 16, count), BF16),
+        ]
+
+    scratch = [pltpu.VMEM(x.shape, x.dtype) for x in projected(rows)]
     message = [shape((width, rows), BF16)]
     work = cost(8 * rows * rows * width, 2 << 20, HEADS * rows * rows)
     half_work = cost(4 * rows * rows * width, 2 << 20, HEADS * rows * half)
+    last_work = cost(2 * rows * rows * width, 2 << 20, HEADS * half * half)
     messages = []
     for step, partner in ((3, three), (2, two)):
         if messages:
@@ -307,21 +358,30 @@
             work,
             scalars=0,
         )
-    one, messages = lax.optimization_barrier((one, messages))
+    one_first, messages = lax.optimization_barrier((one_first, messages))
+    before = called(
+        functools.partial(first_half_kernel, 1),
+        [queries, facts, one_first, wk, wvt],
+        [*projected(half), shape((HEADS, width // HEADS + 16, rows), F32)],
+        [],
+        half_work,
+        scalars=0,
+    )
+    one_second, before = lax.optimization_barrier((one_second, before))
     keys, values, send = called(
-        functools.partial(last_kernel, 1),
-        [place, queries, facts, one, wk, wvt, *messages],
-        [*projected, shape((width, half), BF16)],
+        functools.partial(second_half_kernel, 1),
+        [place, queries, facts, one_second, wk, wvt, *before, *messages],
+        [*projected(half), shape((width, half), BF16)],
         [pltpu.VMEM((width, half), BF16)],
-        half_work,
+        last_work,
     )
     came = lax.ppermute(send, "sub", swap)
     (keep,) = called(
         functools.partial(own_kernel, 1),
-        [place, queries, facts, keys, values, *messages],
+        [place, queries, facts, *before, keys, values, *messages],
         [shape((width, half), F32)],
         [pltpu.VMEM((width, half), BF16)],
-        half_work,
+        last_work,
     )
     came, keep = lax.optimization_barrier((came, keep))
     (result,) = called(

time: 80 us -> 80.6 us (level)
  starting transfers between devices: 10.4 us -> 14.7 us
  waiting for transfers between devices: 3.61 us -> 0.83 us
  local copies, waits for them, and re-layouts: 3.46 us -> 1.1 us
  other arithmetic: 0 us -> 0.89 us
    ppermute x3 -> x4, starting transfers between devices: 7.96 us -> 12.3 us  [fetched(): return lax.ppermute(value, RING, pairs)]
    unnamed x22 -> x18, local copies, waits for them, and re-layouts: 3.46 us -> 0.03 us
    ppermute x3 -> x4, waiting for transfers between devices: 2.49 us -> 0.77 us  [fetched(): return lax.ppermute(value, RING, pairs)]
    slice x0 -> x1, local copies, waits for them, and re-layouts: none -> 1.06 us  [on_device(): one_first = fetched(own_later[:half], 1)]
    ppermute x1, waiting for transfers between devices: 0.95 us -> 0.06 us  [on_device(): qk_other = lax.ppermute(qk_weight, 'sub', swap)]
    concatenate x0 -> x1, other arithmetic: none -> 0.89 us  [on_device(): own_weights = jnp.concatenate([qk_weight, value_weight], axis=1)]
    pallas_call x6 -> x7, Pallas kernels: 60.9 us -> 61.4 us  [called(): pl.pallas_call(kernel, in_specs=[SMEM] * scalars + [VMEM] * (len(args) -...]
  transfers between devices with their start and end apart: 6 -> 7, of which waited for: 3 -> 2; matrix products, arithmetic and copies ran while one was open for 0% -> 2% of each run, Pallas kernels for 62% -> 64%
where the time goes in v7:
time: 80.6 us; the launch traced here: 79.1 us
  Pallas kernels  61.4 us (76%)
  starting transfers between devices  14.7 us (18%)
  local copies, waits for them, and re-layouts  1.1 us (1%)
  other arithmetic  0.89 us (1%)
  waiting for transfers between devices  0.83 us (1%)
    pallas_call x7, Pallas kernels, called(): pl.pallas_call(kernel, in_specs=[SMEM] * scalars + [VMEM] * (len(args) -...  61.4 us
    ppermute x4, starting transfers between devices, fetched(): return lax.ppermute(value, RING, pairs)  12.3 us
    ppermute x1, starting transfers between devices, on_device(): came = lax.ppermute(send, 'sub', swap)  1.83 us
  transfers between devices with their start and end apart: 7, of which 2 were waited for; matrix products, arithmetic and copies ran while one was open for 2% of the time, Pallas kernels for 64%

profile of v7, /device:TPU:17, one launch (start us, length us, event | category | flops | bytes accessed | tf_op | source)
XLA Modules:
  0.0 79.1 jit_solution(16688019254997732819)
XLA Ops:
  0.0 0.0 copy-start.1
  0.0 0.0 copy-start.8
  0.0 0.0 copy-start.6
  0.0 0.0 copy-start.5
  0.0 0.0 copy-start.7
  0.0 0.0 copy-start.4
  0.0 4.3 %collective-permute-start.5 = (bf16[1024,256]{1,0:T(8,128)(2,1)}, bf16[1024,256]{1,0:T(8,128)(2,1)S(1)}, u32[]{:S(2)}, u32[]{:S(2)}) collective-permute-start(bf16[1024,256]{1,0:T(8,128)(2,1)} %bitcast.8), channel_id=1, source_target_pairs={{1,7},{3,9},{5,11},{6,0},{7,13},{8,2},{9,15},{10,4},{12,6},{14,8},... | collective-permute-start | bytes 1572872 | tf_op jit(solution)/shard_map/ppermute | solution.py:300
  4.3 1.9 %collective-permute-start.4 = (bf16[1024,256]{1,0:T(8,128)(2,1)}, bf16[1024,256]{1,0:T(8,128)(2,1)S(1)}, u32[]{:S(2)}, u32[]{:S(2)}) collective-permute-start(bf16[1024,256]{1,0:T(8,128)(2,1)} %bitcast.9), channel_id=1, source_target_pairs={{1,5},{3,7},{4,0},{5,9},{6,2},{7,11},{8,4},{9,13},{10,6},{11,15},{... | collective-permute-start | bytes 1572872 | tf_op jit(solution)/shard_map/ppermute | solution.py:300
  6.2 0.1 collective-permute-start
  6.3 0.5 collective-permute-start.1
  6.8 0.9 %pad_maximum_fusion.own_ref = bf16[256,256]{1,0:T(8,128)(2,1)S(1)} fusion(bf16[256,128]{1,0:T(8,128)(2,1)} %param.14, bf16[256,128]{1,0:T(8,128)(2,1)} %param.13), kind=kLoop, calls=%fused_computation | loop fusion | flops 262144 | bytes 262144 | tf_op jit(solution)/shard_map/concatenate | solution.py:288
  7.7 0.1 collective-permute-done.qk_other_ref
  7.8 1.1 %fusion = (bf16[512,256]{1,0:T(8,128)(2,1)S(1)}, bf16[512,256]{1,0:T(8,128)(2,1)S(1)}) fusion(bf16[1024,256]{1,0:T(8,128)(2,1)} %bitcast.10), kind=kLoop, calls=%fused_computation.1 | loop fusion | bytes 1048576 | tf_op jit(solution)/shard_map/slice | solution.py:304
  8.8 1.9 %collective-permute-start.3 = (bf16[512,256]{1,0:T(8,128)(2,1)S(1)}, bf16[512,256]{1,0:T(8,128)(2,1)S(1)}, u32[]{:S(2)}, u32[]{:S(2)}) collective-permute-start(bf16[512,256]{1,0:T(8,128)(2,1)S(1)} %get-tuple-element.55), channel_id=1, source_target_pairs={{1,3},{2,0},{3,5},{4,2},{5,7},{6,4},{7,9},{8,6},{9,11},{10,8},{11,... | collective-permute-start | bytes 786440 | tf_op jit(solution)/shard_map/ppermute | solution.py:300
  10.8 4.2 %collective-permute-start.2 = (bf16[512,256]{1,0:T(8,128)(2,1)S(1)}, bf16[512,256]{1,0:T(8,128)(2,1)S(1)}, u32[]{:S(2)}, u32[]{:S(2)}) collective-permute-start(bf16[512,256]{1,0:T(8,128)(2,1)S(1)} %get-tuple-element.56), channel_id=1, source_target_pairs={{1,3},{2,0},{3,5},{4,2},{5,7},{6,4},{7,9},{8,6},{9,11},{10,8},{11,... | collective-permute-start | bytes 786440 | tf_op jit(solution)/shard_map/ppermute | solution.py:300
  15.0 0.0 collective-permute-done.1.value_other_ref
  15.0 0.0 copy-done.1
  15.0 0.0 copy-done.8
  15.0 0.0 copy-done.6
  15.0 0.0 copy-done.5
  15.0 0.0 copy-done.7
  15.0 0.0 copy-done.4
  15.1 0.9 %shard_map.109 = (bf16[256,256]{1,0:T(8,128)(2,1)S(1)}, bf16[256,256]{1,0:T(8,128)(2,1)S(1)}, bf16[4,1024,128]{2,1,0:T(8,128)(2,1)S(1)}, f32[8,128]{1,0:T(8,128)...) custom-call(s32[1]{0:T(128)} %bitcast.place_ref, s32[3,8]{1,0:T(4,128)S(1)} %bitcast.12, ...), custom_call_target="tpu_custom_call" | custom-call | flops 268435456 | bytes 4194304 | tf_op jit(solution)/shard_map/pallas_call | solution.py:308
  16.0 0.8 collective-permute-done.5.x_ref
  16.7 19.3 %shard_map.110.first_ref = bf16[256,1024]{1,0:T(8,128)(2,1)S(1)} custom-call(bf16[4,1024,128]{2,1,0:T(8,128)(2,1)S(1)} %get-tuple-element.31.queries_ref, f32[8,128]{1,0:T(8,128)S(1)} %get-tuple-element.32.facts_ref, bf16[1024,256]{1,0:T(8,128)(2,1)S(1)} %collective-permute-done.5.x_ref, bf16[256,256]{1,0:T(8,128)(2,1)S(1)} %get-tuple-element.34.wk_ref, ...), custom_call_target="tpu_custom_call" | custom-call | flops 2147483648 | bytes 2097152 | tf_op jit(solution)/shard_map/pallas_call | solution.py:308
  36.1 0.0 collective-permute-done.4.x_ref
  36.1 19.3 %shard_map.111.second_ref = bf16[256,1024]{1,0:T(8,128)(2,1)S(1)} custom-call(bf16[4,1024,128]{2,1,0:T(8,128)(2,1)S(1)} %get-tuple-element.31.queries_ref, f32[8,128]{1,0:T(8,128)S(1)} %get-tuple-element.32.facts_ref, bf16[1024,256]{1,0:T(8,128)(2,1)S(1)} %collective-permute-done.4.x_ref, bf16[256,256]{1,0:T(8,128)(2,1)S(1)} %get-tuple-element.34.wk_ref, ...), custom_call_target="tpu_custom_call" | custom-call | flops 2147483648 | bytes 2097152 | tf_op jit(solution)/shard_map/pallas_call | solution.py:308
  55.4 0.0 collective-permute-done.3.x_ref
  55.4 2.7 %shard_map.112 = (bf16[512,256]{1,0:T(8,128)(2,1)S(1)}, bf16[4,80,512]{2,1,0:T(8,128)(2,1)S(1)}, f32[4,80,1024]{2,1,0:T(8,128)S(1)}) custom-call(bf16[4,1024,128]{2,1,0:T(8,128)(2,1)S(1)} %get-tuple-element.31.queries_ref, f32[8,128]{1,0:T(8,128)S(1)} %get-tuple-element.32.facts_ref, bf16[512,256]{1,0:T(8,128)(2,1)S(1)} %collective-permute-done.3.x_ref, ...), custom_call_target="tpu_custom_call" | custom-call | flops 1073741824 | bytes 2097152 | tf_op jit(solution)/shard_map/pallas_call | solution.py:308
  58.1 0.0 collective-permute-done.2.x_ref
  58.2 8.7 %shard_map.113 = (bf16[512,256]{1,0:T(8,128)(2,1)S(1)}, bf16[4,80,512]{2,1,0:T(8,128)(2,1)S(1)}, bf16[256,512]{1,0:T(8,128)(2,1)S(1)}) custom-call(s32[1]{0:T(128)} %bitcast.place_ref, bf16[4,1024,128]{2,1,0:T(8,128)(2,1)S(1)} %get-tuple-element.31.queries_ref, f32[8,128]{1,0:T(8,128)S(1)} %get-tuple-element.32.facts_ref, ...), custom_call_target="tpu_custom_call" | custom-call | flops 536870912 | bytes 2097152 | tf_op jit(solution)/shard_map/pallas_call | solution.py:308
  66.8 1.8 %collective-permute-start.6 = (bf16[256,512]{1,0:T(8,128)(2,1)S(1)}, bf16[256,512]{1,0:T(8,128)(2,1)S(1)}, u32[]{:S(2)}, u32[]{:S(2)}) collective-permute-start(bf16[256,512]{1,0:T(8,128)(2,1)S(1)} %get-tuple-element.48), channel_id=1, source_target_pairs={{0,1},{1,0},{2,3},{3,2},{4,5},{5,4},{6,7},{7,6},{8,9},{9,8},{10,11... | collective-permute-start | bytes 786440 | tf_op jit(solution)/shard_map/ppermute | solution.py:378
  68.7 0.0 copy-start
  68.7 0.0 copy-start.2
  68.7 0.0 copy-start.3
  68.7 8.5 %shard_map.114.keep_ref = f32[256,512]{1,0:T(8,128)S(1)} custom-call(s32[1]{0:T(128)} %bitcast.place_ref, bf16[4,1024,128]{2,1,0:T(8,128)(2,1)S(1)} %get-tuple-element.31.queries_ref, f32[8,128]{1,0:T(8,128)S(1)} %get-tuple-element.32.facts_ref, bf16[512,256]{1,0:T(8,128)(2,1)S(1)} %get-tuple-element.43.keys_before_ref, ...), custom_call_target="tpu_custom_call" | custom-call | flops 536870912 | bytes 2097152 | tf_op jit(solution)/shard_map/pallas_call | solution.py:308
  77.2 0.0 collective-permute-done.6.came_ref
  77.2 0.0 copy-done
  77.2 0.0 copy-done.2
  77.2 0.0 copy-done.3
  77.2 1.9 %shard_map.115 = bf16[512,256]{1,0:T(8,128)(2,1)} custom-call(f32[256,512]{1,0:T(8,128)S(1)} %shard_map.114.keep_ref, bf16[256,512]{1,0:T(8,128)(2,1)S(1)} %collective-permute-done.6.came_ref, bf16[512,256]{1,0:T(8,128)(2,1)S(1)} %get-tuple-element.53.rows_ref, bf16[256,256]{1,0:T(8,128)(2,1)S(1)} %copy-done.3, bf16[512,512]{1,0:T(8,128)(2,1)S(1)} %copy-done, ...), custom_call_target="tpu_custom_call" | custom-call | flops 268435456 | bytes 4194304 | tf_op jit(solution)/shard_map/pallas_call | solution.py:308
Async XLA Ops:
  0.0 15.0 %copy-start.1 = (bf16[1,1024,256]{2,1,0:T(8,128)(2,1)S(1)}, bf16[1,1024,256]{2,1,0:T(8,128)(2,1)}, u32[]{:S(2)}) copy-start(bf16[1,1024,256]{2,1,0:T(8,128)(2,1)} %param.11) | copy-start | bytes 1572868
  0.0 15.0 %copy-start.8 = (f32[256]{0:T(256)S(1)}, f32[256]{0:T(256)}, u32[]{:S(2)}) copy-start(f32[256]{0:T(256)} %param.21) | copy-start | bytes 3076
  0.0 15.0 %copy-start.6 = (f32[512]{0:T(512)S(1)}, f32[512]{0:T(512)}, u32[]{:S(2)}) copy-start(f32[512]{0:T(512)} %param.19) | copy-start | bytes 6148
  0.0 15.0 %copy-start.5 = (f32[512]{0:T(512)S(1)}, f32[512]{0:T(512)}, u32[]{:S(2)}) copy-start(f32[512]{0:T(512)} %param.18) | copy-start | bytes 6148
  0.0 15.0 %copy-start.7 = (f32[512]{0:T(512)S(1)}, f32[512]{0:T(512)}, u32[]{:S(2)}) copy-start(f32[512]{0:T(512)} %param.17) | copy-start | bytes 6148
  0.0 15.0 %copy-start.4 = (s32[8,3]{0,1:T(4,128)S(1)}, s32[8,3]{0,1:T(4,128)}, u32[]{:S(2)}) copy-start(s32[8,3]{0,1:T(4,128)} %param.12) | copy-start | bytes 292
  0.0 16.7 %collective-permute-start.5 = (bf16[1024,256]{1,0:T(8,128)(2,1)}, bf16[1024,256]{1,0:T(8,128)(2,1)S(1)}, u32[]{:S(2)}, u32[]{:S(2)}) collective-permute-start(bf16[1024,256]{1,0:T(8,128)(2,1)} %bitcast.8), channel_id=1, source_target_pairs={{1,7},{3,9},{5,11},{6,0},{7,13},{8,2},{9,15},{10,4},{12,6},{14,8},... | collective-permute-start | bytes 1572872 | tf_op jit(solution)/shard_map/ppermute | solution.py:300
  4.3 31.8 %collective-permute-start.4 = (bf16[1024,256]{1,0:T(8,128)(2,1)}, bf16[1024,256]{1,0:T(8,128)(2,1)S(1)}, u32[]{:S(2)}, u32[]{:S(2)}) collective-permute-start(bf16[1024,256]{1,0:T(8,128)(2,1)} %bitcast.9), channel_id=1, source_target_pairs={{1,5},{3,7},{4,0},{5,9},{6,2},{7,11},{8,4},{9,13},{10,6},{11,15},{... | collective-permute-start | bytes 1572872 | tf_op jit(solution)/shard_map/ppermute | solution.py:300
  6.2 1.5 %collective-permute-start = (bf16[256,128]{1,0:T(8,128)(2,1)}, bf16[256,128]{1,0:T(8,128)(2,1)S(1)}, u32[]{:S(2)}, u32[]{:S(2)}) collective-permute-start(bf16[256,128]{1,0:T(8,128)(2,1)} %param.13), channel_id=1, source_target_pairs={{0,1},{1,0},{2,3},{3,2},{4,5},{5,4},{6,7},{7,6},{8,9},{9,8},{10,11... | collective-permute-start | bytes 196616 | tf_op jit(solution)/shard_map/ppermute | solution.py:290
  6.3 8.7 %collective-permute-start.1 = (bf16[256,128]{1,0:T(8,128)(2,1)}, bf16[256,128]{1,0:T(8,128)(2,1)S(1)}, u32[]{:S(2)}, u32[]{:S(2)}) collective-permute-start(bf16[256,128]{1,0:T(8,128)(2,1)} %param.14), channel_id=1, source_target_pairs={{0,1},{1,0},{2,3},{3,2},{4,5},{5,4},{6,7},{7,6},{8,9},{9,8},{10,11... | collective-permute-start | bytes 196616 | tf_op jit(solution)/shard_map/ppermute | solution.py:291
  8.8 46.6 %collective-permute-start.3 = (bf16[512,256]{1,0:T(8,128)(2,1)S(1)}, bf16[512,256]{1,0:T(8,128)(2,1)S(1)}, u32[]{:S(2)}, u32[]{:S(2)}) collective-permute-start(bf16[512,256]{1,0:T(8,128)(2,1)S(1)} %get-tuple-element.55), channel_id=1, source_target_pairs={{1,3},{2,0},{3,5},{4,2},{5,7},{6,4},{7,9},{8,6},{9,11},{10,8},{11,... | collective-permute-start | bytes 786440 | tf_op jit(solution)/shard_map/ppermute | solution.py:300
  10.8 47.4 %collective-permute-start.2 = (bf16[512,256]{1,0:T(8,128)(2,1)S(1)}, bf16[512,256]{1,0:T(8,128)(2,1)S(1)}, u32[]{:S(2)}, u32[]{:S(2)}) collective-permute-start(bf16[512,256]{1,0:T(8,128)(2,1)S(1)} %get-tuple-element.56), channel_id=1, source_target_pairs={{1,3},{2,0},{3,5},{4,2},{5,7},{6,4},{7,9},{8,6},{9,11},{10,8},{11,... | collective-permute-start | bytes 786440 | tf_op jit(solution)/shard_map/ppermute | solution.py:300
  66.8 10.4 %collective-permute-start.6 = (bf16[256,512]{1,0:T(8,128)(2,1)S(1)}, bf16[256,512]{1,0:T(8,128)(2,1)S(1)}, u32[]{:S(2)}, u32[]{:S(2)}) collective-permute-start(bf16[256,512]{1,0:T(8,128)(2,1)S(1)} %get-tuple-element.48), channel_id=1, source_target_pairs={{0,1},{1,0},{2,3},{3,2},{4,5},{5,4},{6,7},{7,6},{8,9},{9,8},{10,11... | collective-permute-start | bytes 786440 | tf_op jit(solution)/shard_map/ppermute | solution.py:378
  68.7 8.5 %copy-start = (bf16[512,512]{1,0:T(8,128)(2,1)S(1)}, bf16[512,512]{1,0:T(8,128)(2,1)}, u32[]{:S(2)}) copy-start(bf16[512,512]{1,0:T(8,128)(2,1)} %mlp_ref.1) | copy-start | bytes 1572868
  68.7 8.5 %copy-start.2 = (bf16[512,256]{1,0:T(8,128)(2,1)S(1)}, bf16[512,256]{1,0:T(8,128)(2,1)}, u32[]{:S(2)}) copy-start(bf16[512,256]{1,0:T(8,128)(2,1)} %mlp_out_ref.1) | copy-start | bytes 786436
  68.7 8.6 %copy-start.3 = (bf16[256,256]{1,0:T(8,128)(2,1)S(1)}, bf16[256,256]{1,0:T(8,128)(2,1)}, u32[]{:S(2)}) copy-start(bf16[256,256]{1,0:T(8,128)(2,1)} %out_ref.1) | copy-start | bytes 393220

commit v8 on v7

--- a/solution.py
+++ b/solution.py
@@ -41,12 +41,15 @@
         parts.append(jnp.where(sub == 0, other, own))
     wk_ref[:, :local], wk_ref[:, local:] = parts[0], parts[1]
     wvt_ref[:local, :], wvt_ref[local:, :] = parts[2].T, parts[3].T
-    keys = dot(x_ref[...], wk_ref[...]).astype(BF16)
-    lane = lax.broadcasted_iota(jnp.int32, (rows, 128), 1)
+    transposed = jnp.concatenate([parts[0].T, parts[1].T], axis=0)
+    queries = dot(transposed, x_ref[...], (1, 1)).astype(BF16)
+    head_width = width // HEADS
     for head in range(HEADS):
-        block, odd = head // 2 * 128, head % 2
-        mine = (lane >= 64) if odd else (lane < 64)
-        queries_ref[head] = jnp.where(mine, keys[:, block : block + 128], jnp.zeros((), BF16))
+        mine, rest = (0, head_width) if head % 2 == 0 else (head_width, 0)
+        queries_ref[head, mine : mine + head_width, :] = queries[
+            head * head_width : (head + 1) * head_width, :
+        ]
+        queries_ref[head, rest : rest + head_width, :] = jnp.zeros((head_width, rows), BF16)
     for step in range(1, SPAN + 1):
         lower = image - sub * step
         inside = jnp.logical_and(lower >= 0, lower + step < images)
@@ -93,10 +96,10 @@
 
     waiting = []
     for head in range(HEADS):
-        queries = queries_ref[head, queries_at, :]
+        queries = queries_ref[head, :, queries_at]
         lanes = slice(head // 2 * 128, head // 2 * 128 + 128)
         for r in range(0, rows, tile):
-            waiting.append((head, r, dot(keys_ref[r : r + tile, lanes], queries, (1, 1))))
+            waiting.append((head, r, dot(keys_ref[r : r + tile, lanes], queries)))
             if len(waiting) > 2:
                 finish(*waiting.pop(0))
     for item in waiting:
@@ -128,9 +131,9 @@
 
         def body(i, carry):
             head, part = i // (span // tile), lax.rem(i, span // tile)
-            queries = queries_ref[head, pl.ds(pl.multiple_of(at + part * tile, tile), tile), :]
+            queries = queries_ref[head, :, pl.ds(pl.multiple_of(at + part * tile, tile), tile)]
             lanes = pl.ds(pl.multiple_of(head // 2 * 128, 128), 128)
-            scores = [dot(keys_ref[:, lanes], queries, (1, 1)) for keys_ref, _ in pieces]
+            scores = [dot(keys_ref[:, lanes], queries) for keys_ref, _ in pieces]
             scores = jnp.concatenate(scores, axis=0) * (1.0 / math.sqrt(head_width))
             powers = jnp.exp(scores - jnp.max(scores, axis=0, keepdims=True))
             weights = (powers / jnp.sum(powers, axis=0, keepdims=True)).astype(BF16)
@@ -325,7 +328,7 @@
         [
             shape((width, width), BF16),
             shape((width, width), BF16),
-            shape((HEADS, rows, 128), BF16),
+            shape((HEADS, 128, rows), BF16),
             shape((8, 128), F32),
             shape((half, width), BF16),
             shape((8, hidden_width), F32),

time: 80.6 us -> 78.2 us (0.970)
  Pallas kernels: 61.4 us -> 59 us
    pallas_call x7, Pallas kernels: 61.4 us -> 59 us  [called(): pl.pallas_call(kernel, in_specs=[SMEM] * scalars + [VMEM] * (len(args) -...]
  transfers between devices with their start and end apart: 7 -> 7, of which waited for: 2 -> 2; matrix products, arithmetic and copies ran while one was open for 2% -> 3% of each run, Pallas kernels for 64% -> 63%
where the time goes in v8:
time: 78.2 us; the launch traced here: 76.8 us
  Pallas kernels  59 us (75%)
  starting transfers between devices  14.7 us (19%)
  local copies, waits for them, and re-layouts  1.1 us (1%)
  other arithmetic  0.89 us (1%)
  waiting for transfers between devices  0.83 us (1%)
    pallas_call x7, Pallas kernels, called(): pl.pallas_call(kernel, in_specs=[SMEM] * scalars + [VMEM] * (len(args) -...  59 us
    ppermute x4, starting transfers between devices, fetched(): return lax.ppermute(value, RING, pairs)  12.3 us
    ppermute x1, starting transfers between devices, on_device(): came = lax.ppermute(send, 'sub', swap)  1.86 us
  transfers between devices with their start and end apart: 7, of which 2 were waited for; matrix products, arithmetic and copies ran while one was open for 3% of the time, Pallas kernels for 63%

profile of v8, /device:TPU:17, one launch (start us, length us, event | category | flops | bytes accessed | tf_op | source)
XLA Modules:
  0.0 76.8 jit_solution(16107324001175804909)
XLA Ops:
  0.0 0.0 copy-start.1
  0.0 0.0 copy-start.8
  0.0 0.0 copy-start.6
  0.0 0.0 copy-start.5
  0.0 0.0 copy-start.7
  0.0 0.0 copy-start.4
  0.0 4.3 %collective-permute-start.5 = (bf16[1024,256]{1,0:T(8,128)(2,1)}, bf16[1024,256]{1,0:T(8,128)(2,1)S(1)}, u32[]{:S(2)}, u32[]{:S(2)}) collective-permute-start(bf16[1024,256]{1,0:T(8,128)(2,1)} %bitcast.8), channel_id=1, source_target_pairs={{1,7},{3,9},{5,11},{6,0},{7,13},{8,2},{9,15},{10,4},{12,6},{14,8},... | collective-permute-start | bytes 1572872 | tf_op jit(solution)/shard_map/ppermute | solution.py:303
  4.3 1.9 %collective-permute-start.4 = (bf16[1024,256]{1,0:T(8,128)(2,1)}, bf16[1024,256]{1,0:T(8,128)(2,1)S(1)}, u32[]{:S(2)}, u32[]{:S(2)}) collective-permute-start(bf16[1024,256]{1,0:T(8,128)(2,1)} %bitcast.9), channel_id=1, source_target_pairs={{1,5},{3,7},{4,0},{5,9},{6,2},{7,11},{8,4},{9,13},{10,6},{11,15},{... | collective-permute-start | bytes 1572872 | tf_op jit(solution)/shard_map/ppermute | solution.py:303
  6.2 0.1 collective-permute-start
  6.3 0.5 collective-permute-start.1
  6.8 0.9 %pad_maximum_fusion.own_ref = bf16[256,256]{1,0:T(8,128)(2,1)S(1)} fusion(bf16[256,128]{1,0:T(8,128)(2,1)} %param.14, bf16[256,128]{1,0:T(8,128)(2,1)} %param.13), kind=kLoop, calls=%fused_computation | loop fusion | flops 262144 | bytes 262144 | tf_op jit(solution)/shard_map/concatenate | solution.py:291
  7.7 0.1 collective-permute-done.qk_other_ref
  7.8 1.1 %fusion = (bf16[512,256]{1,0:T(8,128)(2,1)S(1)}, bf16[512,256]{1,0:T(8,128)(2,1)S(1)}) fusion(bf16[1024,256]{1,0:T(8,128)(2,1)} %bitcast.10), kind=kLoop, calls=%fused_computation.1 | loop fusion | bytes 1048576 | tf_op jit(solution)/shard_map/slice | solution.py:307
  8.8 1.9 %collective-permute-start.3 = (bf16[512,256]{1,0:T(8,128)(2,1)S(1)}, bf16[512,256]{1,0:T(8,128)(2,1)S(1)}, u32[]{:S(2)}, u32[]{:S(2)}) collective-permute-start(bf16[512,256]{1,0:T(8,128)(2,1)S(1)} %get-tuple-element.55), channel_id=1, source_target_pairs={{1,3},{2,0},{3,5},{4,2},{5,7},{6,4},{7,9},{8,6},{9,11},{10,8},{11,... | collective-permute-start | bytes 786440 | tf_op jit(solution)/shard_map/ppermute | solution.py:303
  10.8 4.2 %collective-permute-start.2 = (bf16[512,256]{1,0:T(8,128)(2,1)S(1)}, bf16[512,256]{1,0:T(8,128)(2,1)S(1)}, u32[]{:S(2)}, u32[]{:S(2)}) collective-permute-start(bf16[512,256]{1,0:T(8,128)(2,1)S(1)} %get-tuple-element.56), channel_id=1, source_target_pairs={{1,3},{2,0},{3,5},{4,2},{5,7},{6,4},{7,9},{8,6},{9,11},{10,8},{11,... | collective-permute-start | bytes 786440 | tf_op jit(solution)/shard_map/ppermute | solution.py:303
  15.0 0.0 collective-permute-done.1.value_other_ref
  15.0 0.0 copy-done.1
  15.0 0.0 copy-done.8
  15.0 0.0 copy-done.6
  15.0 0.0 copy-done.5
  15.0 0.0 copy-done.7
  15.0 0.0 copy-done.4
  15.1 0.9 %shard_map.109 = (bf16[256,256]{1,0:T(8,128)(2,1)S(1)}, bf16[256,256]{1,0:T(8,128)(2,1)S(1)}, bf16[4,128,1024]{2,1,0:T(8,128)(2,1)S(1)}, f32[8,128]{1,0:T(8,128)...) custom-call(s32[1]{0:T(128)} %bitcast.place_ref, s32[3,8]{1,0:T(4,128)S(1)} %bitcast.12, ...), custom_call_target="tpu_custom_call" | custom-call | flops 268435456 | bytes 4194304 | tf_op jit(solution)/shard_map/pallas_call | solution.py:311
  16.0 0.8 collective-permute-done.5.x_ref
  16.7 18.4 %shard_map.110.first_ref = bf16[256,1024]{1,0:T(8,128)(2,1)S(1)} custom-call(bf16[4,128,1024]{2,1,0:T(8,128)(2,1)S(1)} %get-tuple-element.31.queries_ref, f32[8,128]{1,0:T(8,128)S(1)} %get-tuple-element.32.facts_ref, bf16[1024,256]{1,0:T(8,128)(2,1)S(1)} %collective-permute-done.5.x_ref, bf16[256,256]{1,0:T(8,128)(2,1)S(1)} %get-tuple-element.34.wk_ref, ...), custom_call_target="tpu_custom_call" | custom-call | flops 2147483648 | bytes 2097152 | tf_op jit(solution)/shard_map/pallas_call | solution.py:311
  35.1 0.0 collective-permute-done.4.x_ref
  35.2 18.4 %shard_map.111.second_ref = bf16[256,1024]{1,0:T(8,128)(2,1)S(1)} custom-call(bf16[4,128,1024]{2,1,0:T(8,128)(2,1)S(1)} %get-tuple-element.31.queries_ref, f32[8,128]{1,0:T(8,128)S(1)} %get-tuple-element.32.facts_ref, bf16[1024,256]{1,0:T(8,128)(2,1)S(1)} %collective-permute-done.4.x_ref, bf16[256,256]{1,0:T(8,128)(2,1)S(1)} %get-tuple-element.34.wk_ref, ...), custom_call_target="tpu_custom_call" | custom-call | flops 2147483648 | bytes 2097152 | tf_op jit(solution)/shard_map/pallas_call | solution.py:311
  53.6 0.0 collective-permute-done.3.x_ref
  53.6 2.6 %shard_map.112 = (bf16[512,256]{1,0:T(8,128)(2,1)S(1)}, bf16[4,80,512]{2,1,0:T(8,128)(2,1)S(1)}, f32[4,80,1024]{2,1,0:T(8,128)S(1)}) custom-call(bf16[4,128,1024]{2,1,0:T(8,128)(2,1)S(1)} %get-tuple-element.31.queries_ref, f32[8,128]{1,0:T(8,128)S(1)} %get-tuple-element.32.facts_ref, bf16[512,256]{1,0:T(8,128)(2,1)S(1)} %collective-permute-done.3.x_ref, ...), custom_call_target="tpu_custom_call" | custom-call | flops 1073741824 | bytes 2097152 | tf_op jit(solution)/shard_map/pallas_call | solution.py:311
  56.1 0.0 collective-permute-done.2.x_ref
  56.1 8.5 %shard_map.113 = (bf16[512,256]{1,0:T(8,128)(2,1)S(1)}, bf16[4,80,512]{2,1,0:T(8,128)(2,1)S(1)}, bf16[256,512]{1,0:T(8,128)(2,1)S(1)}) custom-call(s32[1]{0:T(128)} %bitcast.place_ref, bf16[4,128,1024]{2,1,0:T(8,128)(2,1)S(1)} %get-tuple-element.31.queries_ref, f32[8,128]{1,0:T(8,128)S(1)} %get-tuple-element.32.facts_ref, ...), custom_call_target="tpu_custom_call" | custom-call | flops 536870912 | bytes 2097152 | tf_op jit(solution)/shard_map/pallas_call | solution.py:311
  64.7 1.9 %collective-permute-start.6 = (bf16[256,512]{1,0:T(8,128)(2,1)S(1)}, bf16[256,512]{1,0:T(8,128)(2,1)S(1)}, u32[]{:S(2)}, u32[]{:S(2)}) collective-permute-start(bf16[256,512]{1,0:T(8,128)(2,1)S(1)} %get-tuple-element.48), channel_id=1, source_target_pairs={{0,1},{1,0},{2,3},{3,2},{4,5},{5,4},{6,7},{7,6},{8,9},{9,8},{10,11... | collective-permute-start | bytes 786440 | tf_op jit(solution)/shard_map/ppermute | solution.py:381
  66.5 0.0 copy-start
  66.5 0.0 copy-start.2
  66.5 0.0 copy-start.3
  66.5 8.3 %shard_map.114.keep_ref = f32[256,512]{1,0:T(8,128)S(1)} custom-call(s32[1]{0:T(128)} %bitcast.place_ref, bf16[4,128,1024]{2,1,0:T(8,128)(2,1)S(1)} %get-tuple-element.31.queries_ref, f32[8,128]{1,0:T(8,128)S(1)} %get-tuple-element.32.facts_ref, bf16[512,256]{1,0:T(8,128)(2,1)S(1)} %get-tuple-element.43.keys_before_ref, ...), custom_call_target="tpu_custom_call" | custom-call | flops 536870912 | bytes 2097152 | tf_op jit(solution)/shard_map/pallas_call | solution.py:311
  74.9 0.0 collective-permute-done.6.came_ref
  74.9 0.0 copy-done
  74.9 0.0 copy-done.2
  74.9 0.0 copy-done.3
  74.9 1.9 %shard_map.115 = bf16[512,256]{1,0:T(8,128)(2,1)} custom-call(f32[256,512]{1,0:T(8,128)S(1)} %shard_map.114.keep_ref, bf16[256,512]{1,0:T(8,128)(2,1)S(1)} %collective-permute-done.6.came_ref, bf16[512,256]{1,0:T(8,128)(2,1)S(1)} %get-tuple-element.53.rows_ref, bf16[256,256]{1,0:T(8,128)(2,1)S(1)} %copy-done.3, bf16[512,512]{1,0:T(8,128)(2,1)S(1)} %copy-done, ...), custom_call_target="tpu_custom_call" | custom-call | flops 268435456 | bytes 4194304 | tf_op jit(solution)/shard_map/pallas_call | solution.py:311
Async XLA Ops:
  0.0 15.0 %copy-start.1 = (bf16[1,1024,256]{2,1,0:T(8,128)(2,1)S(1)}, bf16[1,1024,256]{2,1,0:T(8,128)(2,1)}, u32[]{:S(2)}) copy-start(bf16[1,1024,256]{2,1,0:T(8,128)(2,1)} %param.11) | copy-start | bytes 1572868
  0.0 15.0 %copy-start.8 = (f32[256]{0:T(256)S(1)}, f32[256]{0:T(256)}, u32[]{:S(2)}) copy-start(f32[256]{0:T(256)} %param.21) | copy-start | bytes 3076
  0.0 15.0 %copy-start.6 = (f32[512]{0:T(512)S(1)}, f32[512]{0:T(512)}, u32[]{:S(2)}) copy-start(f32[512]{0:T(512)} %param.19) | copy-start | bytes 6148
  0.0 15.0 %copy-start.5 = (f32[512]{0:T(512)S(1)}, f32[512]{0:T(512)}, u32[]{:S(2)}) copy-start(f32[512]{0:T(512)} %param.18) | copy-start | bytes 6148
  0.0 15.0 %copy-start.7 = (f32[512]{0:T(512)S(1)}, f32[512]{0:T(512)}, u32[]{:S(2)}) copy-start(f32[512]{0:T(512)} %param.17) | copy-start | bytes 6148
  0.0 15.0 %copy-start.4 = (s32[8,3]{0,1:T(4,128)S(1)}, s32[8,3]{0,1:T(4,128)}, u32[]{:S(2)}) copy-start(s32[8,3]{0,1:T(4,128)} %param.12) | copy-start | bytes 292
  0.0 16.7 %collective-permute-start.5 = (bf16[1024,256]{1,0:T(8,128)(2,1)}, bf16[1024,256]{1,0:T(8,128)(2,1)S(1)}, u32[]{:S(2)}, u32[]{:S(2)}) collective-permute-start(bf16[1024,256]{1,0:T(8,128)(2,1)} %bitcast.8), channel_id=1, source_target_pairs={{1,7},{3,9},{5,11},{6,0},{7,13},{8,2},{9,15},{10,4},{12,6},{14,8},... | collective-permute-start | bytes 1572872 | tf_op jit(solution)/shard_map/ppermute | solution.py:303
  4.3 30.8 %collective-permute-start.4 = (bf16[1024,256]{1,0:T(8,128)(2,1)}, bf16[1024,256]{1,0:T(8,128)(2,1)S(1)}, u32[]{:S(2)}, u32[]{:S(2)}) collective-permute-start(bf16[1024,256]{1,0:T(8,128)(2,1)} %bitcast.9), channel_id=1, source_target_pairs={{1,5},{3,7},{4,0},{5,9},{6,2},{7,11},{8,4},{9,13},{10,6},{11,15},{... | collective-permute-start | bytes 1572872 | tf_op jit(solution)/shard_map/ppermute | solution.py:303
  6.2 1.5 %collective-permute-start = (bf16[256,128]{1,0:T(8,128)(2,1)}, bf16[256,128]{1,0:T(8,128)(2,1)S(1)}, u32[]{:S(2)}, u32[]{:S(2)}) collective-permute-start(bf16[256,128]{1,0:T(8,128)(2,1)} %param.13), channel_id=1, source_target_pairs={{0,1},{1,0},{2,3},{3,2},{4,5},{5,4},{6,7},{7,6},{8,9},{9,8},{10,11... | collective-permute-start | bytes 196616 | tf_op jit(solution)/shard_map/ppermute | solution.py:293
  6.3 8.7 %collective-permute-start.1 = (bf16[256,128]{1,0:T(8,128)(2,1)}, bf16[256,128]{1,0:T(8,128)(2,1)S(1)}, u32[]{:S(2)}, u32[]{:S(2)}) collective-permute-start(bf16[256,128]{1,0:T(8,128)(2,1)} %param.14), channel_id=1, source_target_pairs={{0,1},{1,0},{2,3},{3,2},{4,5},{5,4},{6,7},{7,6},{8,9},{9,8},{10,11... | collective-permute-start | bytes 196616 | tf_op jit(solution)/shard_map/ppermute | solution.py:294
  8.8 44.7 %collective-permute-start.3 = (bf16[512,256]{1,0:T(8,128)(2,1)S(1)}, bf16[512,256]{1,0:T(8,128)(2,1)S(1)}, u32[]{:S(2)}, u32[]{:S(2)}) collective-permute-start(bf16[512,256]{1,0:T(8,128)(2,1)S(1)} %get-tuple-element.55), channel_id=1, source_target_pairs={{1,3},{2,0},{3,5},{4,2},{5,7},{6,4},{7,9},{8,6},{9,11},{10,8},{11,... | collective-permute-start | bytes 786440 | tf_op jit(solution)/shard_map/ppermute | solution.py:303
  10.8 45.4 %collective-permute-start.2 = (bf16[512,256]{1,0:T(8,128)(2,1)S(1)}, bf16[512,256]{1,0:T(8,128)(2,1)S(1)}, u32[]{:S(2)}, u32[]{:S(2)}) collective-permute-start(bf16[512,256]{1,0:T(8,128)(2,1)S(1)} %get-tuple-element.56), channel_id=1, source_target_pairs={{1,3},{2,0},{3,5},{4,2},{5,7},{6,4},{7,9},{8,6},{9,11},{10,8},{11,... | collective-permute-start | bytes 786440 | tf_op jit(solution)/shard_map/ppermute | solution.py:303
  64.7 10.2 %collective-permute-start.6 = (bf16[256,512]{1,0:T(8,128)(2,1)S(1)}, bf16[256,512]{1,0:T(8,128)(2,1)S(1)}, u32[]{:S(2)}, u32[]{:S(2)}) collective-permute-start(bf16[256,512]{1,0:T(8,128)(2,1)S(1)} %get-tuple-element.48), channel_id=1, source_target_pairs={{0,1},{1,0},{2,3},{3,2},{4,5},{5,4},{6,7},{7,6},{8,9},{9,8},{10,11... | collective-permute-start | bytes 786440 | tf_op jit(solution)/shard_map/ppermute | solution.py:381
  66.5 8.3 %copy-start = (bf16[512,512]{1,0:T(8,128)(2,1)S(1)}, bf16[512,512]{1,0:T(8,128)(2,1)}, u32[]{:S(2)}) copy-start(bf16[512,512]{1,0:T(8,128)(2,1)} %mlp_ref.1) | copy-start | bytes 1572868
  66.5 8.3 %copy-start.2 = (bf16[512,256]{1,0:T(8,128)(2,1)S(1)}, bf16[512,256]{1,0:T(8,128)(2,1)}, u32[]{:S(2)}) copy-start(bf16[512,256]{1,0:T(8,128)(2,1)} %mlp_out_ref.1) | copy-start | bytes 786436
  66.5 8.3 %copy-start.3 = (bf16[256,256]{1,0:T(8,128)(2,1)S(1)}, bf16[256,256]{1,0:T(8,128)(2,1)}, u32[]{:S(2)}) copy-start(bf16[256,256]{1,0:T(8,128)(2,1)} %out_ref.1) | copy-start | bytes 393220

commit v9 on v4

--- a/solution.py
+++ b/solution.py
@@ -41,12 +41,15 @@
         parts.append(jnp.where(sub == 0, other, own))
     wk_ref[:, :local], wk_ref[:, local:] = parts[0], parts[1]
     wvt_ref[:local, :], wvt_ref[local:, :] = parts[2].T, parts[3].T
-    keys = dot(x_ref[...], wk_ref[...]).astype(BF16)
-    lane = lax.broadcasted_iota(jnp.int32, (rows, 128), 1)
+    transposed = jnp.concatenate([parts[0].T, parts[1].T], axis=0)
+    queries = dot(transposed, x_ref[...], (1, 1)).astype(BF16)
+    head_width = width // HEADS
     for head in range(HEADS):
-        block, odd = head // 2 * 128, head % 2
-        mine = (lane >= 64) if odd else (lane < 64)
-        queries_ref[head] = jnp.where(mine, keys[:, block : block + 128], jnp.zeros((), BF16))
+        mine, rest = (0, head_width) if head % 2 == 0 else (head_width, 0)
+        queries_ref[head, mine : mine + head_width, :] = queries[
+            head * head_width : (head + 1) * head_width, :
+        ]
+        queries_ref[head, rest : rest + head_width, :] = jnp.zeros((head_width, rows), BF16)
     for step in range(1, SPAN + 1):
         lower = image - sub * step
         inside = jnp.logical_and(lower >= 0, lower + step < images)
@@ -102,10 +105,10 @@
 
     waiting = []
     for head in range(HEADS):
-        queries = queries_ref[head, queries_at, :]
+        queries = queries_ref[head, :, queries_at]
         lanes = slice(head // 2 * 128, head // 2 * 128 + 128)
         for r in range(0, rows, tile):
-            waiting.append((head, r, dot(keys_ref[r : r + tile, lanes], queries, (1, 1))))
+            waiting.append((head, r, dot(keys_ref[r : r + tile, lanes], queries)))
             if len(waiting) > 2:
                 finish(*waiting.pop(0))
     for item in waiting:
@@ -117,7 +120,7 @@
             head, part = i // (span // tile), lax.rem(i, span // tile)
             part_at = pl.ds(pl.multiple_of(at + part * tile, tile), tile)
             lanes = pl.ds(pl.multiple_of(head // 2 * 128, 128), 128)
-            scores = dot(keys_ref[:, lanes], queries_ref[head, part_at, :], (1, 1)) * scale
+            scores = dot(keys_ref[:, lanes], queries_ref[head, :, part_at]) * scale
             powers = jnp.exp(scores - jnp.max(scores, axis=0, keepdims=True))
             weights = powers / jnp.sum(powers, axis=0, keepdims=True)
             product = dot(values_ref[head, :head_width, :], weights.astype(BF16))
@@ -277,7 +280,7 @@
         [
             shape((width, width), BF16),
             shape((width, width), BF16),
-            shape((HEADS, rows, 128), BF16),
+            shape((HEADS, 128, rows), BF16),
             shape((8, 128), F32),
             shape((half, width), BF16),
             shape((8, hidden_width), F32),

time: 80 us -> 77.9 us (0.974)
  Pallas kernels: 60.9 us -> 58.8 us
    pallas_call x6, Pallas kernels: 60.9 us -> 58.8 us  [called(): pl.pallas_call(kernel, in_specs=[SMEM] * scalars + [VMEM] * (len(args) -...]
where the time goes in v9:
time: 77.9 us; the launch traced here: 76.4 us
  Pallas kernels  58.8 us (75%)
  starting transfers between devices  10.4 us (13%)
  waiting for transfers between devices  3.6 us (5%)
  local copies, waits for them, and re-layouts  3.46 us (4%)
    pallas_call x6, Pallas kernels, called(): pl.pallas_call(kernel, in_specs=[SMEM] * scalars + [VMEM] * (len(args) -...  58.8 us
    ppermute x3, starting transfers between devices, fetched(): return lax.ppermute(own, RING, pairs)  7.96 us
    unnamed x22, local copies, waits for them, and re-layouts  3.46 us
    ppermute x3, waiting for transfers between devices, fetched(): return lax.ppermute(own, RING, pairs)  2.49 us
    ppermute x1, starting transfers between devices, on_device(): came = lax.ppermute(send, 'sub', swap)  1.85 us
  transfers between devices with their start and end apart: 6, of which 3 were waited for; matrix products, arithmetic and copies ran while one was open for 0% of the time, Pallas kernels for 62%

profile of v9, /device:TPU:17, one launch (start us, length us, event | category | flops | bytes accessed | tf_op | source)
XLA Modules:
  0.0 76.4 jit_solution(11886336113868203134)
XLA Ops:
  0.0 4.1 %collective-permute-start.4 = (bf16[1024,256]{1,0:T(8,128)(2,1)}, bf16[1024,256]{1,0:T(8,128)(2,1)S(1)}, u32[]{:S(2)}, u32[]{:S(2)}) collective-permute-start(bf16[1024,256]{1,0:T(8,128)(2,1)} %bitcast.8), channel_id=1, source_target_pairs={{1,7},{3,9},{5,11},{6,0},{7,13},{8,2},{9,15},{10,4},{12,6},{14,8},... | collective-permute-start | bytes 1572872 | tf_op jit(solution)/shard_map/ppermute | solution.py:258
  4.1 1.9 %collective-permute-start.3 = (bf16[1024,256]{1,0:T(8,128)(2,1)}, bf16[1024,256]{1,0:T(8,128)(2,1)S(1)}, u32[]{:S(2)}, u32[]{:S(2)}) collective-permute-start(bf16[1024,256]{1,0:T(8,128)(2,1)} %bitcast.9), channel_id=1, source_target_pairs={{1,5},{3,7},{4,0},{5,9},{6,2},{7,11},{8,4},{9,13},{10,6},{11,15},{... | collective-permute-start | bytes 1572872 | tf_op jit(solution)/shard_map/ppermute | solution.py:258
  6.1 1.9 %collective-permute-start.2 = (bf16[1024,256]{1,0:T(8,128)(2,1)}, bf16[1024,256]{1,0:T(8,128)(2,1)S(1)}, u32[]{:S(2)}, u32[]{:S(2)}) collective-permute-start(bf16[1024,256]{1,0:T(8,128)(2,1)} %bitcast.10), channel_id=1, source_target_pairs={{1,3},{2,0},{3,5},{4,2},{5,7},{6,4},{7,9},{8,6},{9,11},{10,8},{11,... | collective-permute-start | bytes 1572872 | tf_op jit(solution)/shard_map/ppermute | solution.py:258
  8.0 0.1 collective-permute-start
  8.1 0.5 collective-permute-start.1
  8.6 1.0 %collective-permute-done.qk_other_ref = bf16[256,128]{1,0:T(8,128)(2,1)S(1)} collective-permute-done((bf16[256,128]{1,0:T(8,128)(2,1)}, bf16[256,128]{1,0:T(8,128)(2,1)S(1)}, u32[]{:S(2)}, u32[]{:S(2)}) %collective-permute-start) | collective-permute-done | bytes 65568 | tf_op jit(solution)/shard_map/ppermute | solution.py:248
  9.5 0.2 collective-permute-done.1.value_other_ref
  9.7 0.0 copy-start.9
  9.7 0.0 copy-start.8
  9.7 0.0 copy-start.7
  9.7 0.0 copy-start.6
  9.7 0.0 copy-start.10
  9.7 0.7 copy-done.9
  10.4 0.0 copy-done.8
  10.4 0.0 copy-done.7
  10.4 0.0 copy-done.6
  10.4 0.0 copy-done.10
  10.4 0.0 copy-start.3
  10.4 1.0 %copy-done.3 = bf16[1,1024,256]{2,1,0:T(8,128)(2,1)S(1)} copy-done((bf16[1,1024,256]{2,1,0:T(8,128)(2,1)S(1)}, bf16[1,1024,256]{2,1,0:T(8,128)(2,1)}, u32[]{:S(2)}) %copy-start.3) | copy-done | bytes 524312
  11.5 0.0 copy-start.4
  11.5 0.8 %copy-done.4 = bf16[256,128]{1,0:T(8,128)(2,1)S(1)} copy-done((bf16[256,128]{1,0:T(8,128)(2,1)S(1)}, bf16[256,128]{1,0:T(8,128)(2,1)}, u32[]{:S(2)}) %copy-start.4) | copy-done | bytes 65560
  12.3 0.0 copy-start.5
  12.3 0.8 %copy-done.5 = bf16[256,128]{1,0:T(8,128)(2,1)S(1)} copy-done((bf16[256,128]{1,0:T(8,128)(2,1)S(1)}, bf16[256,128]{1,0:T(8,128)(2,1)}, u32[]{:S(2)}) %copy-start.5) | copy-done | bytes 65560
  13.1 0.9 %shard_map.109 = (bf16[256,256]{1,0:T(8,128)(2,1)S(1)}, bf16[256,256]{1,0:T(8,128)(2,1)S(1)}, bf16[4,128,1024]{2,1,0:T(8,128)(2,1)S(1)}, f32[8,128]{1,0:T(8,128)...) custom-call(s32[1]{0:T(128)} %bitcast.place_ref, s32[3,8]{1,0:T(4,128)S(1)} %bitcast.12, ...), custom_call_target="tpu_custom_call" | custom-call | flops 268435456 | bytes 4194304 | tf_op jit(solution)/shard_map/pallas_call | solution.py:263
  14.1 2.5 %collective-permute-done.4.x_ref = bf16[1024,256]{1,0:T(8,128)(2,1)S(1)} collective-permute-done((bf16[1024,256]{1,0:T(8,128)(2,1)}, bf16[1024,256]{1,0:T(8,128)(2,1)S(1)}, u32[]{:S(2)}, u32[]{:S(2)}) %collective-permute-start.4) | collective-permute-done | bytes 524320 | tf_op jit(solution)/shard_map/ppermute | solution.py:258
  16.5 18.5 %shard_map.110.first_ref = bf16[256,1024]{1,0:T(8,128)(2,1)S(1)} custom-call(bf16[4,128,1024]{2,1,0:T(8,128)(2,1)S(1)} %get-tuple-element.21.queries_ref, f32[8,128]{1,0:T(8,128)S(1)} %get-tuple-element.22.facts_ref, bf16[1024,256]{1,0:T(8,128)(2,1)S(1)} %collective-permute-done.4.x_ref, bf16[256,256]{1,0:T(8,128)(2,1)S(1)} %get-tuple-element.23.wk_ref, ...), custom_call_target="tpu_custom_call" | custom-call | flops 2147483648 | bytes 2097152 | tf_op jit(solution)/shard_map/pallas_call | solution.py:263
  35.1 0.0 collective-permute-done.3.x_ref
  35.1 18.5 %shard_map.111.second_ref = bf16[256,1024]{1,0:T(8,128)(2,1)S(1)} custom-call(bf16[4,128,1024]{2,1,0:T(8,128)(2,1)S(1)} %get-tuple-element.21.queries_ref, f32[8,128]{1,0:T(8,128)S(1)} %get-tuple-element.22.facts_ref, bf16[1024,256]{1,0:T(8,128)(2,1)S(1)} %collective-permute-done.3.x_ref, bf16[256,256]{1,0:T(8,128)(2,1)S(1)} %get-tuple-element.23.wk_ref, ...), custom_call_target="tpu_custom_call" | custom-call | flops 2147483648 | bytes 2097152 | tf_op jit(solution)/shard_map/pallas_call | solution.py:263
  53.6 0.0 collective-permute-done.2.x_ref
  53.6 9.8 %shard_map.112 = (bf16[1024,256]{1,0:T(8,128)(2,1)S(1)}, bf16[4,80,1024]{2,1,0:T(8,128)(2,1)S(1)}, bf16[256,512]{1,0:T(8,128)(2,1)S(1)}) custom-call(s32[1]{0:T(128)} %bitcast.place_ref, bf16[4,128,1024]{2,1,0:T(8,128)(2,1)S(1)} %get-tuple-element.21.queries_ref, f32[8,128]{1,0:T(8,128)S(1)} %get-tuple-element.22.facts_ref, ...), custom_call_target="tpu_custom_call" | custom-call | flops 1073741824 | bytes 2097152 | tf_op jit(solution)/shard_map/pallas_call | solution.py:263
  63.4 1.9 %collective-permute-start.5 = (bf16[256,512]{1,0:T(8,128)(2,1)S(1)}, bf16[256,512]{1,0:T(8,128)(2,1)S(1)}, u32[]{:S(2)}, u32[]{:S(2)}) collective-permute-start(bf16[256,512]{1,0:T(8,128)(2,1)S(1)} %get-tuple-element.30), channel_id=1, source_target_pairs={{0,1},{1,0},{2,3},{3,2},{4,5},{5,4},{6,7},{7,6},{8,9},{9,8},{10,11... | collective-permute-start | bytes 786440 | tf_op jit(solution)/shard_map/ppermute | solution.py:321
  65.2 0.0 copy-start
  65.2 0.0 copy-start.1
  65.2 0.0 copy-start.2
  65.2 9.2 %shard_map.113.keep_ref = f32[256,512]{1,0:T(8,128)S(1)} custom-call(s32[1]{0:T(128)} %bitcast.place_ref, bf16[4,128,1024]{2,1,0:T(8,128)(2,1)S(1)} %get-tuple-element.21.queries_ref, f32[8,128]{1,0:T(8,128)S(1)} %get-tuple-element.22.facts_ref, bf16[1024,256]{1,0:T(8,128)(2,1)S(1)} %get-tuple-element.31.keys_ref, ...), custom_call_target="tpu_custom_call" | custom-call | flops 1073741824 | bytes 2097152 | tf_op jit(solution)/shard_map/pallas_call | solution.py:263
  74.4 0.0 collective-permute-done.5.came_ref
  74.5 0.0 copy-done
  74.5 0.0 copy-done.1
  74.5 0.0 copy-done.2
  74.5 1.9 %shard_map.114 = bf16[512,256]{1,0:T(8,128)(2,1)} custom-call(f32[256,512]{1,0:T(8,128)S(1)} %shard_map.113.keep_ref, bf16[256,512]{1,0:T(8,128)(2,1)S(1)} %collective-permute-done.5.came_ref, bf16[512,256]{1,0:T(8,128)(2,1)S(1)} %get-tuple-element.35.rows_ref, bf16[256,256]{1,0:T(8,128)(2,1)S(1)} %copy-done.2, bf16[512,512]{1,0:T(8,128)(2,1)S(1)} %copy-done, ...), custom_call_target="tpu_custom_call" | custom-call | flops 268435456 | bytes 4194304 | tf_op jit(solution)/shard_map/pallas_call | solution.py:263
Async XLA Ops:
  0.0 16.5 %collective-permute-start.4 = (bf16[1024,256]{1,0:T(8,128)(2,1)}, bf16[1024,256]{1,0:T(8,128)(2,1)S(1)}, u32[]{:S(2)}, u32[]{:S(2)}) collective-permute-start(bf16[1024,256]{1,0:T(8,128)(2,1)} %bitcast.8), channel_id=1, source_target_pairs={{1,7},{3,9},{5,11},{6,0},{7,13},{8,2},{9,15},{10,4},{12,6},{14,8},... | collective-permute-start | bytes 1572872 | tf_op jit(solution)/shard_map/ppermute | solution.py:258
  4.1 30.9 %collective-permute-start.3 = (bf16[1024,256]{1,0:T(8,128)(2,1)}, bf16[1024,256]{1,0:T(8,128)(2,1)S(1)}, u32[]{:S(2)}, u32[]{:S(2)}) collective-permute-start(bf16[1024,256]{1,0:T(8,128)(2,1)} %bitcast.9), channel_id=1, source_target_pairs={{1,5},{3,7},{4,0},{5,9},{6,2},{7,11},{8,4},{9,13},{10,6},{11,15},{... | collective-permute-start | bytes 1572872 | tf_op jit(solution)/shard_map/ppermute | solution.py:258
  6.1 47.5 %collective-permute-start.2 = (bf16[1024,256]{1,0:T(8,128)(2,1)}, bf16[1024,256]{1,0:T(8,128)(2,1)S(1)}, u32[]{:S(2)}, u32[]{:S(2)}) collective-permute-start(bf16[1024,256]{1,0:T(8,128)(2,1)} %bitcast.10), channel_id=1, source_target_pairs={{1,3},{2,0},{3,5},{4,2},{5,7},{6,4},{7,9},{8,6},{9,11},{10,8},{11,... | collective-permute-start | bytes 1572872 | tf_op jit(solution)/shard_map/ppermute | solution.py:258
  8.0 1.5 %collective-permute-start = (bf16[256,128]{1,0:T(8,128)(2,1)}, bf16[256,128]{1,0:T(8,128)(2,1)S(1)}, u32[]{:S(2)}, u32[]{:S(2)}) collective-permute-start(bf16[256,128]{1,0:T(8,128)(2,1)} %qk_ref.1), channel_id=1, source_target_pairs={{0,1},{1,0},{2,3},{3,2},{4,5},{5,4},{6,7},{7,6},{8,9},{9,8},{10,11... | collective-permute-start | bytes 196616 | tf_op jit(solution)/shard_map/ppermute | solution.py:248
  8.1 1.6 %collective-permute-start.1 = (bf16[256,128]{1,0:T(8,128)(2,1)}, bf16[256,128]{1,0:T(8,128)(2,1)S(1)}, u32[]{:S(2)}, u32[]{:S(2)}) collective-permute-start(bf16[256,128]{1,0:T(8,128)(2,1)} %value_ref.1), channel_id=1, source_target_pairs={{0,1},{1,0},{2,3},{3,2},{4,5},{5,4},{6,7},{7,6},{8,9},{9,8},{10,11... | collective-permute-start | bytes 196616 | tf_op jit(solution)/shard_map/ppermute | solution.py:249
  9.7 0.7 copy-start.9
  9.7 0.7 copy-start.8
  9.7 0.7 copy-start.7
  9.7 0.7 copy-start.6
  9.7 0.7 copy-start.10
  10.4 1.0 %copy-start.3 = (bf16[1,1024,256]{2,1,0:T(8,128)(2,1)S(1)}, bf16[1,1024,256]{2,1,0:T(8,128)(2,1)}, u32[]{:S(2)}) copy-start(bf16[1,1024,256]{2,1,0:T(8,128)(2,1)} %param.11) | copy-start | bytes 1572868
  11.5 0.8 %copy-start.4 = (bf16[256,128]{1,0:T(8,128)(2,1)S(1)}, bf16[256,128]{1,0:T(8,128)(2,1)}, u32[]{:S(2)}) copy-start(bf16[256,128]{1,0:T(8,128)(2,1)} %qk_ref.1) | copy-start | bytes 196612
  12.3 0.8 %copy-start.5 = (bf16[256,128]{1,0:T(8,128)(2,1)S(1)}, bf16[256,128]{1,0:T(8,128)(2,1)}, u32[]{:S(2)}) copy-start(bf16[256,128]{1,0:T(8,128)(2,1)} %value_ref.1) | copy-start | bytes 196612
  63.4 11.1 %collective-permute-start.5 = (bf16[256,512]{1,0:T(8,128)(2,1)S(1)}, bf16[256,512]{1,0:T(8,128)(2,1)S(1)}, u32[]{:S(2)}, u32[]{:S(2)}) collective-permute-start(bf16[256,512]{1,0:T(8,128)(2,1)S(1)} %get-tuple-element.30), channel_id=1, source_target_pairs={{0,1},{1,0},{2,3},{3,2},{4,5},{5,4},{6,7},{7,6},{8,9},{9,8},{10,11... | collective-permute-start | bytes 786440 | tf_op jit(solution)/shard_map/ppermute | solution.py:321
  65.2 9.3 %copy-start = (bf16[512,512]{1,0:T(8,128)(2,1)S(1)}, bf16[512,512]{1,0:T(8,128)(2,1)}, u32[]{:S(2)}) copy-start(bf16[512,512]{1,0:T(8,128)(2,1)} %mlp_ref.1) | copy-start | bytes 1572868
  65.2 9.3 %copy-start.1 = (bf16[512,256]{1,0:T(8,128)(2,1)S(1)}, bf16[512,256]{1,0:T(8,128)(2,1)}, u32[]{:S(2)}) copy-start(bf16[512,256]{1,0:T(8,128)(2,1)} %mlp_out_ref.1) | copy-start | bytes 786436
  65.2 9.3 %copy-start.2 = (bf16[256,256]{1,0:T(8,128)(2,1)S(1)}, bf16[256,256]{1,0:T(8,128)(2,1)}, u32[]{:S(2)}) copy-start(bf16[256,256]{1,0:T(8,128)(2,1)} %out_ref.1) | copy-start | bytes 393220

commit v10 on v6

--- a/solution.py
+++ b/solution.py
@@ -41,12 +41,15 @@
         parts.append(jnp.where(sub == 0, other, own))
     wk_ref[:, :local], wk_ref[:, local:] = parts[0], parts[1]
     wvt_ref[:local, :], wvt_ref[local:, :] = parts[2].T, parts[3].T
-    keys = dot(x_ref[...], wk_ref[...]).astype(BF16)
-    lane = lax.broadcasted_iota(jnp.int32, (rows, 128), 1)
+    transposed = jnp.concatenate([parts[0].T, parts[1].T], axis=0)
+    queries = dot(transposed, x_ref[...], (1, 1)).astype(BF16)
+    head_width = width // HEADS
     for head in range(HEADS):
-        block, odd = head // 2 * 128, head % 2
-        mine = (lane >= 64) if odd else (lane < 64)
-        queries_ref[head] = jnp.where(mine, keys[:, block : block + 128], jnp.zeros((), BF16))
+        mine, rest = (0, head_width) if head % 2 == 0 else (head_width, 0)
+        queries_ref[head, mine : mine + head_width, :] = queries[
+            head * head_width : (head + 1) * head_width, :
+        ]
+        queries_ref[head, rest : rest + head_width, :] = jnp.zeros((head_width, rows), BF16)
     for step in range(1, SPAN + 1):
         lower = image - sub * step
         inside = jnp.logical_and(lower >= 0, lower + step < images)
@@ -104,10 +107,10 @@
 
     waiting = []
     for head in range(HEADS):
-        queries = queries_ref[head, queries_at, :]
+        queries = queries_ref[head, :, queries_at]
         lanes = slice(head // 2 * 128, head // 2 * 128 + 128)
         for r in range(0, rows, tile):
-            waiting.append((head, r, dot(keys_ref[r : r + tile, lanes], queries, (1, 1))))
+            waiting.append((head, r, dot(keys_ref[r : r + tile, lanes], queries)))
             if len(waiting) > 2:
                 finish(*waiting.pop(0))
     for item in waiting:
@@ -119,7 +122,7 @@
             head, part = i // (span // tile), lax.rem(i, span // tile)
             part_at = pl.ds(pl.multiple_of(at + part * tile, tile), tile)
             lanes = pl.ds(pl.multiple_of(head // 2 * 128, 128), 128)
-            scores = dot(keys_ref[:, lanes], queries_ref[head, part_at, :], (1, 1)) * scale
+            scores = dot(keys_ref[:, lanes], queries_ref[head, :, part_at]) * scale
             powers = jnp.exp(scores - jnp.max(scores, axis=0, keepdims=True))
             weights = powers / jnp.sum(powers, axis=0, keepdims=True)
             product = dot(values_ref[head, :head_width, :], weights.astype(BF16))
@@ -135,11 +138,16 @@
     return lax.rem(place // 2, 2) == lax.rem(place, 2)
 
 
-def partner_kernel(step, two, place_ref, queries_ref, facts_ref, x_ref, *refs):
+def is_linked(facts_ref, steps, place):
+    near, far = (jnp.max(facts_ref[step : step + 1, :]) for step in steps)
+    return jnp.where(near_first(place), near, far) > 0.0
+
+
+def partner_kernel(steps, two, place_ref, queries_ref, facts_ref, x_ref, *refs):
     other_ref, *refs = refs if two else (None, *refs)
     wk_ref, wvt_ref, message_ref, keys_ref, values_ref = refs
     rows, _ = keys_ref.shape
-    linked = jnp.max(facts_ref[step : step + 1, :]) > 0.0
+    linked = is_linked(facts_ref, steps, place_ref[0])
 
     @pl.when(jnp.logical_not(linked))
     def _():
@@ -160,14 +168,14 @@
 
 
 def last_kernel(
-    step, place_ref, queries_ref, facts_ref, x_ref, other_ref, wk_ref, wvt_ref, first_ref,
+    steps, place_ref, queries_ref, facts_ref, x_ref, other_ref, wk_ref, wvt_ref, first_ref,
     second_ref, keys_ref, values_ref, send_ref, message_ref,
 ):
     half = message_ref.shape[1]
     place = place_ref[0]
     at = pl.multiple_of((1 - lax.rem(place, 2)) * half, half)
     here = pl.ds(at, half)
-    linked = jnp.max(facts_ref[step : step + 1, :]) > 0.0
+    linked = is_linked(facts_ref, steps, place_ref[0])
     total = first_ref[:, here].astype(F32) + second_ref[:, here].astype(F32)
 
     @pl.when(jnp.logical_not(linked))
@@ -183,13 +191,13 @@
 
 
 def own_kernel(
-    step, place_ref, queries_ref, facts_ref, keys_ref, values_ref, first_ref, second_ref, keep_ref,
+    steps, place_ref, queries_ref, facts_ref, keys_ref, values_ref, first_ref, second_ref, keep_ref,
     message_ref,
 ):
     half = message_ref.shape[1]
     at = pl.multiple_of(lax.rem(place_ref[0], 2) * half, half)
     here = pl.ds(at, half)
-    linked = jnp.max(facts_ref[step : step + 1, :]) > 0.0
+    linked = is_linked(facts_ref, steps, place_ref[0])
 
     @pl.when(jnp.logical_not(linked))
     def _():
@@ -315,7 +323,7 @@
         [
             shape((width, width), BF16),
             shape((width, width), BF16),
-            shape((HEADS, rows, 128), BF16),
+            shape((HEADS, 128, rows), BF16),
             shape((8, 128), F32),
             shape((half, width), BF16),
             shape((8, hidden_width), F32),
@@ -325,11 +333,10 @@
         scalars=2,
     )
 
-    own_later, facts = lax.optimization_barrier((own, facts))
-    one_outer = carried(own_later, outer)
-    one_inner, facts = lax.optimization_barrier((one_inner, facts))
+    one_inner, facts, own_later = lax.optimization_barrier((one_inner, facts, own))
     three_outer = carried(one_inner, far_outer)
     three_inner = carried(one_inner, far_inner)
+    one_outer = carried(own_later, outer)
 
     projected = [
         shape((rows, width), BF16),
@@ -340,34 +347,32 @@
     work = cost(8 * rows * rows * width, 2 << 20, HEADS * rows * rows)
     half_work = cost(4 * rows * rows * width, 2 << 20, HEADS * rows * half)
     (message,) = called(
-        functools.partial(partner_kernel, 2, False),
+        functools.partial(partner_kernel, (2, 2), False),
         [place, queries, facts, two, wk, wvt],
         message_shape,
         scratch,
         work,
     )
-    one_outer, message = lax.optimization_barrier((one_outer, message))
+    three_outer, message = lax.optimization_barrier((three_outer, message))
     messages = [message]
     messages += called(
-        functools.partial(partner_kernel, 1, True),
-        [place, queries, facts, one_outer, one_inner, wk, wvt],
+        functools.partial(partner_kernel, (1, 3), True),
+        [place, queries, facts, three_outer, one_inner, wk, wvt],
         message_shape,
         scratch,
         work,
     )
-    three_outer, three_inner, messages = lax.optimization_barrier(
-        (three_outer, three_inner, messages)
-    )
+    one_outer, three_inner, messages = lax.optimization_barrier((one_outer, three_inner, messages))
     keys, values, send = called(
-        functools.partial(last_kernel, 3),
-        [place, queries, facts, three_outer, three_inner, wk, wvt, *messages],
+        functools.partial(last_kernel, (3, 1)),
+        [place, queries, facts, one_outer, three_inner, wk, wvt, *messages],
         [*projected, shape((width, half), BF16)],
         [pltpu.VMEM((width, half), BF16)],
         half_work,
     )
     came = lax.ppermute(send, "sub", swap)
     (keep,) = called(
-        functools.partial(own_kernel, 3),
+        functools.partial(own_kernel, (3, 1)),
         [place, queries, facts, keys, values, *messages],
         [shape((width, half), F32)],
         [pltpu.VMEM((width, half), BF16)],

time: 77.5 us -> 76.4 us (0.986)
  the two profiles are of different devices: /device:TPU:8 before, /device:TPU:17 now
where the time goes in v10:
time: 76.4 us; the launch traced here: 75.4 us
  Pallas kernels  59.4 us (78%)
  starting transfers between devices  14 us (18%)
  other arithmetic  0.89 us (1%)
    pallas_call x6, Pallas kernels, called(): pl.pallas_call(kernel, in_specs=[SMEM] * scalars + [VMEM] * (len(args) -...  59.4 us
    ppermute x5, starting transfers between devices, carried(): return lax.ppermute(value, RING, pairs)  11.1 us
    ppermute x1, starting transfers between devices, on_device(): came = lax.ppermute(send, 'sub', swap)  2.32 us
  transfers between devices with their start and end apart: 8, of which 2 were waited for; matrix products, arithmetic and copies ran while one was open for 1% of the time, Pallas kernels for 63%

profile of v10, /device:TPU:17, one launch (start us, length us, event | category | flops | bytes accessed | tf_op | source)
XLA Modules:
  0.0 75.4 jit_solution(11762029526564552163)
XLA Ops:
  0.0 3.1 %collective-permute-start.2 = (bf16[1024,256]{1,0:T(8,128)(2,1)}, bf16[1024,256]{1,0:T(8,128)(2,1)S(1)}, u32[]{:S(2)}, u32[]{:S(2)}) collective-permute-start(bf16[1024,256]{1,0:T(8,128)(2,1)} %bitcast.2.x_ref), channel_id=1, source_target_pairs={{2,0},{1,3},{6,4},{5,7},{10,8},{9,11},{14,12},{13,15},{18,16},{17,... | collective-permute-start | bytes 1572872 | tf_op jit(solution)/shard_map/ppermute | solution.py:271
  3.1 3.2 %collective-permute-start.6 = (bf16[1024,256]{1,0:T(8,128)(2,1)}, bf16[1024,256]{1,0:T(8,128)(2,1)S(1)}, u32[]{:S(2)}, u32[]{:S(2)}) collective-permute-start(bf16[1024,256]{1,0:T(8,128)(2,1)} %bitcast.2.x_ref), channel_id=1, source_target_pairs={{4,0},{6,2},{8,4},{1,5},{10,6},{3,7},{12,8},{5,9},{14,10},{7,11},{... | collective-permute-start | bytes 1572872 | tf_op jit(solution)/shard_map/ppermute | solution.py:271
  6.4 0.1 collective-permute-start
  6.4 0.5 collective-permute-start.1
  6.9 0.9 %pad_maximum_fusion.own_ref = bf16[256,256]{1,0:T(8,128)(2,1)S(1)} fusion(bf16[256,128]{1,0:T(8,128)(2,1)} %param.14, bf16[256,128]{1,0:T(8,128)(2,1)} %param.13), kind=kLoop, calls=%fused_computation | loop fusion | flops 262144 | bytes 262144 | tf_op jit(solution)/shard_map/concatenate | solution.py:259
  7.8 0.1 collective-permute-done.qk_other_ref
  7.9 0.2 collective-permute-done.1.value_other_ref
  8.1 0.0 copy-start.6
  8.1 0.0 copy-start.4
  8.1 0.0 copy-start.5
  8.1 0.0 copy-start.3
  8.1 0.0 copy-start.7
  8.1 0.7 copy-done.6
  8.7 0.0 copy-done.4
  8.7 0.0 copy-done.5
  8.8 0.0 copy-done.3
  8.8 0.0 copy-done.7
  8.8 1.4 %shard_map.109 = (bf16[256,256]{1,0:T(8,128)(2,1)S(1)}, bf16[256,256]{1,0:T(8,128)(2,1)S(1)}, bf16[4,128,1024]{2,1,0:T(8,128)(2,1)S(1)}, f32[8,128]{1,0:T(8,128)...) custom-call(s32[1]{0:T(128)} %bitcast.place_ref, s32[3,8]{1,0:T(4,128)S(1)} %bitcast.8, ...), custom_call_target="tpu_custom_call" | custom-call | flops 268435456 | bytes 4194304 | tf_op jit(solution)/shard_map/pallas_call | solution.py:306
  10.2 0.0 collective-permute-done.2.refs_0_
  10.2 1.3 %collective-permute-start.5 = (bf16[1024,256]{1,0:T(8,128)(2,1)S(1)}, bf16[1024,256]{1,0:T(8,128)(2,1)S(1)}, u32[]{:S(2)}, u32[]{:S(2)}) collective-permute-start(bf16[1024,256]{1,0:T(8,128)(2,1)S(1)} %collective-permute-done.2.refs_0_), channel_id=1, source_target_pairs={{11,2},{15,6},{0,9},{4,13},{27,18},{31,22},{16,25},{20,29}} | collective-permute-start | bytes 1572872 | tf_op jit(solution)/shard_map/ppermute | solution.py:271
  11.5 2.8 %collective-permute-start.3 = (bf16[1024,256]{1,0:T(8,128)(2,1)}, bf16[1024,256]{1,0:T(8,128)(2,1)S(1)}, u32[]{:S(2)}, u32[]{:S(2)}) collective-permute-start(bf16[1024,256]{1,0:T(8,128)(2,1)} %bitcast.2.x_ref), channel_id=1, source_target_pairs={{5,2},{2,5},{9,6},{6,9},{13,10},{10,13},{21,18},{18,21},{25,22},{2... | collective-permute-start | bytes 1572872 | tf_op jit(solution)/shard_map/ppermute | solution.py:271
  14.3 0.7 collective-permute-start.4
  15.0 0.0 collective-permute-done.6.x_ref
  15.0 18.5 %shard_map.110.first_ref = bf16[256,1024]{1,0:T(8,128)(2,1)S(1)} custom-call(s32[1]{0:T(128)} %bitcast.place_ref, bf16[4,128,1024]{2,1,0:T(8,128)(2,1)S(1)} %get-tuple-element.25.queries_ref, f32[8,128]{1,0:T(8,128)S(1)} %get-tuple-element.27.facts_ref, bf16[1024,256]{1,0:T(8,128)(2,1)S(1)} %collective-permute-done.6.x_ref, ...), custom_call_target="tpu_custom_call" | custom-call | flops 2147483648 | bytes 2097152 | tf_op jit(solution)/shard_map/pallas_call | solution.py:306
  33.5 0.0 collective-permute-done.5.x_ref
  33.5 18.5 %shard_map.111.second_ref = bf16[256,1024]{1,0:T(8,128)(2,1)S(1)} custom-call(s32[1]{0:T(128)} %bitcast.place_ref, bf16[4,128,1024]{2,1,0:T(8,128)(2,1)S(1)} %get-tuple-element.25.queries_ref, f32[8,128]{1,0:T(8,128)S(1)} %get-tuple-element.27.facts_ref, bf16[1024,256]{1,0:T(8,128)(2,1)S(1)} %collective-permute-done.5.x_ref, ...), custom_call_target="tpu_custom_call" | custom-call | flops 2147483648 | bytes 2097152 | tf_op jit(solution)/shard_map/pallas_call | solution.py:306
  52.1 0.0 collective-permute-done.3.x_ref
  52.1 0.0 collective-permute-done.4.other_ref
  52.1 9.8 %shard_map.112 = (bf16[1024,256]{1,0:T(8,128)(2,1)S(1)}, bf16[4,80,1024]{2,1,0:T(8,128)(2,1)S(1)}, bf16[256,512]{1,0:T(8,128)(2,1)S(1)}) custom-call(s32[1]{0:T(128)} %bitcast.place_ref, bf16[4,128,1024]{2,1,0:T(8,128)(2,1)S(1)} %get-tuple-element.25.queries_ref, f32[8,128]{1,0:T(8,128)S(1)} %get-tuple-element.27.facts_ref, ...), custom_call_target="tpu_custom_call" | custom-call | flops 1073741824 | bytes 2097152 | tf_op jit(solution)/shard_map/pallas_call | solution.py:306
  61.9 2.3 %collective-permute-start.7 = (bf16[256,512]{1,0:T(8,128)(2,1)S(1)}, bf16[256,512]{1,0:T(8,128)(2,1)S(1)}, u32[]{:S(2)}, u32[]{:S(2)}) collective-permute-start(bf16[256,512]{1,0:T(8,128)(2,1)S(1)} %get-tuple-element.38), channel_id=1, source_target_pairs={{0,1},{1,0},{2,3},{3,2},{4,5},{5,4},{6,7},{7,6},{8,9},{9,8},{10,11... | collective-permute-start | bytes 786440 | tf_op jit(solution)/shard_map/ppermute | solution.py:373
  64.2 0.0 copy-start
  64.2 0.0 copy-start.1
  64.2 0.0 copy-start.2
  64.2 9.3 %shard_map.113.keep_ref = f32[256,512]{1,0:T(8,128)S(1)} custom-call(s32[1]{0:T(128)} %bitcast.place_ref, bf16[4,128,1024]{2,1,0:T(8,128)(2,1)S(1)} %get-tuple-element.25.queries_ref, f32[8,128]{1,0:T(8,128)S(1)} %get-tuple-element.27.facts_ref, bf16[1024,256]{1,0:T(8,128)(2,1)S(1)} %get-tuple-element.39.keys_ref, ...), custom_call_target="tpu_custom_call" | custom-call | flops 1073741824 | bytes 2097152 | tf_op jit(solution)/shard_map/pallas_call | solution.py:306
  73.5 0.0 collective-permute-done.7.came_ref
  73.5 0.0 copy-done
  73.5 0.0 copy-done.1
  73.5 0.0 copy-done.2
  73.5 1.9 %shard_map.114 = bf16[512,256]{1,0:T(8,128)(2,1)} custom-call(f32[256,512]{1,0:T(8,128)S(1)} %shard_map.113.keep_ref, bf16[256,512]{1,0:T(8,128)(2,1)S(1)} %collective-permute-done.7.came_ref, bf16[512,256]{1,0:T(8,128)(2,1)S(1)} %get-tuple-element.43.rows_ref, bf16[256,256]{1,0:T(8,128)(2,1)S(1)} %copy-done.2, bf16[512,512]{1,0:T(8,128)(2,1)S(1)} %copy-done, ...), custom_call_target="tpu_custom_call" | custom-call | flops 268435456 | bytes 4194304 | tf_op jit(solution)/shard_map/pallas_call | solution.py:306
Async XLA Ops:
  0.0 10.2 %collective-permute-start.2 = (bf16[1024,256]{1,0:T(8,128)(2,1)}, bf16[1024,256]{1,0:T(8,128)(2,1)S(1)}, u32[]{:S(2)}, u32[]{:S(2)}) collective-permute-start(bf16[1024,256]{1,0:T(8,128)(2,1)} %bitcast.2.x_ref), channel_id=1, source_target_pairs={{2,0},{1,3},{6,4},{5,7},{10,8},{9,11},{14,12},{13,15},{18,16},{17,... | collective-permute-start | bytes 1572872 | tf_op jit(solution)/shard_map/ppermute | solution.py:271
  3.1 11.9 %collective-permute-start.6 = (bf16[1024,256]{1,0:T(8,128)(2,1)}, bf16[1024,256]{1,0:T(8,128)(2,1)S(1)}, u32[]{:S(2)}, u32[]{:S(2)}) collective-permute-start(bf16[1024,256]{1,0:T(8,128)(2,1)} %bitcast.2.x_ref), channel_id=1, source_target_pairs={{4,0},{6,2},{8,4},{1,5},{10,6},{3,7},{12,8},{5,9},{14,10},{7,11},{... | collective-permute-start | bytes 1572872 | tf_op jit(solution)/shard_map/ppermute | solution.py:271
  6.4 1.5 %collective-permute-start = (bf16[256,128]{1,0:T(8,128)(2,1)}, bf16[256,128]{1,0:T(8,128)(2,1)S(1)}, u32[]{:S(2)}, u32[]{:S(2)}) collective-permute-start(bf16[256,128]{1,0:T(8,128)(2,1)} %param.13), channel_id=1, source_target_pairs={{0,1},{1,0},{2,3},{3,2},{4,5},{5,4},{6,7},{7,6},{8,9},{9,8},{10,11... | collective-permute-start | bytes 196616 | tf_op jit(solution)/shard_map/ppermute | solution.py:261
  6.4 1.6 %collective-permute-start.1 = (bf16[256,128]{1,0:T(8,128)(2,1)}, bf16[256,128]{1,0:T(8,128)(2,1)S(1)}, u32[]{:S(2)}, u32[]{:S(2)}) collective-permute-start(bf16[256,128]{1,0:T(8,128)(2,1)} %param.14), channel_id=1, source_target_pairs={{0,1},{1,0},{2,3},{3,2},{4,5},{5,4},{6,7},{7,6},{8,9},{9,8},{10,11... | collective-permute-start | bytes 196616 | tf_op jit(solution)/shard_map/ppermute | solution.py:262
  8.1 0.7 copy-start.6
  8.1 0.7 copy-start.4
  8.1 0.7 copy-start.5
  8.1 0.7 copy-start.3
  8.1 0.7 copy-start.7
  10.2 23.3 %collective-permute-start.5 = (bf16[1024,256]{1,0:T(8,128)(2,1)S(1)}, bf16[1024,256]{1,0:T(8,128)(2,1)S(1)}, u32[]{:S(2)}, u32[]{:S(2)}) collective-permute-start(bf16[1024,256]{1,0:T(8,128)(2,1)S(1)} %collective-permute-done.2.refs_0_), channel_id=1, source_target_pairs={{11,2},{15,6},{0,9},{4,13},{27,18},{31,22},{16,25},{20,29}} | collective-permute-start | bytes 1572872 | tf_op jit(solution)/shard_map/ppermute | solution.py:271
  11.5 40.6 %collective-permute-start.3 = (bf16[1024,256]{1,0:T(8,128)(2,1)}, bf16[1024,256]{1,0:T(8,128)(2,1)S(1)}, u32[]{:S(2)}, u32[]{:S(2)}) collective-permute-start(bf16[1024,256]{1,0:T(8,128)(2,1)} %bitcast.2.x_ref), channel_id=1, source_target_pairs={{5,2},{2,5},{9,6},{6,9},{13,10},{10,13},{21,18},{18,21},{25,22},{2... | collective-permute-start | bytes 1572872 | tf_op jit(solution)/shard_map/ppermute | solution.py:271
  14.3 37.8 %collective-permute-start.4 = (bf16[1024,256]{1,0:T(8,128)(2,1)S(1)}, bf16[1024,256]{1,0:T(8,128)(2,1)S(1)}, u32[]{:S(2)}, u32[]{:S(2)}) collective-permute-start(bf16[1024,256]{1,0:T(8,128)(2,1)S(1)} %collective-permute-done.2.refs_0_), channel_id=1, source_target_pairs={{4,0},{8,4},{3,7},{12,8},{7,11},{11,15},{20,16},{24,20},{19,23},{2... | collective-permute-start | bytes 1572872 | tf_op jit(solution)/shard_map/ppermute | solution.py:271
  61.9 11.6 %collective-permute-start.7 = (bf16[256,512]{1,0:T(8,128)(2,1)S(1)}, bf16[256,512]{1,0:T(8,128)(2,1)S(1)}, u32[]{:S(2)}, u32[]{:S(2)}) collective-permute-start(bf16[256,512]{1,0:T(8,128)(2,1)S(1)} %get-tuple-element.38), channel_id=1, source_target_pairs={{0,1},{1,0},{2,3},{3,2},{4,5},{5,4},{6,7},{7,6},{8,9},{9,8},{10,11... | collective-permute-start | bytes 786440 | tf_op jit(solution)/shard_map/ppermute | solution.py:373
  64.2 9.3 %copy-start = (bf16[512,512]{1,0:T(8,128)(2,1)S(1)}, bf16[512,512]{1,0:T(8,128)(2,1)}, u32[]{:S(2)}) copy-start(bf16[512,512]{1,0:T(8,128)(2,1)} %mlp_ref.1) | copy-start | bytes 1572868
  64.2 9.3 %copy-start.1 = (bf16[512,256]{1,0:T(8,128)(2,1)S(1)}, bf16[512,256]{1,0:T(8,128)(2,1)}, u32[]{:S(2)}) copy-start(bf16[512,256]{1,0:T(8,128)(2,1)} %mlp_out_ref.1) | copy-start | bytes 786436
  64.2 9.3 %copy-start.2 = (bf16[256,256]{1,0:T(8,128)(2,1)S(1)}, bf16[256,256]{1,0:T(8,128)(2,1)}, u32[]{:S(2)}) copy-start(bf16[256,256]{1,0:T(8,128)(2,1)} %out_ref.1) | copy-start | bytes 393220

commit v11 on v6

--- a/solution.py
+++ b/solution.py
@@ -41,12 +41,15 @@
         parts.append(jnp.where(sub == 0, other, own))
     wk_ref[:, :local], wk_ref[:, local:] = parts[0], parts[1]
     wvt_ref[:local, :], wvt_ref[local:, :] = parts[2].T, parts[3].T
-    keys = dot(x_ref[...], wk_ref[...]).astype(BF16)
-    lane = lax.broadcasted_iota(jnp.int32, (rows, 128), 1)
+    transposed = jnp.concatenate([parts[0].T, parts[1].T], axis=0)
+    queries = dot(transposed, x_ref[...], (1, 1)).astype(BF16)
+    head_width = width // HEADS
     for head in range(HEADS):
-        block, odd = head // 2 * 128, head % 2
-        mine = (lane >= 64) if odd else (lane < 64)
-        queries_ref[head] = jnp.where(mine, keys[:, block : block + 128], jnp.zeros((), BF16))
+        mine, rest = (0, head_width) if head % 2 == 0 else (head_width, 0)
+        queries_ref[head, mine : mine + head_width, :] = queries[
+            head * head_width : (head + 1) * head_width, :
+        ]
+        queries_ref[head, rest : rest + head_width, :] = jnp.zeros((head_width, rows), BF16)
     for step in range(1, SPAN + 1):
         lower = image - sub * step
         inside = jnp.logical_and(lower >= 0, lower + step < images)
@@ -104,10 +107,10 @@
 
     waiting = []
     for head in range(HEADS):
-        queries = queries_ref[head, queries_at, :]
+        queries = queries_ref[head, :, queries_at]
         lanes = slice(head // 2 * 128, head // 2 * 128 + 128)
         for r in range(0, rows, tile):
-            waiting.append((head, r, dot(keys_ref[r : r + tile, lanes], queries, (1, 1))))
+            waiting.append((head, r, dot(keys_ref[r : r + tile, lanes], queries)))
             if len(waiting) > 2:
                 finish(*waiting.pop(0))
     for item in waiting:
@@ -119,7 +122,7 @@
             head, part = i // (span // tile), lax.rem(i, span // tile)
             part_at = pl.ds(pl.multiple_of(at + part * tile, tile), tile)
             lanes = pl.ds(pl.multiple_of(head // 2 * 128, 128), 128)
-            scores = dot(keys_ref[:, lanes], queries_ref[head, part_at, :], (1, 1)) * scale
+            scores = dot(keys_ref[:, lanes], queries_ref[head, :, part_at]) * scale
             powers = jnp.exp(scores - jnp.max(scores, axis=0, keepdims=True))
             weights = powers / jnp.sum(powers, axis=0, keepdims=True)
             product = dot(values_ref[head, :head_width, :], weights.astype(BF16))
@@ -315,7 +318,7 @@
         [
             shape((width, width), BF16),
             shape((width, width), BF16),
-            shape((HEADS, rows, 128), BF16),
+            shape((HEADS, 128, rows), BF16),
             shape((8, 128), F32),
             shape((half, width), BF16),
             shape((8, hidden_width), F32),

time: 77.5 us -> 75.4 us (0.973)
  the two profiles are of different devices: /device:TPU:8 before, /device:TPU:12 now
where the time goes in v11:
time: 75.4 us; the launch traced here: 75.1 us
  Pallas kernels  59.4 us (79%)
  starting transfers between devices  12.7 us (17%)
  waiting for transfers between devices  1.2 us (2%)
  other arithmetic  0.89 us (1%)
    pallas_call x6, Pallas kernels, called(): pl.pallas_call(kernel, in_specs=[SMEM] * scalars + [VMEM] * (len(args) -...  59.4 us
    ppermute x5, starting transfers between devices, carried(): return lax.ppermute(value, RING, pairs)  9.98 us
    ppermute x1, starting transfers between devices, on_device(): qk_other = lax.ppermute(qk_weight, 'sub', swap)  2.6 us
  transfers between devices with their start and end apart: 8, of which 3 were waited for; matrix products, arithmetic and copies ran while one was open for 1% of the time, Pallas kernels for 64%

profile of v11, /device:TPU:12, one launch (start us, length us, event | category | flops | bytes accessed | tf_op | source)
XLA Modules:
  0.0 75.1 jit_solution(16214983589486650533)
XLA Ops:
  0.0 1.3 %collective-permute-start.2 = (bf16[1024,256]{1,0:T(8,128)(2,1)}, bf16[1024,256]{1,0:T(8,128)(2,1)S(1)}, u32[]{:S(2)}, u32[]{:S(2)}) collective-permute-start(bf16[1024,256]{1,0:T(8,128)(2,1)} %bitcast.2.x_ref), channel_id=1, source_target_pairs={{2,0},{1,3},{6,4},{5,7},{10,8},{9,11},{14,12},{13,15},{18,16},{17,... | collective-permute-start | bytes 1572872 | tf_op jit(solution)/shard_map/ppermute | solution.py:266
  1.3 2.4 %collective-permute-start.6 = (bf16[1024,256]{1,0:T(8,128)(2,1)}, bf16[1024,256]{1,0:T(8,128)(2,1)S(1)}, u32[]{:S(2)}, u32[]{:S(2)}) collective-permute-start(bf16[1024,256]{1,0:T(8,128)(2,1)} %bitcast.2.x_ref), channel_id=1, source_target_pairs={{4,0},{6,2},{8,4},{1,5},{10,6},{3,7},{12,8},{5,9},{14,10},{7,11},{... | collective-permute-start | bytes 1572872 | tf_op jit(solution)/shard_map/ppermute | solution.py:266
  3.7 2.6 %collective-permute-start = (bf16[256,128]{1,0:T(8,128)(2,1)}, bf16[256,128]{1,0:T(8,128)(2,1)S(1)}, u32[]{:S(2)}, u32[]{:S(2)}) collective-permute-start(bf16[256,128]{1,0:T(8,128)(2,1)} %param.13), channel_id=1, source_target_pairs={{0,1},{1,0},{2,3},{3,2},{4,5},{5,4},{6,7},{7,6},{8,9},{9,8},{10,11... | collective-permute-start | bytes 196616 | tf_op jit(solution)/shard_map/ppermute | solution.py:256
  6.3 0.1 collective-permute-start.1
  6.3 0.9 %pad_maximum_fusion.own_ref = bf16[256,256]{1,0:T(8,128)(2,1)S(1)} fusion(bf16[256,128]{1,0:T(8,128)(2,1)} %param.14, bf16[256,128]{1,0:T(8,128)(2,1)} %param.13), kind=kLoop, calls=%fused_computation | loop fusion | flops 262144 | bytes 262144 | tf_op jit(solution)/shard_map/concatenate | solution.py:254
  7.2 0.1 collective-permute-done.qk_other_ref
  7.4 0.4 collective-permute-done.1.value_other_ref
  7.7 0.0 copy-start.6
  7.7 0.0 copy-start.4
  7.7 0.0 copy-start.5
  7.7 0.0 copy-start.3
  7.7 0.0 copy-start.7
  7.8 0.7 copy-done.6
  8.4 0.0 copy-done.4
  8.4 0.0 copy-done.5
  8.4 0.0 copy-done.3
  8.5 0.0 copy-done.7
  8.5 1.4 %shard_map.109 = (bf16[256,256]{1,0:T(8,128)(2,1)S(1)}, bf16[256,256]{1,0:T(8,128)(2,1)S(1)}, bf16[4,128,1024]{2,1,0:T(8,128)(2,1)S(1)}, f32[8,128]{1,0:T(8,128)...) custom-call(s32[1]{0:T(128)} %bitcast.place_ref, s32[3,8]{1,0:T(4,128)S(1)} %bitcast.8, ...), custom_call_target="tpu_custom_call" | custom-call | flops 268435456 | bytes 4194304 | tf_op jit(solution)/shard_map/pallas_call | solution.py:301
  9.9 0.7 collective-permute-start.5
  10.6 0.7 collective-permute-done.2.refs_0_
  11.3 2.3 %collective-permute-start.4 = (bf16[1024,256]{1,0:T(8,128)(2,1)S(1)}, bf16[1024,256]{1,0:T(8,128)(2,1)S(1)}, u32[]{:S(2)}, u32[]{:S(2)}) collective-permute-start(bf16[1024,256]{1,0:T(8,128)(2,1)S(1)} %collective-permute-done.2.refs_0_), channel_id=1, source_target_pairs={{4,0},{8,4},{3,7},{12,8},{7,11},{11,15},{20,16},{24,20},{19,23},{2... | collective-permute-start | bytes 1572872 | tf_op jit(solution)/shard_map/ppermute | solution.py:266
  13.6 3.3 %collective-permute-start.3 = (bf16[1024,256]{1,0:T(8,128)(2,1)S(1)}, bf16[1024,256]{1,0:T(8,128)(2,1)S(1)}, u32[]{:S(2)}, u32[]{:S(2)}) collective-permute-start(bf16[1024,256]{1,0:T(8,128)(2,1)S(1)} %collective-permute-done.2.refs_0_), channel_id=1, source_target_pairs={{11,2},{15,6},{0,9},{4,13},{27,18},{31,22},{16,25},{20,29}} | collective-permute-start | bytes 1572872 | tf_op jit(solution)/shard_map/ppermute | solution.py:266
  16.9 0.0 collective-permute-done.6.x_ref
  17.0 18.5 %shard_map.110.first_ref = bf16[256,1024]{1,0:T(8,128)(2,1)S(1)} custom-call(s32[1]{0:T(128)} %bitcast.place_ref, bf16[4,128,1024]{2,1,0:T(8,128)(2,1)S(1)} %get-tuple-element.26.queries_ref, f32[8,128]{1,0:T(8,128)S(1)} %get-tuple-element.29.facts_ref, bf16[1024,256]{1,0:T(8,128)(2,1)S(1)} %collective-permute-done.6.x_ref, ...), custom_call_target="tpu_custom_call" | custom-call | flops 2147483648 | bytes 2097152 | tf_op jit(solution)/shard_map/pallas_call | solution.py:301
  35.5 0.0 collective-permute-done.5.x_ref
  35.5 18.5 %shard_map.111.second_ref = bf16[256,1024]{1,0:T(8,128)(2,1)S(1)} custom-call(s32[1]{0:T(128)} %bitcast.place_ref, bf16[4,128,1024]{2,1,0:T(8,128)(2,1)S(1)} %get-tuple-element.26.queries_ref, f32[8,128]{1,0:T(8,128)S(1)} %get-tuple-element.29.facts_ref, bf16[1024,256]{1,0:T(8,128)(2,1)S(1)} %collective-permute-done.5.x_ref, ...), custom_call_target="tpu_custom_call" | custom-call | flops 2147483648 | bytes 2097152 | tf_op jit(solution)/shard_map/pallas_call | solution.py:301
  54.0 0.0 collective-permute-done.4.other_ref
  54.0 0.0 collective-permute-done.3.x_ref
  54.0 9.7 %shard_map.112 = (bf16[1024,256]{1,0:T(8,128)(2,1)S(1)}, bf16[4,80,1024]{2,1,0:T(8,128)(2,1)S(1)}, bf16[256,512]{1,0:T(8,128)(2,1)S(1)}) custom-call(s32[1]{0:T(128)} %bitcast.place_ref, bf16[4,128,1024]{2,1,0:T(8,128)(2,1)S(1)} %get-tuple-element.26.queries_ref, f32[8,128]{1,0:T(8,128)S(1)} %get-tuple-element.29.facts_ref, ...), custom_call_target="tpu_custom_call" | custom-call | flops 1073741824 | bytes 2097152 | tf_op jit(solution)/shard_map/pallas_call | solution.py:301
  63.8 0.1 collective-permute-start.7
  63.9 0.0 copy-start
  63.9 0.0 copy-start.1
  63.9 0.0 copy-start.2
  63.9 9.3 %shard_map.113.keep_ref = f32[256,512]{1,0:T(8,128)S(1)} custom-call(s32[1]{0:T(128)} %bitcast.place_ref, bf16[4,128,1024]{2,1,0:T(8,128)(2,1)S(1)} %get-tuple-element.26.queries_ref, f32[8,128]{1,0:T(8,128)S(1)} %get-tuple-element.29.facts_ref, bf16[1024,256]{1,0:T(8,128)(2,1)S(1)} %get-tuple-element.41.keys_ref, ...), custom_call_target="tpu_custom_call" | custom-call | flops 1073741824 | bytes 2097152 | tf_op jit(solution)/shard_map/pallas_call | solution.py:301
  73.2 0.0 collective-permute-done.7.came_ref
  73.2 0.0 copy-done
  73.2 0.0 copy-done.1
  73.2 0.0 copy-done.2
  73.2 1.9 %shard_map.114 = bf16[512,256]{1,0:T(8,128)(2,1)} custom-call(f32[256,512]{1,0:T(8,128)S(1)} %shard_map.113.keep_ref, bf16[256,512]{1,0:T(8,128)(2,1)S(1)} %collective-permute-done.7.came_ref, bf16[512,256]{1,0:T(8,128)(2,1)S(1)} %get-tuple-element.45.rows_ref, bf16[256,256]{1,0:T(8,128)(2,1)S(1)} %copy-done.2, bf16[512,512]{1,0:T(8,128)(2,1)S(1)} %copy-done, ...), custom_call_target="tpu_custom_call" | custom-call | flops 268435456 | bytes 4194304 | tf_op jit(solution)/shard_map/pallas_call | solution.py:301
Async XLA Ops:
  0.0 11.3 %collective-permute-start.2 = (bf16[1024,256]{1,0:T(8,128)(2,1)}, bf16[1024,256]{1,0:T(8,128)(2,1)S(1)}, u32[]{:S(2)}, u32[]{:S(2)}) collective-permute-start(bf16[1024,256]{1,0:T(8,128)(2,1)} %bitcast.2.x_ref), channel_id=1, source_target_pairs={{2,0},{1,3},{6,4},{5,7},{10,8},{9,11},{14,12},{13,15},{18,16},{17,... | collective-permute-start | bytes 1572872 | tf_op jit(solution)/shard_map/ppermute | solution.py:266
  1.3 15.7 %collective-permute-start.6 = (bf16[1024,256]{1,0:T(8,128)(2,1)}, bf16[1024,256]{1,0:T(8,128)(2,1)S(1)}, u32[]{:S(2)}, u32[]{:S(2)}) collective-permute-start(bf16[1024,256]{1,0:T(8,128)(2,1)} %bitcast.2.x_ref), channel_id=1, source_target_pairs={{4,0},{6,2},{8,4},{1,5},{10,6},{3,7},{12,8},{5,9},{14,10},{7,11},{... | collective-permute-start | bytes 1572872 | tf_op jit(solution)/shard_map/ppermute | solution.py:266
  3.7 3.7 %collective-permute-start = (bf16[256,128]{1,0:T(8,128)(2,1)}, bf16[256,128]{1,0:T(8,128)(2,1)S(1)}, u32[]{:S(2)}, u32[]{:S(2)}) collective-permute-start(bf16[256,128]{1,0:T(8,128)(2,1)} %param.13), channel_id=1, source_target_pairs={{0,1},{1,0},{2,3},{3,2},{4,5},{5,4},{6,7},{7,6},{8,9},{9,8},{10,11... | collective-permute-start | bytes 196616 | tf_op jit(solution)/shard_map/ppermute | solution.py:256
  6.3 1.5 %collective-permute-start.1 = (bf16[256,128]{1,0:T(8,128)(2,1)}, bf16[256,128]{1,0:T(8,128)(2,1)S(1)}, u32[]{:S(2)}, u32[]{:S(2)}) collective-permute-start(bf16[256,128]{1,0:T(8,128)(2,1)} %param.14), channel_id=1, source_target_pairs={{0,1},{1,0},{2,3},{3,2},{4,5},{5,4},{6,7},{7,6},{8,9},{9,8},{10,11... | collective-permute-start | bytes 196616 | tf_op jit(solution)/shard_map/ppermute | solution.py:257
  7.7 0.7 copy-start.6
  7.7 0.7 copy-start.4
  7.7 0.7 copy-start.5
  7.7 0.7 copy-start.3
  7.7 0.7 copy-start.7
  9.9 25.6 %collective-permute-start.5 = (bf16[1024,256]{1,0:T(8,128)(2,1)}, bf16[1024,256]{1,0:T(8,128)(2,1)S(1)}, u32[]{:S(2)}, u32[]{:S(2)}) collective-permute-start(bf16[1024,256]{1,0:T(8,128)(2,1)} %bitcast.2.x_ref), channel_id=1, source_target_pairs={{5,2},{2,5},{9,6},{6,9},{13,10},{10,13},{21,18},{18,21},{25,22},{2... | collective-permute-start | bytes 1572872 | tf_op jit(solution)/shard_map/ppermute | solution.py:266
  11.3 42.7 %collective-permute-start.4 = (bf16[1024,256]{1,0:T(8,128)(2,1)S(1)}, bf16[1024,256]{1,0:T(8,128)(2,1)S(1)}, u32[]{:S(2)}, u32[]{:S(2)}) collective-permute-start(bf16[1024,256]{1,0:T(8,128)(2,1)S(1)} %collective-permute-done.2.refs_0_), channel_id=1, source_target_pairs={{4,0},{8,4},{3,7},{12,8},{7,11},{11,15},{20,16},{24,20},{19,23},{2... | collective-permute-start | bytes 1572872 | tf_op jit(solution)/shard_map/ppermute | solution.py:266
  13.6 40.4 %collective-permute-start.3 = (bf16[1024,256]{1,0:T(8,128)(2,1)S(1)}, bf16[1024,256]{1,0:T(8,128)(2,1)S(1)}, u32[]{:S(2)}, u32[]{:S(2)}) collective-permute-start(bf16[1024,256]{1,0:T(8,128)(2,1)S(1)} %collective-permute-done.2.refs_0_), channel_id=1, source_target_pairs={{11,2},{15,6},{0,9},{4,13},{27,18},{31,22},{16,25},{20,29}} | collective-permute-start | bytes 1572872 | tf_op jit(solution)/shard_map/ppermute | solution.py:266
  63.8 9.4 %collective-permute-start.7 = (bf16[256,512]{1,0:T(8,128)(2,1)S(1)}, bf16[256,512]{1,0:T(8,128)(2,1)S(1)}, u32[]{:S(2)}, u32[]{:S(2)}) collective-permute-start(bf16[256,512]{1,0:T(8,128)(2,1)S(1)} %get-tuple-element.40), channel_id=1, source_target_pairs={{0,1},{1,0},{2,3},{3,2},{4,5},{5,4},{6,7},{7,6},{8,9},{9,8},{10,11... | collective-permute-start | bytes 786440 | tf_op jit(solution)/shard_map/ppermute | solution.py:371
  63.9 9.3 %copy-start = (bf16[512,512]{1,0:T(8,128)(2,1)S(1)}, bf16[512,512]{1,0:T(8,128)(2,1)}, u32[]{:S(2)}) copy-start(bf16[512,512]{1,0:T(8,128)(2,1)} %mlp_ref.1) | copy-start | bytes 1572868
  63.9 9.3 %copy-start.1 = (bf16[512,256]{1,0:T(8,128)(2,1)S(1)}, bf16[512,256]{1,0:T(8,128)(2,1)}, u32[]{:S(2)}) copy-start(bf16[512,256]{1,0:T(8,128)(2,1)} %mlp_out_ref.1) | copy-start | bytes 786436
  63.9 9.3 %copy-start.2 = (bf16[256,256]{1,0:T(8,128)(2,1)S(1)}, bf16[256,256]{1,0:T(8,128)(2,1)}, u32[]{:S(2)}) copy-start(bf16[256,256]{1,0:T(8,128)(2,1)} %out_ref.1) | copy-start | bytes 393220
